TPU v7x, 32 devices: a whole 2x2x4 slice. The times are simulated.
32 devices in a mesh: tm: 2 (over x), cell: 16 (over z, y, core).
Axes of the slice: x: 2, y: 2, z: 4, core: 2. Of those that a mesh axis runs over, the one named last changes fastest.
Arguments:
- initial: float32 [4096, 128], P('cell'), may hold values from 0.2 to 6, as said below
- source: float32 [4, 4096, 128], P('tm', 'cell'), may hold values from -1.8 to 1.8
- mix_rate: float32 [128], replicated, may hold values from 0.05 to 0.4
- fine_inverse: float32 [4, 32, 128, 128], P('tm', 'cell'), may hold values from -0.1 to 0.9, as said below
- coarse_inverse: float32 [4, 32, 128, 128], P('tm', 'cell'), may hold values from -0.1 to 1, as said below
- step_counts: int32 [4096], P('cell'), may hold values from 4 to 8
Outputs:
- finals: float32 [4, 4096, 128], P('tm', 'cell')
Inputs may be any that keep to these rules, and one draw needn't show every extreme that they name: `initial`: positive compositions. `fine_inverse`: each matrix is a positive diagonal plus small off-diagonal entries. `coarse_inverse`: each matrix is a positive diagonal plus small off-diagonal entries.
All inputs are finite; a program needn't handle non-finite values.
Results may differ from a plain program's by a relative error of at most 0.00011.
Values sent between devices are 32-bit elements; how exact they have to be, the bound alone decides.
No kernel may reach another device: no remote copies, remote signals or barrier semaphores. Data moves between devices by JAX's collectives and lax.ppermute only.
A program may use at most 64 MiB of HBM per device.

v0:
```python
import jax
import jax.numpy as jnp
from jax import lax
from jax.sharding import PartitionSpec as P

FINE_MAX = 8
ITERS = 2


def from_behind(block, axis, distance):
    devices = range(lax.axis_size(axis))
    route = [(i - distance, i) for i in devices if i - distance in devices]
    return lax.ppermute(block, axis, route)


def group_mul(state, matrices):
    count, width = state.shape
    groups = matrices.shape[0]
    shaped = state.reshape(groups, count // groups, width)
    result = jnp.einsum("gcs,gst->gct", shaped, matrices, precision=lax.Precision.HIGHEST)
    return result.reshape(count, width)


def slices_mul(state, matrices):
    lead, count, width = state.shape
    groups = matrices.shape[1]
    shaped = state.reshape(lead, groups, count // groups, width)
    result = jnp.einsum("lgcs,lgst->lgct", shaped, matrices, precision=lax.Precision.HIGHEST)
    return result.reshape(lead, count, width)


def local_chain(incoming, offsets, coarse_inverse):
    state = incoming
    results = []
    for index in range(offsets.shape[0]):
        state = group_mul(state, coarse_inverse[index]) + offsets[index]
        results.append(state)
    return jnp.stack(results, axis=0)


def zero_start_end(offsets, coarse_inverse):
    state = offsets[0]
    state = group_mul(state, coarse_inverse[1]) + offsets[1]
    return state


def across(initial, offsets, coarse_inverse):
    composed = coarse_inverse[0]
    composed = jnp.einsum(
        "gst,gtu->gsu", composed, coarse_inverse[1], precision=lax.Precision.HIGHEST
    )
    shifted = zero_start_end(offsets, coarse_inverse)
    leading = lax.axis_index("tm") == 0

    def advance(turn, incoming):
        ending = group_mul(incoming, composed) + shifted
        received = from_behind(ending, "tm", 1)
        return jnp.where(leading, initial, received)

    incoming = lax.fori_loop(0, lax.axis_size("tm") - 1, advance, initial)
    return (incoming, local_chain(incoming, offsets, coarse_inverse))


def body(initial, source, mix_rate, fine_inverse, coarse_inverse, step_counts):
    total = initial.shape[0] * lax.axis_size("cell")
    offsets0 = slices_mul(source, coarse_inverse)
    incoming, finals = across(initial, offsets0, coarse_inverse)
    for sweep_round in range(ITERS):
        starts = jnp.concatenate([incoming[None], finals[:-1]], axis=0)
        state = starts
        for substep in range(FINE_MAX):
            average = lax.psum(jnp.sum(state, axis=1), "cell") / total
            moved = slices_mul(
                state + source + mix_rate * (average[:, None, :] - state), fine_inverse
            )
            active = (substep < step_counts)[None, :, None]
            state = jnp.where(active, moved, state)
        coarse_ends = slices_mul(starts, coarse_inverse) + offsets0
        offsets = offsets0 + state - coarse_ends
        incoming, finals = across(initial, offsets, coarse_inverse)
    return finals


def solution(mesh):
    return jax.shard_map(
        body,
        mesh=mesh,
        in_specs=(
            P("cell", None),
            P("tm", "cell", None),
            P(),
            P("tm", "cell", None, None),
            P("tm", "cell", None, None),
            P("cell"),
        ),
        out_specs=P("tm", "cell", None),
        check_vma=False,
    )
```

profile of v0, /device:TPU:0, one launch (start us, length us, event | category | flops | bytes accessed | tf_op | source)
XLA Modules:
  0.0 515.5 jit_solution(2411006129935054928)
XLA Ops:
  0.0 1.5 fusion.61
  4.6 4.9 collective-permute-start
  10.2 2.0 collective-permute-done
  13.3 32.6 %psum.112 = f32[2,128]{1,0:T(2,128)S(1)} all-reduce(f32[2,128]{1,0:T(2,128)S(1)} %fusion.9), channel_id=1, replica_groups=mesh['tm'=2,'cell'=16] {'cell'}, use_global_device_ids=true, to_apply=%region_1.2 | all-reduce | flops 256 | bytes 2048 | tf_op jit(solution)/shard_map/psum | solution.py:72
  47.4 29.5 %psum.113 = f32[2,128]{1,0:T(2,128)S(1)} all-reduce(f32[2,128]{1,0:T(2,128)S(1)} %get-tuple-element.85), channel_id=1, replica_groups=mesh['tm'=2,'cell'=16] {'cell'}, use_global_device_ids=true, to_apply=%region_3.4 | all-reduce | flops 256 | bytes 2048 | tf_op jit(solution)/shard_map/psum | solution.py:72
  77.4 29.5 %psum.114 = f32[2,128]{1,0:T(2,128)S(1)} all-reduce(f32[2,128]{1,0:T(2,128)S(1)} %get-tuple-element.100), channel_id=1, replica_groups=mesh['tm'=2,'cell'=16] {'cell'}, use_global_device_ids=true, to_apply=%region_5.6 | all-reduce | flops 256 | bytes 2048 | tf_op jit(solution)/shard_map/psum | solution.py:72
  107.5 29.5 %psum.115 = f32[2,128]{1,0:T(2,128)S(1)} all-reduce(f32[2,128]{1,0:T(2,128)S(1)} %get-tuple-element.81), channel_id=1, replica_groups=mesh['tm'=2,'cell'=16] {'cell'}, use_global_device_ids=true, to_apply=%region_7.8 | all-reduce | flops 256 | bytes 2048 | tf_op jit(solution)/shard_map/psum | solution.py:72
  137.6 29.5 %psum.116 = f32[2,128]{1,0:T(2,128)S(1)} all-reduce(f32[2,128]{1,0:T(2,128)S(1)} %get-tuple-element.103), channel_id=1, replica_groups=mesh['tm'=2,'cell'=16] {'cell'}, use_global_device_ids=true, to_apply=%region_9.10 | all-reduce | flops 256 | bytes 2048 | tf_op jit(solution)/shard_map/psum | solution.py:72
  167.6 29.5 %psum.117 = f32[2,128]{1,0:T(2,128)S(1)} all-reduce(f32[2,128]{1,0:T(2,128)S(1)} %get-tuple-element.77), channel_id=1, replica_groups=mesh['tm'=2,'cell'=16] {'cell'}, use_global_device_ids=true, to_apply=%region_11.12 | all-reduce | flops 256 | bytes 2048 | tf_op jit(solution)/shard_map/psum | solution.py:72
  197.7 29.5 %psum.118 = f32[2,128]{1,0:T(2,128)S(1)} all-reduce(f32[2,128]{1,0:T(2,128)S(1)} %get-tuple-element.106), channel_id=1, replica_groups=mesh['tm'=2,'cell'=16] {'cell'}, use_global_device_ids=true, to_apply=%region_13.14 | all-reduce | flops 256 | bytes 2048 | tf_op jit(solution)/shard_map/psum | solution.py:72
  227.8 29.5 %psum.119 = f32[2,128]{1,0:T(2,128)S(1)} all-reduce(f32[2,128]{1,0:T(2,128)S(1)} %get-tuple-element.108), channel_id=1, replica_groups=mesh['tm'=2,'cell'=16] {'cell'}, use_global_device_ids=true, to_apply=%region_15.16 | all-reduce | flops 256 | bytes 2048 | tf_op jit(solution)/shard_map/psum | solution.py:72
  258.3 4.4 collective-permute-start.1
  262.7 2.8 collective-permute-done.1
  265.8 29.5 %psum.120 = f32[2,128]{1,0:T(2,128)S(1)} all-reduce(f32[2,128]{1,0:T(2,128)S(1)} %fusion.8), channel_id=1, replica_groups=mesh['tm'=2,'cell'=16] {'cell'}, use_global_device_ids=true, to_apply=%region_17.18 | all-reduce | flops 256 | bytes 2048 | tf_op jit(solution)/shard_map/psum | solution.py:72
  296.2 29.5 %psum.121 = f32[2,128]{1,0:T(2,128)S(1)} all-reduce(f32[2,128]{1,0:T(2,128)S(1)} %get-tuple-element.63), channel_id=1, replica_groups=mesh['tm'=2,'cell'=16] {'cell'}, use_global_device_ids=true, to_apply=%region_19.20 | all-reduce | flops 256 | bytes 2048 | tf_op jit(solution)/shard_map/psum | solution.py:72
  326.2 29.5 %psum.122 = f32[2,128]{1,0:T(2,128)S(1)} all-reduce(f32[2,128]{1,0:T(2,128)S(1)} %get-tuple-element.111), channel_id=1, replica_groups=mesh['tm'=2,'cell'=16] {'cell'}, use_global_device_ids=true, to_apply=%region_21.22 | all-reduce | flops 256 | bytes 2048 | tf_op jit(solution)/shard_map/psum | solution.py:72
  356.3 29.5 %psum.123 = f32[2,128]{1,0:T(2,128)S(1)} all-reduce(f32[2,128]{1,0:T(2,128)S(1)} %get-tuple-element.53), channel_id=1, replica_groups=mesh['tm'=2,'cell'=16] {'cell'}, use_global_device_ids=true, to_apply=%region_23.24 | all-reduce | flops 256 | bytes 2048 | tf_op jit(solution)/shard_map/psum | solution.py:72
  386.4 29.5 %psum.124 = f32[2,128]{1,0:T(2,128)S(1)} all-reduce(f32[2,128]{1,0:T(2,128)S(1)} %get-tuple-element.114), channel_id=1, replica_groups=mesh['tm'=2,'cell'=16] {'cell'}, use_global_device_ids=true, to_apply=%region_25.26 | all-reduce | flops 256 | bytes 2048 | tf_op jit(solution)/shard_map/psum | solution.py:72
  416.4 29.5 %psum.125 = f32[2,128]{1,0:T(2,128)S(1)} all-reduce(f32[2,128]{1,0:T(2,128)S(1)} %get-tuple-element.49), channel_id=1, replica_groups=mesh['tm'=2,'cell'=16] {'cell'}, use_global_device_ids=true, to_apply=%region_27.28 | all-reduce | flops 256 | bytes 2048 | tf_op jit(solution)/shard_map/psum | solution.py:72
  446.5 29.5 %psum.126 = f32[2,128]{1,0:T(2,128)S(1)} all-reduce(f32[2,128]{1,0:T(2,128)S(1)} %get-tuple-element.117), channel_id=1, replica_groups=mesh['tm'=2,'cell'=16] {'cell'}, use_global_device_ids=true, to_apply=%region_29.30 | all-reduce | flops 256 | bytes 2048 | tf_op jit(solution)/shard_map/psum | solution.py:72
  476.6 29.5 %psum.127 = f32[2,128]{1,0:T(2,128)S(1)} all-reduce(f32[2,128]{1,0:T(2,128)S(1)} %get-tuple-element.119), channel_id=1, replica_groups=mesh['tm'=2,'cell'=16] {'cell'}, use_global_device_ids=true, to_apply=%region_31.32 | all-reduce | flops 256 | bytes 2048 | tf_op jit(solution)/shard_map/psum | solution.py:72
  507.0 4.4 collective-permute-start.2
  511.5 2.7 collective-permute-done.2
  514.8 0.7 copy-done.8
  (96 shorter events, 16.8 us)
Async XLA Ops:
  0.0 47.0 %copy-start = (f32[2,2,128,128]{3,2,1,0:T(8,128)S(1)}, f32[2,2,128,128]{3,2,1,0:T(8,128)}, u32[]{:S(2)}) copy-start(f32[2,2,128,128]{3,2,1,0:T(8,128)} %param.9) | copy-start | bytes 786436
  1.5 0.7 copy-start.3
  1.5 1.0 copy-start.2
  2.8 0.9 copy-start.5
  3.7 0.9 slice-start
  4.6 7.6 %collective-permute-start = (f32[256,128]{1,0:T(8,128)S(1)}, f32[256,128]{1,0:T(8,128)S(1)}, u32[]{:S(2)}, u32[]{:S(2)}) collective-permute-start(f32[256,128]{1,0:T(8,128)S(1)} %fusion.13), channel_id=1, source_target_pairs={{0,16},{1,17},{2,18},{3,19},{4,20},{5,21},{6,22},{7,23},{8,24},{9,... | collective-permute-start | bytes 393224 | tf_op jit(solution)/shard_map/while/body/eval_jaxpr/ppermute | solution.py:13
  9.5 0.7 copy-start.7
  12.3 1.0 copy-start.4
  46.0 1.0 copy-start.1
  46.0 1.0 copy-start.6
  258.3 7.2 %collective-permute-start.1 = (f32[256,128]{1,0:T(8,128)S(1)}, f32[256,128]{1,0:T(8,128)S(1)}, u32[]{:S(2)}, u32[]{:S(2)}) collective-permute-start(f32[256,128]{1,0:T(8,128)S(1)} %fusion.11), channel_id=1, source_target_pairs={{0,16},{1,17},{2,18},{3,19},{4,20},{5,21},{6,22},{7,23},{8,24},{9,... | collective-permute-start | bytes 393224 | tf_op jit(solution)/shard_map/while/body/eval_jaxpr/ppermute | solution.py:13
  507.0 7.2 %collective-permute-start.2 = (f32[256,128]{1,0:T(8,128)S(1)}, f32[256,128]{1,0:T(8,128)S(1)}, u32[]{:S(2)}, u32[]{:S(2)}) collective-permute-start(f32[256,128]{1,0:T(8,128)S(1)} %fusion.12), channel_id=1, source_target_pairs={{0,16},{1,17},{2,18},{3,19},{4,20},{5,21},{6,22},{7,23},{8,24},{9,... | collective-permute-start | bytes 393224 | tf_op jit(solution)/shard_map/while/body/eval_jaxpr/ppermute | solution.py:13
  514.8 0.7 copy-start.8
where the time goes:
time: 516 us
  blocking collectives  475 us (92%)
  starting transfers between devices  13.7 us (3%)
  matrix products  11.5 us (2%)
  waiting for transfers between devices  7.54 us (1%)
    psum x16, blocking collectives, body(): average = lax.psum(jnp.sum(state, axis=1), 'cell') / total  475 us
    ppermute x3, starting transfers between devices, from_behind(): return lax.ppermute(block, axis, route)  13.7 us
  transfers between devices with their start and end apart: 3, of which 3 were waited for; matrix products, arithmetic and copies ran while one was open for 0% of the time, Pallas kernels for 0%

commit v1 on v0

v1 whole, which is shorter than its diff:
```python
import jax
import jax.numpy as jnp
from jax import lax
from jax.sharding import PartitionSpec as P

FINE_MAX = 8
FINE_MIN = 4
CLASSES = FINE_MAX - FINE_MIN + 1
MATS = 7


def mm(a, b):
    return jnp.dot(a, b, precision=lax.Precision.HIGHEST)


def from_behind(block, axis, distance):
    devices = range(lax.axis_size(axis))
    route = [(i - distance, i) for i in devices if i - distance in devices]
    return lax.ppermute(block, axis, route)


def swap_core(block):
    n = lax.axis_size("cell")
    return lax.ppermute(block, "cell", [(i, i ^ 1) for i in range(n)])


def same_core():
    n = lax.axis_size("cell")
    return [list(range(c, n, 2)) for c in range(2)]


def spread(block, groups=None):
    n = lax.axis_size("cell") if groups is None else len(groups[0])
    return lax.all_to_all(
        jnp.broadcast_to(block[None], (n,) + block.shape), "cell", 0, 0,
        axis_index_groups=groups,
    )


def total(block):
    return spread(block).sum(0)


def body(initial, source, mix_rate, fine_inverse, coarse_inverse, step_counts):
    slices, groups, width, _ = fine_inverse.shape
    cells = initial.shape[0]
    per = cells // groups
    n_cell = lax.axis_size("cell")
    turns = lax.axis_size("tm") - 1
    everyone = cells * n_cell
    leading = lax.axis_index("tm") == 0
    core = lax.axis_index("cell") % 2
    rate = mix_rate[None, :]
    keep = 1.0 - rate
    keep_col = keep.reshape(width, 1)

    W = []
    for l in range(slices):
        row = []
        for g in range(groups):
            w1 = fine_inverse[l, g]
            w2 = mm(w1, keep_col * w1)
            w34 = mm(jnp.concatenate([w1, w2]), keep_col * w2)
            w4 = w34[width:]
            w58 = mm(jnp.concatenate([w1, w2, w34]), keep_col * w4)
            row.append([None, w1, w2, w34[:width], w4] + [w58[i * width:(i + 1) * width] for i in range(4)])
        W.append(row)
    counts = step_counts.reshape(groups, per)
    active = {q: jnp.sum((counts >= q).astype(jnp.float32), axis=1) for q in range(FINE_MIN, FINE_MAX + 2)}
    parts = []
    for l in range(slices):
        mats = [sum(W[l][g][d] for g in range(groups)) * (per / everyone) for d in range(1, 5)]
        e6 = sum(active[6][g] * W[l][g][1] for g in range(groups)) / everyone
        e7 = sum(active[7][g] * W[l][g][1] for g in range(groups)) / everyone
        e72 = sum(active[7][g] * W[l][g][2] for g in range(groups)) / everyone
        parts.append(jnp.stack(mats + [e6, e6 + e72 - e7, e7]))
    half = slices // 2
    parts = jnp.stack(parts)
    low, high = parts[:half], parts[half:]
    mine = jnp.where(core == 0, low, high)
    other = jnp.where(core == 0, high, low)
    mine = mine + swap_core(other)
    shard = lax.all_to_all(
        mine.reshape(n_cell // 2, -1, width), "cell", 0, 0, axis_index_groups=same_core()
    ).sum(0)
    mixing = spread(shard, same_core()).reshape(half, MATS, width, width)
    theirs = swap_core(mixing)
    mixing = jnp.where(
        core == 0, jnp.concatenate([mixing, theirs]), jnp.concatenate([theirs, mixing])
    )

    def by_group(state, matrices):
        return jnp.concatenate(
            [mm(state[g * per:(g + 1) * per], matrices[g]) for g in range(groups)]
        )

    def fine_alone(state, l):
        rows = []
        for g in range(groups):
            here = slice(g * per, (g + 1) * per)
            v, s = state[here] * keep, source[l, here]
            k = step_counts[here][:, None]
            summed = sum(W[l][g][d] for d in range(1, FINE_MIN))
            out = 0.0
            for d in range(FINE_MIN, FINE_MAX + 1):
                summed = summed + W[l][g][d]
                out = jnp.where(k == d, mm(v, W[l][g][d]) + mm(s, summed), out)
            rows.append(out)
        return jnp.concatenate(rows)

    def handed(start, advance):
        incoming = start
        for _ in range(turns):
            received = from_behind(advance(incoming), "tm", 1)
            incoming = jnp.where(leading, start, received)
        return incoming

    def coarse_run(incoming):
        states = [incoming]
        for l in range(slices):
            states.append(by_group(states[-1] + source[l], coarse_inverse[l]))
        return states

    starts = coarse_run(handed(initial, lambda u: coarse_run(u)[-1]))
    alone = [starts]
    for _ in range(2):
        old = alone[-1]
        fines = [fine_alone(old[l], l) for l in range(slices)]

        def run(incoming):
            states = [incoming]
            for l in range(slices):
                states.append(fines[l] + by_group(states[l] - old[l], coarse_inverse[l]))
            return states

        alone.append(run(handed(initial, lambda u: run(u)[-1])))

    def sums(state):
        rows = []
        for g in range(groups):
            here = slice(g * per, (g + 1) * per)
            mask = (step_counts[here][None, :] >= jnp.arange(FINE_MIN, FINE_MAX + 1)[:, None])
            rows.append(mm(mask.astype(jnp.float32), state[here]))
        return rows

    source_sums = [sums(source[l]) for l in range(slices)]

    def first_rows(V, l):
        out = [sum(V[g][0:1] for g in range(groups))]
        for m in range(1, FINE_MIN + 1):
            row = 0.0
            for g in range(groups):
                row = row + mm(V[g][0:1] * keep, W[l][g][m])
                row = row + mm(source_sums[l][g][0:1], sum(W[l][g][d] for d in range(1, m + 1)))
            out.append(row)
        return jnp.concatenate(out) / everyone

    def folded(a, W_lg, m, known):
        return sum(mm(a[j] * rate, W_lg[m - j]) for j in range(min(m, known)))

    def second_rows(V, a, l):
        out = []
        base = 0.0
        for g in range(groups):
            w = W[l][g]
            base = base + mm(V[g][0:1] * keep, w[4]) + mm(source_sums[l][g][0:1], w[1] + w[2] + w[3] + w[4])
            base = base + per * folded(a, w, 4, 5)
        for m in range(5, 8):
            q = m - FINE_MIN
            for g in range(groups):
                w = W[l][g]
                base = base + mm(V[g][q:q + 1] * keep, w[m] - w[m - 1]) + mm(source_sums[l][g][q:q + 1], w[m])
                base = base + active[m][g] * (folded(a, w, m, 5) - folded(a, w, m - 1, 5))
            out.append(base)
        return jnp.concatenate(out) / everyone

    def averages(V):
        rows = jnp.stack([first_rows(V[l], l) for l in range(slices)])
        rows = total(rows)
        a = []
        for l in range(slices):
            known = []
            for m in range(5):
                known.append(rows[l, m:m + 1] + sum(mm(known[j] * rate, mixing[l, m - j - 1]) for j in range(m)))
            a.append(known)
        rows = jnp.stack([second_rows(V[l], a[l], l) for l in range(slices)])
        rows = total(rows)
        for l in range(slices):
            a5 = rows[l, 0:1]
            a6 = rows[l, 1:2] + mm(a5 * rate, mixing[l, 4])
            a7 = rows[l, 2:3] + mm(a5 * rate, mixing[l, 5]) + mm(a6 * rate, mixing[l, 6])
            a[l] = a[l] + [a5, a6, a7]
        return a

    def pushes(a, l):
        return [
            jnp.concatenate([folded(a, W[l][g], k, k) for k in range(FINE_MIN, FINE_MAX + 1)])
            for g in range(groups)
        ]

    def coarse_vectors(x, l):
        return [mm(x[g], coarse_inverse[l, g]) for g in range(groups)]

    V = [sums(alone[0][l]) for l in range(slices)]
    a = averages(V)
    h = [pushes(a[l], l) for l in range(slices)]

    def run1(incoming):
        xs = [[incoming[g] for g in range(groups)]]
        for l in range(slices):
            moved = coarse_vectors(xs[l], l)
            xs.append([h[l][g] + moved[g] for g in range(groups)])
        return xs

    zero = jnp.zeros((groups, CLASSES, width), jnp.float32)
    x1 = run1(handed(zero, lambda x: jnp.stack(run1(x)[-1])))
    V = []
    for l in range(slices):
        plain = sums(alone[1][l])
        rows = []
        for g in range(groups):
            row = plain[g]
            exact = [active[k][g] - active[k + 1][g] for k in range(FINE_MIN, FINE_MAX + 1)]
            weighted = [exact[i] * x1[l][g][i:i + 1] for i in range(CLASSES)]
            tails = [sum(weighted[i:]) for i in range(CLASSES)]
            rows.append(row + jnp.concatenate(tails))
        V.append(rows)
    a = averages(V)
    h = [pushes(a[l], l) for l in range(slices)]
    y = [
        [
            h[l][g] + jnp.concatenate(
                [mm(x1[l][g][i:i + 1] * keep, W[l][g][FINE_MIN + i]) for i in range(CLASSES)]
            )
            for g in range(groups)
        ]
        for l in range(slices)
    ]

    def run2(incoming):
        xs = [[incoming[g] for g in range(groups)]]
        for l in range(slices):
            moved = coarse_vectors([xs[l][g] - x1[l][g] for g in range(groups)], l)
            xs.append([y[l][g] + moved[g] for g in range(groups)])
        return xs

    x2 = run2(handed(zero, lambda x: jnp.stack(run2(x)[-1])))
    outs = []
    for l in range(slices):
        rows = []
        for g in range(groups):
            here = slice(g * per, (g + 1) * per)
            k = step_counts[here][:, None]
            out = alone[2][l + 1][here]
            for i in range(CLASSES):
                out = out + jnp.where(k == FINE_MIN + i, x2[l + 1][g][i:i + 1], 0.0)
            rows.append(out)
        outs.append(jnp.concatenate(rows))
    return jnp.stack(outs)


def solution(mesh):
    return jax.shard_map(
        body,
        mesh=mesh,
        in_specs=(
            P("cell", None),
            P("tm", "cell", None),
            P(),
            P("tm", "cell", None, None),
            P("tm", "cell", None, None),
            P("cell"),
        ),
        out_specs=P("tm", "cell", None),
        check_vma=False,
    )
```

time: 516 us -> 377 us (0.73); the launches traced: 516 us -> 370 us
  blocking collectives: 475 us -> 0 us
  matrix products: 11.5 us -> 169 us
  local copies, waits for them, and re-layouts: 4.91 us -> 78.7 us
  starting transfers between devices: 13.7 us -> 45.4 us
  other arithmetic: 2.54 us -> 28.3 us
  waiting for transfers between devices: 7.54 us -> 32.9 us
  between operations: 0.44 us -> 15.3 us
    psum x16 -> x0, blocking collectives: 475 us -> none  [body(): average = lax.psum(jnp.sum(state, axis=1), 'cell') / total]
    dot_general x28 -> x514, matrix products: 11.5 us -> 169 us  [mm(): return jnp.dot(a, b, precision=lax.Precision.HIGHEST)]
    unnamed x18 -> x560, local copies, waits for them, and re-layouts: 4.26 us -> 66.3 us
    all_to_all x0 -> x6, waiting for transfers between devices: none -> 31.5 us  [the longest x5 23.9 us: spread(): lax.all_to_all(jnp.broadcast_to(block[None], (n,) + block.shape), 'cell',...]
    all_to_all x0 -> x6, starting transfers between devices: none -> 29.5 us  [the longest x5 23.5 us: spread(): lax.all_to_all(jnp.broadcast_to(block[None], (n,) + block.shape), 'cell',...]
    concatenate x0 -> x20, local copies, waits for them, and re-layouts: none -> 7.01 us  [the longest x8 2.94 us: pushes(): jnp.concatenate([folded(a, W[l][g], k, k) for k in range(FINE_MIN, FINE_M...]
    ppermute x3 -> x5, waiting for transfers between devices: 7.54 us -> 1.27 us  [from_behind(): return lax.ppermute(block, axis, route)]
    unnamed x0 -> x8, other arithmetic: none -> 6.24 us
  transfers between devices with their start and end apart: 3 -> 13, of which waited for: 3 -> 7; matrix products, arithmetic and copies ran while one was open for 0% -> 25% of each run, Pallas kernels for 0% -> 0%
where the time goes in v1:
time: 377 us; the launch traced here: 370 us
  matrix products  169 us (45%)
  local copies, waits for them, and re-layouts  78.7 us (21%)
  starting transfers between devices  45.4 us (12%)
  waiting for transfers between devices  32.9 us (9%)
  other arithmetic  28.3 us (8%)
  between operations  15.3 us (4%)
    dot_general x514, matrix products, mm(): return jnp.dot(a, b, precision=lax.Precision.HIGHEST)  169 us
    unnamed x560, local copies, waits for them, and re-layouts  66.3 us
    all_to_all x5, waiting for transfers between devices, spread(): lax.all_to_all(jnp.broadcast_to(block[None], (n,) + block.shape), 'cell',...  23.9 us
    all_to_all x5, starting transfers between devices, spread(): lax.all_to_all(jnp.broadcast_to(block[None], (n,) + block.shape), 'cell',...  23.5 us
    ppermute x5, starting transfers between devices, from_behind(): return lax.ppermute(block, axis, route)  15.4 us
  transfers between devices with their start and end apart: 13, of which 7 were waited for; matrix products, arithmetic and copies ran while one was open for 25% of the time, Pallas kernels for 0%

profile of v1, /device:TPU:0, one launch (start us, length us, event | category | flops | bytes accessed | tf_op | source)
XLA Modules:
  0.0 369.6 jit_solution(15945163036551283220)
XLA Ops:
  5.2 1.4 multiply_dynamic-update-slice_fusion.4
  6.6 2.6 bitcast_dynamic-update-slice_fusion.4
  10.2 1.4 multiply_dynamic-update-slice_fusion.1
  11.6 2.6 multiply_dynamic-update-slice_fusion.3
  18.8 5.7 %collective-permute-start = (f32[256,128]{1,0:T(8,128)}, f32[256,128]{1,0:T(8,128)}, u32[]{:S(2)}, u32[]{:S(2)}) collective-permute-start(f32[256,128]{1,0:T(8,128)} %pad_maximum_fusion.1), channel_id=1, source_target_pairs={{0,16},{1,17},{2,18},{3,19},{4,20},{5,21},{6,22},{7,23},{8,24},{9,... | collective-permute-start | bytes 393224 | tf_op jit(solution)/shard_map/ppermute | solution.py:19
  109.6 2.2 collective-permute-start.1
  117.1 6.5 %all-to-all-start = ((f32[16,2,5,128]{3,1,2,0:T(2,128)}), f32[16,2,5,128]{3,1,2,0:T(2,128)}, u32[]{:S(2)}, u32[]{:S(2)}) async-start(f32[16,2,5,128]{3,1,2,0:T(2,128)} %broadcast_in_dim.466), calls=%async_computation | async-start | bytes 163840 | tf_op jit(solution)/shard_map/all_to_all | solution.py:34
  140.9 2.3 collective-permute-start.2
  143.2 1.5 reduce_sum.101
  153.4 1.9 select_add_fusion
  155.4 6.0 %all-to-all-start.1 = ((f32[8,112,128]{2,1,0:T(8,128)}), f32[8,112,128]{2,1,0:T(8,128)S(1)}, u32[]{:S(2)}, u32[]{:S(2)}) async-start(f32[8,112,128]{2,1,0:T(8,128)} %bitcast.3756), calls=%async_computation.1 | async-start | bytes 917504 | tf_op jit(solution)/shard_map/all_to_all | solution.py:83
  166.9 7.5 %all-to-all-done.1 = f32[8,112,128]{2,1,0:T(8,128)S(1)} async-done(((f32[8,112,128]{2,1,0:T(8,128)}), f32[8,112,128]{2,1,0:T(8,128)S(1)}, u32[]{:S(2)}, u32[]{:S(2)}) %all-to-all-start.1) | async-done | bytes 458784 | tf_op jit(solution)/shard_map/all_to_all | solution.py:83
  175.3 3.8 %all-to-all-start.2 = ((f32[8,112,128]{2,1,0:T(8,128)}), f32[8,112,128]{2,1,0:T(8,128)S(1)}, u32[]{:S(2)}, u32[]{:S(2)}) async-start(f32[8,112,128]{2,1,0:T(8,128)} %broadcast_in_dim.467), calls=%async_computation.2 | async-start | bytes 917504 | tf_op jit(solution)/shard_map/all_to_all | solution.py:34
  180.3 12.0 %all-to-all-done.2 = f32[8,112,128]{2,1,0:T(8,128)S(1)} async-done(((f32[8,112,128]{2,1,0:T(8,128)}), f32[8,112,128]{2,1,0:T(8,128)S(1)}, u32[]{:S(2)}, u32[]{:S(2)}) %all-to-all-start.2) | async-done | bytes 458784 | tf_op jit(solution)/shard_map/all_to_all | solution.py:34
  230.0 4.1 %all-to-all-start.3 = ((f32[16,2,3,128]{3,1,2,0:T(2,128)}), f32[16,2,3,128]{3,1,2,0:T(2,128)}, u32[]{:S(2)}, u32[]{:S(2)}) async-start(f32[16,2,3,128]{3,1,2,0:T(2,128)} %broadcast_in_dim.468), calls=%async_computation.3 | async-start | bytes 98304 | tf_op jit(solution)/shard_map/all_to_all | solution.py:34
  267.4 1.4 collective-permute-start.5
  268.9 1.7 fusion.550
  278.7 1.5 convolution_add_fusion.40
  283.8 1.5 convolution_add_fusion.41
  302.8 5.4 %all-to-all-start.4 = ((f32[16,2,5,128]{3,1,2,0:T(2,128)}), f32[16,2,5,128]{3,1,2,0:T(2,128)S(1)}, u32[]{:S(2)}, u32[]{:S(2)}) async-start(f32[16,2,5,128]{3,1,2,0:T(2,128)} %broadcast_in_dim.469), calls=%async_computation.4 | async-start | bytes 163840 | tf_op jit(solution)/shard_map/all_to_all | solution.py:34
  308.6 6.8 %all-to-all-done.4 = f32[16,2,5,128]{3,1,2,0:T(2,128)S(1)} async-done(((f32[16,2,5,128]{3,1,2,0:T(2,128)}), f32[16,2,5,128]{3,1,2,0:T(2,128)S(1)}, u32[]{:S(2)}, u32[]{:S(2)}) %all-to-all-start.4) | async-done | bytes 81952 | tf_op jit(solution)/shard_map/all_to_all | solution.py:34
  344.1 3.7 %all-to-all-start.5 = ((f32[16,2,3,128]{3,1,2,0:T(2,128)}), f32[16,2,3,128]{3,1,2,0:T(2,128)S(1)}, u32[]{:S(2)}, u32[]{:S(2)}) async-start(f32[16,2,3,128]{3,1,2,0:T(2,128)} %broadcast_in_dim.470), calls=%async_computation.5 | async-start | bytes 98304 | tf_op jit(solution)/shard_map/all_to_all | solution.py:34
  349.9 4.7 %all-to-all-done.5 = f32[16,2,3,128]{3,1,2,0:T(2,128)S(1)} async-done(((f32[16,2,3,128]{3,1,2,0:T(2,128)}), f32[16,2,3,128]{3,1,2,0:T(2,128)S(1)}, u32[]{:S(2)}, u32[]{:S(2)}) %all-to-all-start.5) | async-done | bytes 49184 | tf_op jit(solution)/shard_map/all_to_all | solution.py:34
  360.6 3.7 %collective-permute-start.6 = (f32[2,5,128]{2,1,0:T(8,128)S(1)}, f32[2,5,128]{2,1,0:T(8,128)S(1)}, u32[]{:S(2)}, u32[]{:S(2)}) collective-permute-start(f32[2,5,128]{2,1,0:T(8,128)S(1)} %pad_maximum_fusion.8), channel_id=1, source_target_pairs={{0,16},{1,17},{2,18},{3,19},{4,20},{5,21},{6,22},{7,23},{8,24},{9,... | collective-permute-start | bytes 15368 | tf_op jit(solution)/shard_map/ppermute | solution.py:19
  (1193 shorter events, 262.5 us)
Async XLA Ops:
  16.3 137.2 %collective-permute-start.3 = (f32[1,7,128,128]{3,2,1,0:T(8,128)}, f32[1,7,128,128]{3,2,1,0:T(8,128)}, u32[]{:S(2)}, u32[]{:S(2)}) collective-permute-start(f32[1,7,128,128]{3,2,1,0:T(8,128)} %broadcast_select_fusion), channel_id=1, source_target_pairs={{0,1},{1,0},{2,3},{3,2},{4,5},{5,4},{6,7},{7,6},{8,9},{9,8},{10,11... | collective-permute-start | bytes 1376264 | tf_op jit(solution)/shard_map/ppermute | solution.py:24
  18.8 60.0 %collective-permute-start = (f32[256,128]{1,0:T(8,128)}, f32[256,128]{1,0:T(8,128)}, u32[]{:S(2)}, u32[]{:S(2)}) collective-permute-start(f32[256,128]{1,0:T(8,128)} %pad_maximum_fusion.1), channel_id=1, source_target_pairs={{0,16},{1,17},{2,18},{3,19},{4,20},{5,21},{6,22},{7,23},{8,24},{9,... | collective-permute-start | bytes 393224 | tf_op jit(solution)/shard_map/ppermute | solution.py:19
  25.4 55.4 %copy-start.66 = (s32[5]{0:T(128)}, s32[5]{0:T(128)S(1)}, u32[]{:S(2)}) copy-start(s32[5]{0:T(128)S(1)} %iota_add_fusion) | copy-start | bytes 64
  25.4 55.2 %copy-start.91 = (s32[128]{0:T(128)}, s32[128]{0:T(128)S(1)}, u32[]{:S(2)}) copy-start(s32[128]{0:T(128)S(1)} %get-tuple-element.112) | copy-start | bytes 1540
  98.6 15.3 %copy-start.232 = (f32[128]{0:T(128)}, f32[128]{0:T(128)S(1)}, u32[]{:S(2)}) copy-start(f32[128]{0:T(128)S(1)} %convolution_bitcast_fusion.369) | copy-start | bytes 1540
  109.6 14.0 %collective-permute-start.1 = (f32[256,128]{1,0:T(8,128)S(1)}, f32[256,128]{1,0:T(8,128)}, u32[]{:S(2)}, u32[]{:S(2)}) collective-permute-start(f32[256,128]{1,0:T(8,128)S(1)} %maximum_add_fusion.1), channel_id=1, source_target_pairs={{0,16},{1,17},{2,18},{3,19},{4,20},{5,21},{6,22},{7,23},{8,24},{9,... | collective-permute-start | bytes 393224 | tf_op jit(solution)/shard_map/ppermute | solution.py:19
  117.1 26.1 %all-to-all-start = ((f32[16,2,5,128]{3,1,2,0:T(2,128)}), f32[16,2,5,128]{3,1,2,0:T(2,128)}, u32[]{:S(2)}, u32[]{:S(2)}) async-start(f32[16,2,5,128]{3,1,2,0:T(2,128)} %broadcast_in_dim.466), calls=%async_computation | async-start | bytes 163840 | tf_op jit(solution)/shard_map/all_to_all | solution.py:34
  140.9 38.9 %collective-permute-start.2 = (f32[256,128]{1,0:T(8,128)}, f32[256,128]{1,0:T(8,128)}, u32[]{:S(2)}, u32[]{:S(2)}) collective-permute-start(f32[256,128]{1,0:T(8,128)} %maximum_add_fusion.5), channel_id=1, source_target_pairs={{0,16},{1,17},{2,18},{3,19},{4,20},{5,21},{6,22},{7,23},{8,24},{9,... | collective-permute-start | bytes 393224 | tf_op jit(solution)/shard_map/ppermute | solution.py:19
  155.4 19.1 %all-to-all-start.1 = ((f32[8,112,128]{2,1,0:T(8,128)}), f32[8,112,128]{2,1,0:T(8,128)S(1)}, u32[]{:S(2)}, u32[]{:S(2)}) async-start(f32[8,112,128]{2,1,0:T(8,128)} %bitcast.3756), calls=%async_computation.1 | async-start | bytes 917504 | tf_op jit(solution)/shard_map/all_to_all | solution.py:83
  175.3 17.0 %all-to-all-start.2 = ((f32[8,112,128]{2,1,0:T(8,128)}), f32[8,112,128]{2,1,0:T(8,128)S(1)}, u32[]{:S(2)}, u32[]{:S(2)}) async-start(f32[8,112,128]{2,1,0:T(8,128)} %broadcast_in_dim.467), calls=%async_computation.2 | async-start | bytes 917504 | tf_op jit(solution)/shard_map/all_to_all | solution.py:34
  192.3 1.8 collective-permute-start.4
  201.2 21.7 %copy-start.217 = (f32[128]{0:T(128)}, f32[128]{0:T(128)S(1)}, u32[]{:S(2)}) copy-start(f32[128]{0:T(128)S(1)} %fusion.287) | copy-start | bytes 1540
  202.4 19.8 %copy-start.219 = (f32[128]{0:T(128)}, f32[128]{0:T(128)S(1)}, u32[]{:S(2)}) copy-start(f32[128]{0:T(128)S(1)} %fusion.292) | copy-start | bytes 1540
  203.5 19.4 %copy-start.149 = (f32[128]{0:T(128)}, f32[128]{0:T(128)S(1)}, u32[]{:S(2)}) copy-start(f32[128]{0:T(128)S(1)} %fusion.297) | copy-start | bytes 1540
  204.6 17.6 %copy-start.151 = (f32[128]{0:T(128)}, f32[128]{0:T(128)S(1)}, u32[]{:S(2)}) copy-start(f32[128]{0:T(128)S(1)} %fusion.302) | copy-start | bytes 1540
  205.7 15.5 %copy-start.157 = (f32[128]{0:T(128)}, f32[128]{0:T(128)S(1)}, u32[]{:S(2)}) copy-start(f32[128]{0:T(128)S(1)} %fusion.307) | copy-start | bytes 1540
  211.6 16.9 %copy-start.221 = (f32[128]{0:T(128)}, f32[128]{0:T(128)S(1)}, u32[]{:S(2)}) copy-start(f32[128]{0:T(128)S(1)} %fusion.262) | copy-start | bytes 1540
  212.2 15.5 %copy-start.223 = (f32[128]{0:T(128)}, f32[128]{0:T(128)S(1)}, u32[]{:S(2)}) copy-start(f32[128]{0:T(128)S(1)} %fusion.267) | copy-start | bytes 1540
  213.4 14.4 %copy-start.153 = (f32[128]{0:T(128)}, f32[128]{0:T(128)S(1)}, u32[]{:S(2)}) copy-start(f32[128]{0:T(128)S(1)} %fusion.330) | copy-start | bytes 1540
  230.0 10.9 %all-to-all-start.3 = ((f32[16,2,3,128]{3,1,2,0:T(2,128)}), f32[16,2,3,128]{3,1,2,0:T(2,128)}, u32[]{:S(2)}, u32[]{:S(2)}) async-start(f32[16,2,3,128]{3,1,2,0:T(2,128)} %broadcast_in_dim.468), calls=%async_computation.3 | async-start | bytes 98304 | tf_op jit(solution)/shard_map/all_to_all | solution.py:34
  267.4 3.1 collective-permute-start.5
  302.8 12.5 %all-to-all-start.4 = ((f32[16,2,5,128]{3,1,2,0:T(2,128)}), f32[16,2,5,128]{3,1,2,0:T(2,128)S(1)}, u32[]{:S(2)}, u32[]{:S(2)}) async-start(f32[16,2,5,128]{3,1,2,0:T(2,128)} %broadcast_in_dim.469), calls=%async_computation.4 | async-start | bytes 163840 | tf_op jit(solution)/shard_map/all_to_all | solution.py:34
  344.1 10.4 %all-to-all-start.5 = ((f32[16,2,3,128]{3,1,2,0:T(2,128)}), f32[16,2,3,128]{3,1,2,0:T(2,128)S(1)}, u32[]{:S(2)}, u32[]{:S(2)}) async-start(f32[16,2,3,128]{3,1,2,0:T(2,128)} %broadcast_in_dim.470), calls=%async_computation.5 | async-start | bytes 98304 | tf_op jit(solution)/shard_map/all_to_all | solution.py:34
  360.6 5.1 %collective-permute-start.6 = (f32[2,5,128]{2,1,0:T(8,128)S(1)}, f32[2,5,128]{2,1,0:T(8,128)S(1)}, u32[]{:S(2)}, u32[]{:S(2)}) collective-permute-start(f32[2,5,128]{2,1,0:T(8,128)S(1)} %pad_maximum_fusion.8), channel_id=1, source_target_pairs={{0,16},{1,17},{2,18},{3,19},{4,20},{5,21},{6,22},{7,23},{8,24},{9,... | collective-permute-start | bytes 15368 | tf_op jit(solution)/shard_map/ppermute | solution.py:19
  (269 other events, 490.4 us)

commit v2 on v0

v2 whole, which is shorter than its diff:
```python
import functools

import jax
import jax.numpy as jnp
from jax import lax
from jax.experimental import pallas as pl
from jax.experimental.pallas import tpu as pltpu
from jax.sharding import PartitionSpec as P

FINE_MAX = 8
FINE_MIN = 4
CLASSES = FINE_MAX - FINE_MIN + 1
MATS = 7
ROWS = 8
F32 = jnp.float32
BF16 = jnp.bfloat16


def high_low(x):
    high = x.astype(BF16).astype(F32)
    return high, x - high


def stacked(w):
    high, low = high_low(w)
    return jnp.concatenate([high, low], axis=0).astype(BF16)


def mul(x, w):
    rows = x.shape[0]
    high, low = high_low(x)
    left = jnp.concatenate([high, low], axis=0).astype(BF16)
    right = jnp.concatenate([high, jnp.zeros_like(low)], axis=0).astype(BF16)
    out = jnp.dot(jnp.concatenate([left, right], axis=1), w, preferred_element_type=F32)
    return out[:rows] + out[rows:]


def row_is(i, shape):
    return lax.broadcasted_iota(jnp.int32, shape, 0) == i


def leading():
    return lax.axis_index("tm") == 0


def from_behind(block, axis, distance):
    devices = range(lax.axis_size(axis))
    route = [(i - distance, i) for i in devices if i - distance in devices]
    return lax.ppermute(block, axis, route)


def swap_core(block):
    n = lax.axis_size("cell")
    return lax.ppermute(block, "cell", [(i, i ^ 1) for i in range(n)])


def same_core():
    n = lax.axis_size("cell")
    return [list(range(c, n, 2)) for c in range(2)]


def exchange(block, groups=None):
    return lax.all_to_all(block, "cell", 0, 0, axis_index_groups=groups)


def call(kernel, name, outs, args, scratch=(), flops=0):
    size = sum(x.size * x.dtype.itemsize for x in args)
    size += sum(x.size * x.dtype.itemsize for x in outs)
    return pl.pallas_call(
        kernel,
        out_shape=outs,
        in_specs=[pl.BlockSpec(memory_space=pltpu.VMEM)] * len(args),
        out_specs=[pl.BlockSpec(memory_space=pltpu.VMEM)] * len(outs),
        scratch_shapes=list(scratch),
        compiler_params=pltpu.CompilerParams(vmem_limit_bytes=24 << 20),
        cost_estimate=pl.CostEstimate(flops=flops, bytes_accessed=size, transcendentals=0),
        name=name,
    )(*args)


def shape(*dims, dtype=F32):
    return jax.ShapeDtypeStruct(dims, dtype)


def group_rows(g, per):
    return slice(g * per, (g + 1) * per)


def block(d, width):
    return slice((d - 1) * width, d * width)


def coarse_kernel(start, received, source, coarse, out):
    slices, groups, width, _ = coarse.shape
    per = start.shape[0] // groups
    for g in range(groups):
        here = group_rows(g, per)
        u = jnp.where(leading(), start[here], received[here])
        for l in range(slices):
            u = mul(u + source[l, here], stacked(coarse[l, g]))
        out[here] = u


def setup_kernel(everyone, fine, rate, counts, own, other, powers, spread, active):
    slices, groups, width, _ = fine.shape
    per = counts.shape[1]
    half = slices // 2
    keep = 1.0 - rate[...]
    core = lax.rem(lax.axis_index("cell"), 2)
    alive = []
    for g in range(groups):
        k = counts[g:g + 1].astype(F32)
        spread[group_rows(g, per)] = jnp.broadcast_to(k, (per, per)).T
        rows = [
            jnp.sum((k >= q).astype(F32), axis=1, keepdims=True)
            for q in range(FINE_MIN, FINE_MAX + 1)
        ]
        alive.append(rows)
        filled = jnp.zeros((ROWS, width), F32)
        for i, n in enumerate(rows):
            filled = jnp.where(row_is(i, filled.shape), n, filled)
        active[g] = filled
    for l in range(slices):
        sums = [0.0] * 4
        e6, e7, e72 = 0.0, 0.0, 0.0
        for g in range(groups):
            w1 = fine[l, g]
            st1 = stacked(w1)
            w2 = mul(w1 * keep, st1)
            st2 = stacked(w2)
            first = jnp.concatenate([w1, w2], axis=0)
            w34 = mul(first * keep, st2)
            w3, w4 = w34[:width], w34[width:]
            st4 = stacked(w4)
            w58 = mul(jnp.concatenate([first, w34], axis=0) * keep, st4)
            powers[l, g, :, block(1, width)] = st1
            powers[l, g, :, block(2, width)] = st2
            powers[l, g, :, block(3, width)] = stacked(w3)
            powers[l, g, :, block(4, width)] = st4
            for i in range(4):
                powers[l, g, :, block(5 + i, width)] = stacked(w58[i * width:(i + 1) * width])
            sums = [t + w for t, w in zip(sums, (w1, w2, w3, w4))]
            e6 = e6 + alive[g][2] * w1
            e7 = e7 + alive[g][3] * w1
            e72 = e72 + alive[g][3] * w2
        mats = [t * (per / everyone) for t in sums]
        mats += [e6 / everyone, (e6 + e72 - e7) / everyone, e7 / everyone]
        for i, m in enumerate(mats):
            at = slice(((l % half) * MATS + i) * width, ((l % half) * MATS + i + 1) * width)

            @pl.when(core == l // half)
            def _():
                own[at] = m

            @pl.when(core != l // half)
            def _():
                other[at] = m


def class_sums(state, k):
    mask = k >= (FINE_MIN + lax.broadcasted_iota(jnp.int32, (ROWS, k.shape[1]), 0))
    mask = mask.astype(F32)
    left = jnp.concatenate([mask, mask], axis=1)
    left = jnp.concatenate([left, jnp.zeros_like(left)], axis=0).astype(BF16)
    return jnp.dot(left, stacked(state), preferred_element_type=F32)[:ROWS]


def picked(products, first, width):
    out = jnp.zeros((ROWS, width), F32)
    for i in range(CLASSES):
        d = first + i
        if 1 <= d <= FINE_MAX:
            out = out + jnp.where(row_is(i, out.shape), products[:, block(d, width)], 0.0)
    return out


def sums_of_state(V, keep, powers, width):
    x = mul(V * keep, powers)
    rows = [V[0:1]] + [x[0:1, block(m, width)] for m in range(1, FINE_MIN + 1)]
    gain = picked(x, FINE_MIN, width) - picked(x, FINE_MIN - 1, width)
    for i in range(1, 4):
        rows.append(rows[-1] + gain[i:i + 1])
    return jnp.concatenate(rows, axis=0)


def sums_of_source(S, powers, width):
    x = mul(S, powers)
    rows = [jnp.zeros((1, width), F32)]
    for m in range(1, FINE_MAX):
        i = max(m - FINE_MIN, 0)
        rows.append(rows[-1] + x[i:i + 1, block(m, width)])
    return jnp.concatenate(rows, axis=0)


def by_count(products, k, first, width):
    out = jnp.zeros(k.shape, F32)
    for i in range(CLASSES):
        d = i * width
        out = jnp.where(k == float(FINE_MIN + i), products[:, d:d + width], out)
    return out


def fine_of_state(v, keep, powers, k, width):
    return by_count(mul(v * keep, powers), k, FINE_MIN, width)


def start_kernel(everyone, initial, received, source, coarse, powers, rate, counts, spread,
                 base, ofsource, starts, fines, sourced):
    slices, groups, width, _ = coarse.shape
    per = counts.shape[1]
    keep = 1.0 - rate[...]
    states = [
        jnp.where(leading(), initial[group_rows(g, per)], received[group_rows(g, per)])
        for g in range(groups)
    ]
    for l in range(slices):
        rows, rows_source = 0.0, 0.0
        for g in range(groups):
            here = group_rows(g, per)
            k = counts[g:g + 1]
            u, s, w = states[g], source[l, here], powers[l, g]
            starts[l, here] = u
            rows = rows + sums_of_state(class_sums(u, k), keep, w, width)
            rows_source = rows_source + sums_of_source(class_sums(s, k), w, width)
            if l + 1 < slices:
                states[g] = mul(u + s, stacked(coarse[l, g]))
        rows_source = rows_source / everyone
        at = slice(l * ROWS, (l + 1) * ROWS)
        ofsource[at] = rows_source
        base[at] = rows / everyone + rows_source
    for l in range(slices):
        for g in range(groups):
            here = group_rows(g, per)
            n = spread[here]
            w = powers[l, g]
            x = mul(source[l, here], w)
            total = x[:, block(1, width)]
            for d in range(2, FINE_MIN + 1):
                total = total + x[:, block(d, width)]
            out = jnp.where(n == float(FINE_MIN), total, 0.0)
            for d in range(FINE_MIN + 1, FINE_MAX + 1):
                total = total + x[:, block(d, width)]
                out = jnp.where(n == float(d), total, out)
            sourced[l, here] = out
            v = starts[l, here]
            w = powers[l, g, :, (FINE_MIN - 1) * width:]
            fines[l, here] = out + fine_of_state(v, keep, w, n, width)


def chain_kernel(start, received, old, fines, coarse, out):
    slices, groups, _, _ = coarse.shape
    per = start.shape[0] // groups
    for g in range(groups):
        here = group_rows(g, per)
        u = jnp.where(leading(), start[here], received[here])
        for l in range(slices):
            u = fines[l, here] + mul(u - old[l, here], stacked(coarse[l, g]))
        out[here] = u


def again_kernel(start, received, old, fines, sourced, coarse, powers, rate, counts, spread,
                 starts, fines_out, sums):
    slices, groups, width, _ = coarse.shape
    per = counts.shape[1]
    keep = 1.0 - rate[...]
    for g in range(groups):
        here = group_rows(g, per)
        n = spread[here]
        u = jnp.where(leading(), start[here], received[here])
        for l in range(slices):
            starts[l, here] = u
            sums[l, g] = class_sums(u, counts[g:g + 1])
            w = powers[l, g, :, (FINE_MIN - 1) * width:]
            fines_out[l, here] = sourced[l, here] + fine_of_state(u, keep, w, n, width)
            if l + 1 < slices:
                u = fines[l, here] + mul(u - old[l, here], stacked(coarse[l, g]))


def ends_kernel(start, received, old, fines, coarse, out):
    slices, groups, _, _ = coarse.shape
    per = start.shape[0] // groups
    for g in range(groups):
        here = group_rows(g, per)
        u = jnp.where(leading(), start[here], received[here])
        for l in range(slices):
            u = fines[l, here] + mul(u - old[l, here], stacked(coarse[l, g]))
            out[l, here] = u


def gather_kernel(parts, base, out):
    n, rows, _ = parts.shape
    total = parts[0]
    for p in range(1, n):
        total = total + parts[p]
    for p in range(n):
        out[p, :rows] = total
        out[p, rows:] = base[...]


def wide(row):
    return jnp.broadcast_to(row, (ROWS, row.shape[-1]))


def assembled(known, width):
    out = jnp.zeros((ROWS, width), F32)
    for m, a in enumerate(known):
        out = jnp.where(row_is(m, out.shape), a, out)
    return out


def first_averages(rows, mixing, rate, width):
    known, sent = [], []
    for m in range(FINE_MIN + 1):
        a = wide(rows[m:m + 1])
        for j in range(m):
            a = a + sent[j][:, block(m - j, width)]
        known.append(a)
        if m < FINE_MIN:
            sent.append(mul(a * rate, mixing[:, :(FINE_MIN - m) * width]))
    return assembled(known, width)


def folded(a, rate, powers, width):
    x = mul(a * rate, powers)
    out = jnp.zeros((2 * ROWS, width), F32)
    for d in range(1, FINE_MAX + 1):
        z = jnp.concatenate([x[:, block(d, width)], jnp.zeros((ROWS, width), F32)], axis=0)
        out = out + pltpu.roll(z, d, 0)
    return out


def second_rows(everyone, per, a, base, rate, powers, active, l, width):
    groups = powers.shape[1]
    rows = [0.0] * 3
    for g in range(groups):
        h = folded(a, rate, powers[l, g], width)
        total = per * h[4:5]
        for i in range(1, 4):
            total = total + active[g, i:i + 1] * (h[4 + i:5 + i] - h[3 + i:4 + i])
            rows[i - 1] = rows[i - 1] + total
    at = l * ROWS + FINE_MIN + 1
    return [rows[i] / everyone + base[at + i:at + i + 1] for i in range(3)]


def send_rows(everyone, per, a, base, rate, powers, active, out, width):
    slices = powers.shape[0]
    rows = []
    for l in range(slices):
        rows += second_rows(everyone, per, a[l], base, rate, powers, active, l, width)
        rows.append(jnp.zeros((1, width), F32))
    rows = jnp.concatenate(rows, axis=0)
    for p in range(out.shape[0]):
        out[p] = rows


def mixing_kernel(everyone, per, mine, theirs, base, powers, rate, active,
                  mixing, averages, out, held):
    slices, _, _, wider = powers.shape
    width = wider // FINE_MAX
    half = slices // 2
    n, rows, _ = mine.shape
    rows -= slices * ROWS
    core = lax.rem(lax.axis_index("cell"), 2)
    mixed = 0.0
    for ref, at in ((mine, core), (theirs, 1 - core)):
        for p in range(n):
            place = at * (half * MATS * width) + p * rows
            held[pl.ds(place, rows), :] = ref[p, :rows]
            mixed = mixed + ref[p, rows:]
    a = []
    for l in range(slices):
        for i in range(MATS):
            at = (l * MATS + i) * width
            mixing[l, :, block(i + 1, width)] = stacked(held[at:at + width])
        a.append(first_averages(mixed[l * ROWS:(l + 1) * ROWS], mixing[l], rate[...], width))
        averages[l] = a[-1]
    send_rows(everyone, per, a, base, rate[...], powers, active, out, width)


def first_kernel(everyone, per, received, base, mixing, powers, rate, active, averages, out):
    slices, _, _, wider = powers.shape
    width = wider // FINE_MAX
    total = received[0]
    for p in range(1, received.shape[0]):
        total = total + received[p]
    a = []
    for l in range(slices):
        rows = total[l * (FINE_MIN + 1):(l + 1) * (FINE_MIN + 1)]
        a.append(first_averages(rows, mixing[l], rate[...], width))
        averages[l] = a[-1]
    send_rows(everyone, per, a, base, rate[...], powers, active, out, width)


def push_kernel(received, averages, mixing, powers, rate, coarse, *refs):
    if len(refs) == 2:
        plain, starts, (pushes, end) = None, None, refs
    else:
        plain, starts, pushes, end = refs
    slices, groups, _, wider = powers.shape
    width = wider // FINE_MAX
    r = rate[...]
    total = received[0]
    for p in range(1, received.shape[0]):
        total = total + received[p]
    x = [jnp.zeros((ROWS, width), F32) for _ in range(groups)]
    for l in range(slices):
        a5 = wide(total[l * 4:l * 4 + 1])
        z = mul(a5 * r, mixing[l, :, 4 * width:6 * width])
        a6 = wide(total[l * 4 + 1:l * 4 + 2]) + z[:, :width]
        a7 = wide(total[l * 4 + 2:l * 4 + 3]) + z[:, width:]
        a7 = a7 + mul(a6 * r, mixing[l, :, 6 * width:])
        a = averages[l]
        for m, row in ((5, a5), (6, a6), (7, a7)):
            a = jnp.where(row_is(m, a.shape), row, a)
        for g in range(groups):
            h = folded(a, r, powers[l, g], width)[FINE_MIN:FINE_MIN + ROWS]
            if plain is not None:
                h = h + plain[l, g]
            pushes[l, g] = h
            old = x[g] if starts is None else x[g] - starts[l, g]
            x[g] = h + mul(old, stacked(coarse[l, g]))
    for g in range(groups):
        end[g] = x[g]


def vectors_kernel(received, pushes, starts, coarse, end):
    slices, groups, _, _ = coarse.shape
    for g in range(groups):
        x = jnp.where(leading(), 0.0, received[g])
        for l in range(slices):
            x = pushes[l, g] + mul(x - starts[l, g], stacked(coarse[l, g]))
        end[g] = x


def second_kernel(everyone, received, pushes, coarse, sums, active, powers, rate, ofsource,
                  starts, base, out):
    slices, groups, width, _ = coarse.shape
    keep = 1.0 - rate[...]
    x = [jnp.where(leading(), 0.0, received[g]) for g in range(groups)]
    sent = []
    for l in range(slices):
        rows = 0.0
        for g in range(groups):
            starts[l, g] = x[g]
            n = active[g]
            exact = n - pltpu.roll(n, ROWS - 1, 0)
            exact = jnp.where(row_is(ROWS - 1, n.shape), 0.0, exact)
            weighted = exact * x[g]
            tail = jnp.zeros((1, width), F32)
            V = sums[l, g]
            for i in reversed(range(CLASSES)):
                tail = tail + weighted[i:i + 1]
                V = jnp.where(row_is(i, V.shape), V + tail, V)
            rows = rows + sums_of_state(V, keep, powers[l, g], width)
            if l + 1 < slices:
                x[g] = pushes[l, g] + mul(x[g], stacked(coarse[l, g]))
        at = slice(l * ROWS, (l + 1) * ROWS)
        rows = rows / everyone + ofsource[at]
        base[at] = rows
        sent.append(rows[:FINE_MIN + 1])
    sent = jnp.concatenate(sent, axis=0)
    for p in range(out.shape[0]):
        out[p] = sent


def plain_kernel(starts, powers, rate, out):
    slices, groups, _, wider = powers.shape
    width = wider // FINE_MAX
    keep = 1.0 - rate[...]
    for l in range(slices):
        for g in range(groups):
            out[l, g] = picked(mul(starts[l, g] * keep, powers[l, g]), FINE_MIN, width)


def finish_kernel(received, pushes, starts, coarse, ends, spread, out):
    slices, groups, width, _ = coarse.shape
    per = spread.shape[0] // groups
    for g in range(groups):
        here = group_rows(g, per)
        n = spread[here]
        x = jnp.where(leading(), 0.0, received[g])
        for l in range(slices):
            x = pushes[l, g] + mul(x - starts[l, g], stacked(coarse[l, g]))
            add = jnp.zeros((per, width), F32)
            for i in range(CLASSES):
                add = jnp.where(n == float(FINE_MIN + i), x[i:i + 1], add)
            out[l, here] = ends[l, here] + add


def body(initial, source, mix_rate, fine, coarse, step_counts):
    slices, groups, width, _ = fine.shape
    cells = initial.shape[0]
    per = cells // groups
    n_cell = lax.axis_size("cell")
    turns = lax.axis_size("tm") - 1
    everyone = cells * n_cell
    half = slices // 2
    peers = n_cell // 2
    shard = half * MATS * width // peers
    rate = mix_rate.reshape(1, width)
    counts = step_counts.reshape(groups, per)
    state = shape(cells, width)
    states = shape(slices, cells, width)
    vectors = shape(slices, groups, ROWS, width)
    vector = shape(groups, ROWS, width)
    rows8 = shape(slices * ROWS, width)
    rows4 = shape(n_cell, slices * 4, width)
    averages = shape(slices, ROWS, width)

    def handed(first, advance):
        received = first
        for _ in range(turns):
            received = from_behind(advance(received), "tm", 1)
        return received

    received = handed(
        initial, lambda u: call(coarse_kernel, "coarse", [state], (initial, u, source, coarse))[0]
    )
    mats = shape(half * MATS * width, width)
    own, other, powers, spread, active = call(
        functools.partial(setup_kernel, everyone), "setup",
        [mats, mats, shape(slices, groups, 2 * width, FINE_MAX * width, dtype=BF16), state, vector],
        (fine, rate, counts),
    )
    mine = (own + swap_core(other)).reshape(peers, shard, width)
    parts = exchange(mine, same_core())
    base, ofsource, starts0, fines1, sourced = call(
        functools.partial(start_kernel, everyone), "start",
        [rows8, rows8, states, states, states],
        (initial, received, source, coarse, powers, rate, counts, spread),
    )
    payload, = call(
        gather_kernel, "gather", [shape(peers, shard + slices * ROWS, width)], (parts, base)
    )
    gathered = exchange(payload, same_core())
    received = handed(
        initial,
        lambda u: call(chain_kernel, "chain", [state], (initial, u, starts0, fines1, coarse))[0],
    )
    starts1, fines2, sums = call(
        again_kernel, "again", [states, states, vectors],
        (initial, received, starts0, fines1, sourced, coarse, powers, rate, counts, spread),
    )
    theirs = swap_core(gathered)
    mixing, first, out = call(
        functools.partial(mixing_kernel, everyone, per), "mixing",
        [shape(slices, 2 * width, MATS * width, dtype=BF16), averages, rows4],
        (gathered, theirs, base, powers, rate, active),
        scratch=[pltpu.VMEM((slices * MATS * width, width), F32)],
    )
    pushes1, end = call(
        push_kernel, "push", [vectors, vector],
        (exchange(out), first, mixing, powers, rate, coarse),
    )
    nothing = jnp.zeros(vectors.shape, F32)
    moved = end
    for turn in range(turns):
        moved = from_behind(moved, "tm", 1)
        if turn + 1 < turns:
            moved, = call(vectors_kernel, "vectors", [vector], (moved, pushes1, nothing, coarse))
    moved1, base, out = call(
        functools.partial(second_kernel, everyone), "second",
        [vectors, rows8, shape(n_cell, slices * (FINE_MIN + 1), width)],
        (moved, pushes1, coarse, sums, active, powers, rate, ofsource),
    )
    got = exchange(out)
    plain, = call(plain_kernel, "plain", [vectors], (moved1, powers, rate))
    received = handed(
        initial,
        lambda u: call(chain_kernel, "chain", [state], (initial, u, starts1, fines2, coarse))[0],
    )
    ends, = call(
        ends_kernel, "ends", [states], (initial, received, starts1, fines2, coarse)
    )
    first, out = call(
        functools.partial(first_kernel, everyone, per), "first", [averages, rows4],
        (got, base, mixing, powers, rate, active),
    )
    pushes2, end = call(
        push_kernel, "push", [vectors, vector],
        (exchange(out), first, mixing, powers, rate, coarse, plain, moved1),
    )
    moved = end
    for turn in range(turns):
        moved = from_behind(moved, "tm", 1)
        if turn + 1 < turns:
            moved, = call(vectors_kernel, "vectors", [vector], (moved, pushes2, moved1, coarse))
    out, = call(
        finish_kernel, "finish", [states], (moved, pushes2, moved1, coarse, ends, spread)
    )
    return out


def solution(mesh):
    return jax.shard_map(
        body,
        mesh=mesh,
        in_specs=(
            P("cell", None),
            P("tm", "cell", None),
            P(),
            P("tm", "cell", None, None),
            P("tm", "cell", None, None),
            P("cell"),
        ),
        out_specs=P("tm", "cell", None),
        check_vma=False,
    )
```

time: 516 us -> 107 us (0.21)
  blocking collectives: 475 us -> 29.7 us
  starting transfers between devices: 13.7 us -> 32.8 us
  Pallas kernels: 0 us -> 18.7 us
  matrix products: 11.5 us -> 0 us
  local copies, waits for them, and re-layouts: 4.91 us -> 15.5 us
    psum x16 -> x0, blocking collectives: 475 us -> none  [body(): average = lax.psum(jnp.sum(state, axis=1), 'cell') / total]
    all_to_all x0 -> x2, blocking collectives: none -> 29.7 us  [exchange(): return lax.all_to_all(block, 'cell', 0, 0, axis_index_groups=groups)]
    pallas_call x0 -> x15, Pallas kernels: none -> 18.7 us  [call(): pl.pallas_call(kernel, out_shape=outs, in_specs=[pl.BlockSpec(memory_spac...]
    all_to_all x0 -> x3, starting transfers between devices: none -> 15.5 us  [exchange(): return lax.all_to_all(block, 'cell', 0, 0, axis_index_groups=groups)]
    dot_general x28 -> x0, matrix products: 11.5 us -> none  [the longest x19 9.1 us: slices_mul(): jnp.einsum('lgcs,lgst->lgct', shaped, matrices, precision=lax.Precision.H...]
    unnamed x18 -> x78, local copies, waits for them, and re-layouts: 4.26 us -> 15.5 us
    ppermute x3 -> x5, starting transfers between devices: 13.7 us -> 16.8 us  [from_behind(): return lax.ppermute(block, axis, route)]
  transfers between devices with their start and end apart: 3 -> 10, of which waited for: 3 -> 4; matrix products, arithmetic and copies ran while one was open for 0% -> 0% of each run, Pallas kernels for 0% -> 11%
where the time goes in v2:
time: 107 us; the launch traced here: 106 us
  starting transfers between devices  32.8 us (31%)
  blocking collectives  29.7 us (28%)
  Pallas kernels  18.7 us (17%)
  local copies, waits for them, and re-layouts  15.5 us (14%)
  waiting for transfers between devices  8.28 us (8%)
    all_to_all x2, blocking collectives, exchange(): return lax.all_to_all(block, 'cell', 0, 0, axis_index_groups=groups)  29.7 us
    pallas_call x15, Pallas kernels, call(): pl.pallas_call(kernel, out_shape=outs, in_specs=[pl.BlockSpec(memory_spac...  18.7 us
    ppermute x5, starting transfers between devices, from_behind(): return lax.ppermute(block, axis, route)  16.8 us
    unnamed x78, local copies, waits for them, and re-layouts  15.5 us
    all_to_all x3, starting transfers between devices, exchange(): return lax.all_to_all(block, 'cell', 0, 0, axis_index_groups=groups)  15.5 us
    ppermute x2, waiting for transfers between devices, swap_core(): return lax.ppermute(block, 'cell', [(i, i ^ 1) for i in range(n)])  3.35 us
    ppermute x5, waiting for transfers between devices, from_behind(): return lax.ppermute(block, axis, route)  2.76 us
    all_to_all x3, waiting for transfers between devices, exchange(): return lax.all_to_all(block, 'cell', 0, 0, axis_index_groups=groups)  2.16 us
  transfers between devices with their start and end apart: 10, of which 4 were waited for; matrix products, arithmetic and copies ran while one was open for 0% of the time, Pallas kernels for 11%

profile of v2, /device:TPU:0, one launch (start us, length us, event | category | flops | bytes accessed | tf_op | source)
XLA Modules:
  0.0 106.3 jit_solution(5133412330060865251)
XLA Ops:
  2.4 2.6 %setup.1 = (f32[896,128]{1,0:T(8,128)S(1)}, f32[896,128]{1,0:T(8,128)S(1)}, bf16[2,2,256,1024]{3,2,1,0:T(8,128)(2,1)S(1)}, f32[256,128]{1,0:T(8,128)S(1)}, f32[2,8,128]{2,1,0:T(8,128)S(1)}) custom-call(f32[2,2,128,128]{3,2,1,0:T(8,128)S(1)} %copy-done.15, f32[1,128]{1,0:T(1,128)S(1)} %bitcast.3, s32[2,128]{1,0:T(2,128)S(1)} %bitcast.12), custom_call_target="tpu_custom_call" | custom-call | bytes 3417600 | tf_op jit(solution)/shard_map/setup/pallas_call | solution.py:69
  5.6 1.4 %collective-permute-done = f32[896,128]{1,0:T(8,128)S(1)} collective-permute-done((f32[896,128]{1,0:T(8,128)S(1)}, f32[896,128]{1,0:T(8,128)S(1)}, u32[]{:S(2)}, u32[]{:S(2)}) %collective-permute-start) | collective-permute-done | bytes 458784 | tf_op jit(solution)/shard_map/ppermute | solution.py:54
  7.8 7.2 %all-to-all-start = ((f32[8,112,128]{2,1,0:T(8,128)}), f32[8,112,128]{2,1,0:T(8,128)S(1)}, u32[]{:S(2)}, u32[]{:S(2)}) async-start(f32[8,112,128]{2,1,0:T(8,128)} %bitcast.15), calls=%async_computation | async-start | bytes 917504 | tf_op jit(solution)/shard_map/all_to_all | solution.py:63
  15.5 3.4 %collective-permute-start.1 = (f32[256,128]{1,0:T(8,128)S(1)}, f32[256,128]{1,0:T(8,128)S(1)}, u32[]{:S(2)}, u32[]{:S(2)}) collective-permute-start(f32[256,128]{1,0:T(8,128)S(1)} %coarse.11), channel_id=1, source_target_pairs={{0,16},{1,17},{2,18},{3,19},{4,20},{5,21},{6,22},{7,23},{8,24},{9,... | collective-permute-start | bytes 393224 | tf_op jit(solution)/shard_map/ppermute | solution.py:49
  18.9 2.8 %collective-permute-done.1.received = f32[256,128]{1,0:T(8,128)S(1)} collective-permute-done((f32[256,128]{1,0:T(8,128)S(1)}, f32[256,128]{1,0:T(8,128)S(1)}, u32[]{:S(2)}, u32[]{:S(2)}) %collective-permute-start.1) | collective-permute-done | bytes 131104 | tf_op jit(solution)/shard_map/ppermute | solution.py:49
  21.7 2.5 %start.7 = (f32[16,128]{1,0:T(8,128)S(1)}, f32[16,128]{1,0:T(8,128)S(1)}, f32[2,256,128]{2,1,0:T(8,128)S(1)}, f32[2,256,128]{2,1,0:T(8,128)S(1)}, f32[2,256,128]{2,1,0:T(8,128)S(1)}) custom-call(f32[256,128]{1,0:T(8,128)S(1)} %copy-done.1, f32[256,128]{1,0:T(8,128)S(1)} %collective-permute-done.1.received, f32[2,256,128]{2,1,0:T(8,128)S(1)} %copy-done.2, ...), custom_call_target="tpu_custom_call" | custom-call | bytes 3819008 | tf_op jit(solution)/shard_map/start/pallas_call | solution.py:69
  26.3 2.2 %all-to-all-done.parts = f32[8,112,128]{2,1,0:T(8,128)S(1)} async-done(((f32[8,112,128]{2,1,0:T(8,128)}), f32[8,112,128]{2,1,0:T(8,128)S(1)}, u32[]{:S(2)}, u32[]{:S(2)}) %all-to-all-start) | async-done | bytes 458784 | tf_op jit(solution)/shard_map/all_to_all | solution.py:63
  28.5 18.1 %all_to_all.25.mine = f32[8,128,128]{2,1,0:T(8,128)S(1)} all-to-all(f32[8,128,128]{2,1,0:T(8,128)S(1)} %gather.1), channel_id=1, replica_groups={{0,2,4,6,8,10,12,14},{1,3,5,7,9,11,13,15},{16,18,20,22,24,26,28,30},{17..., dimensions={0} | all-to-all | bytes 1048576 | tf_op jit(solution)/shard_map/all_to_all | solution.py:63
  46.6 1.9 %collective-permute-done.2.theirs = f32[8,128,128]{2,1,0:T(8,128)S(1)} collective-permute-done((f32[8,128,128]{2,1,0:T(8,128)S(1)}, f32[8,128,128]{2,1,0:T(8,128)S(1)}, u32[]{:S(2)}, u32[]{:S(2)}) %collective-permute-start.2) | collective-permute-done | bytes 524320 | tf_op jit(solution)/shard_map/ppermute | solution.py:54
  49.2 1.3 %mixing.1 = (bf16[2,256,896]{2,1,0:T(8,128)(2,1)S(1)}, f32[2,8,128]{2,1,0:T(8,128)S(1)}, f32[16,8,128]{2,1,0:T(8,128)S(1)}) custom-call(f32[8,128,128]{2,1,0:T(8,128)S(1)} %all_to_all.25.mine, f32[8,128,128]{2,1,0:T(8,128)S(1)} %collective-permute-done.2.theirs, f32[16,128]{1,0:T(8,128)S(1)} %copy-done.30, ...), custom_call_target="tpu_custom_call" | custom-call | bytes 4153856 | tf_op jit(solution)/shard_map/mixing/pallas_call | solution.py:69
  51.7 4.1 %all-to-all-start.2 = ((f32[16,8,128]{2,1,0:T(8,128)}), f32[16,8,128]{2,1,0:T(8,128)}, u32[]{:S(2)}, u32[]{:S(2)}) async-start(f32[16,8,128]{2,1,0:T(8,128)} %copy-done.23), calls=%async_computation.2 | async-start | bytes 131072 | tf_op jit(solution)/shard_map/all_to_all | solution.py:63
  57.8 1.1 %chain.2 = f32[256,128]{1,0:T(8,128)} custom-call(f32[256,128]{1,0:T(8,128)S(1)} %copy-done.1, f32[256,128]{1,0:T(8,128)S(1)} %copy-done.1, f32[2,256,128]{2,1,0:T(8,128)S(1)} %copy-done.10, f32[2,256,128]{2,1,0:T(8,128)S(1)} %copy-done.13, f32[2,2,128,128]{3,2,1,0:T(8,128)S(1)} %copy-done), custom_call_target="tpu_custom_call" | custom-call | bytes 1179648 | tf_op jit(solution)/shard_map/chain/pallas_call | solution.py:69
  58.9 4.0 %collective-permute-start.4 = (f32[256,128]{1,0:T(8,128)}, f32[256,128]{1,0:T(8,128)}, u32[]{:S(2)}, u32[]{:S(2)}) collective-permute-start(f32[256,128]{1,0:T(8,128)} %chain.2), channel_id=1, source_target_pairs={{0,16},{1,17},{2,18},{3,19},{4,20},{5,21},{6,22},{7,23},{8,24},{9,... | collective-permute-start | bytes 393224 | tf_op jit(solution)/shard_map/ppermute | solution.py:49
  63.7 1.7 %push.2 = (f32[2,2,8,128]{3,2,1,0:T(8,128)S(1)}, f32[2,8,128]{2,1,0:T(8,128)S(1)}) custom-call(f32[16,8,128]{2,1,0:T(8,128)} %all-to-all-done.2.received, f32[2,8,128]{2,1,0:T(8,128)S(1)} %copy-done.38, bf16[2,256,896]{2,1,0:T(8,128)(2,1)S(1)} %get-tuple-element.38.mixing, bf16[2,2,256,1024]{3,2,1,0:T(8,128)(2,1)S(1)} %get-tuple-element.32.powers, ...), custom_call_target="tpu_custom_call" | custom-call | bytes 3375616 | tf_op jit(solution)/shard_map/push/pallas_call | solution.py:69
  65.5 3.4 %collective-permute-start.3 = (f32[2,8,128]{2,1,0:T(8,128)S(1)}, f32[2,8,128]{2,1,0:T(8,128)S(1)}, u32[]{:S(2)}, u32[]{:S(2)}) collective-permute-start(f32[2,8,128]{2,1,0:T(8,128)S(1)} %get-tuple-element.39), channel_id=1, source_target_pairs={{0,16},{1,17},{2,18},{3,19},{4,20},{5,21},{6,22},{7,23},{8,24},{9,... | collective-permute-start | bytes 24584 | tf_op jit(solution)/shard_map/ppermute | solution.py:49
  68.9 1.8 %again.1 = (f32[2,256,128]{2,1,0:T(8,128)S(1)}, f32[2,256,128]{2,1,0:T(8,128)S(1)}, f32[2,2,8,128]{3,2,1,0:T(8,128)S(1)}) custom-call(f32[256,128]{1,0:T(8,128)S(1)} %copy-done.1, f32[256,128]{1,0:T(8,128)} %collective-permute-done.4.received, f32[2,256,128]{2,1,0:T(8,128)S(1)} %copy-done.11, f32[2,256,128]{2,1,0:T(8,128)S(1)} %copy-done.14, ...), custom_call_target="tpu_custom_call" | custom-call | bytes 4081152 | tf_op jit(solution)/shard_map/again/pallas_call | solution.py:69
  71.3 11.6 %all_to_all.26.received = f32[16,10,128]{2,1,0:T(8,128)S(1)} all-to-all(f32[16,10,128]{2,1,0:T(8,128)S(1)} %get-tuple-element.46), channel_id=1, replica_groups=mesh['tm'=2,'cell'=16] {'cell'}, dimensions={0} | all-to-all | bytes 163840 | tf_op jit(solution)/shard_map/all_to_all | solution.py:63
  82.9 1.2 %first.1 = (f32[2,8,128]{2,1,0:T(8,128)S(1)}, f32[16,8,128]{2,1,0:T(8,128)S(1)}) custom-call(f32[16,10,128]{2,1,0:T(8,128)S(1)} %all_to_all.26.received, f32[16,128]{1,0:T(8,128)S(1)} %get-tuple-element.47.base, bf16[2,256,896]{2,1,0:T(8,128)(2,1)S(1)} %get-tuple-element.38.mixing, bf16[2,2,256,1024]{3,2,1,0:T(8,128)(2,1)S(1)} %get-tuple-element.32.powers, ...), custom_call_target="tpu_custom_call" | custom-call | bytes 3187200 | tf_op jit(solution)/shard_map/first/pallas_call | solution.py:69
  85.4 4.1 %all-to-all-start.4 = ((f32[16,8,128]{2,1,0:T(8,128)}), f32[16,8,128]{2,1,0:T(8,128)}, u32[]{:S(2)}, u32[]{:S(2)}) async-start(f32[16,8,128]{2,1,0:T(8,128)} %copy-done.22), calls=%async_computation.4 | async-start | bytes 131072 | tf_op jit(solution)/shard_map/all_to_all | solution.py:63
  91.4 1.1 %chain.3 = f32[256,128]{1,0:T(8,128)} custom-call(f32[256,128]{1,0:T(8,128)S(1)} %copy-done.1, f32[256,128]{1,0:T(8,128)S(1)} %copy-done.1, f32[2,256,128]{2,1,0:T(8,128)S(1)} %copy-done.4, f32[2,256,128]{2,1,0:T(8,128)S(1)} %copy-done.7, f32[2,2,128,128]{3,2,1,0:T(8,128)S(1)} %copy-done), custom_call_target="tpu_custom_call" | custom-call | bytes 1179648 | tf_op jit(solution)/shard_map/chain/pallas_call | solution.py:69
  92.5 4.2 %collective-permute-start.6 = (f32[256,128]{1,0:T(8,128)}, f32[256,128]{1,0:T(8,128)}, u32[]{:S(2)}, u32[]{:S(2)}) collective-permute-start(f32[256,128]{1,0:T(8,128)} %chain.3), channel_id=1, source_target_pairs={{0,16},{1,17},{2,18},{3,19},{4,20},{5,21},{6,22},{7,23},{8,24},{9,... | collective-permute-start | bytes 393224 | tf_op jit(solution)/shard_map/ppermute | solution.py:49
  100.5 1.7 %push.3 = (f32[2,2,8,128]{3,2,1,0:T(8,128)S(1)}, f32[2,8,128]{2,1,0:T(8,128)S(1)}) custom-call(f32[16,8,128]{2,1,0:T(8,128)} %all-to-all-done.4.received, f32[2,8,128]{2,1,0:T(8,128)S(1)} %copy-done.36, bf16[2,256,896]{2,1,0:T(8,128)(2,1)S(1)} %get-tuple-element.38.mixing, bf16[2,2,256,1024]{3,2,1,0:T(8,128)(2,1)S(1)} %get-tuple-element.32.powers, ...), custom_call_target="tpu_custom_call" | custom-call | bytes 3408384 | tf_op jit(solution)/shard_map/push/pallas_call | solution.py:69
  102.2 1.7 %collective-permute-start.5 = (f32[2,8,128]{2,1,0:T(8,128)S(1)}, f32[2,8,128]{2,1,0:T(8,128)S(1)}, u32[]{:S(2)}, u32[]{:S(2)}) collective-permute-start(f32[2,8,128]{2,1,0:T(8,128)S(1)} %get-tuple-element.51), channel_id=1, source_target_pairs={{0,16},{1,17},{2,18},{3,19},{4,20},{5,21},{6,22},{7,23},{8,24},{9,... | collective-permute-start | bytes 24584 | tf_op jit(solution)/shard_map/ppermute | solution.py:49
  103.9 1.3 %ends.1 = f32[2,256,128]{2,1,0:T(8,128)S(1)} custom-call(f32[256,128]{1,0:T(8,128)S(1)} %copy-done.1, f32[256,128]{1,0:T(8,128)} %collective-permute-done.6.received, f32[2,256,128]{2,1,0:T(8,128)S(1)} %copy-done.5, f32[2,256,128]{2,1,0:T(8,128)S(1)} %copy-done.8, f32[2,2,128,128]{3,2,1,0:T(8,128)S(1)} %copy-done), custom_call_target="tpu_custom_call" | custom-call | bytes 1310720 | tf_op jit(solution)/shard_map/ends/pallas_call | solution.py:69
  (92 shorter events, 19.2 us)
Async XLA Ops:
  0.0 15.0 %copy-start = (f32[2,2,128,128]{3,2,1,0:T(8,128)S(1)}, f32[2,2,128,128]{3,2,1,0:T(8,128)}, u32[]{:S(2)}) copy-start(f32[2,2,128,128]{3,2,1,0:T(8,128)} %coarse.21) | copy-start | bytes 786436
  0.0 15.0 %copy-start.1 = (f32[256,128]{1,0:T(8,128)S(1)}, f32[256,128]{1,0:T(8,128)}, u32[]{:S(2)}) copy-start(f32[256,128]{1,0:T(8,128)} %start.11) | copy-start | bytes 393220
  0.0 15.0 %copy-start.2 = (f32[2,256,128]{2,1,0:T(8,128)S(1)}, f32[2,256,128]{2,1,0:T(8,128)}, u32[]{:S(2)}) copy-start(f32[2,256,128]{2,1,0:T(8,128)} %source.3) | copy-start | bytes 786436
  2.4 19.3 %copy-start.25 = (f32[128]{0:T(128)S(1)}, f32[128]{0:T(128)}, u32[]{:S(2)}) copy-start(f32[128]{0:T(128)} %param.8) | copy-start | bytes 1540
  2.4 19.3 %copy-start.32 = (s32[256]{0:T(256)S(1)}, s32[256]{0:T(256)}, u32[]{:S(2)}) copy-start(s32[256]{0:T(256)} %param.11) | copy-start | bytes 3076
  5.0 43.5 %copy-start.18 = (f32[2,8,128]{2,1,0:T(8,128)}, f32[2,8,128]{2,1,0:T(8,128)S(1)}, u32[]{:S(2)}) copy-start(f32[2,8,128]{2,1,0:T(8,128)S(1)} %get-tuple-element.35.active) | copy-start | bytes 24580
  5.0 2.0 %collective-permute-start = (f32[896,128]{1,0:T(8,128)S(1)}, f32[896,128]{1,0:T(8,128)S(1)}, u32[]{:S(2)}, u32[]{:S(2)}) collective-permute-start(f32[896,128]{1,0:T(8,128)S(1)} %get-tuple-element.31), channel_id=1, source_target_pairs={{0,1},{1,0},{2,3},{3,2},{4,5},{5,4},{6,7},{7,6},{8,9},{9,8},{10,11... | collective-permute-start | bytes 1376264 | tf_op jit(solution)/shard_map/ppermute | solution.py:54
  7.8 20.6 %all-to-all-start = ((f32[8,112,128]{2,1,0:T(8,128)}), f32[8,112,128]{2,1,0:T(8,128)S(1)}, u32[]{:S(2)}, u32[]{:S(2)}) async-start(f32[8,112,128]{2,1,0:T(8,128)} %bitcast.15), calls=%async_computation | async-start | bytes 917504 | tf_op jit(solution)/shard_map/all_to_all | solution.py:63
  15.5 6.2 %collective-permute-start.1 = (f32[256,128]{1,0:T(8,128)S(1)}, f32[256,128]{1,0:T(8,128)S(1)}, u32[]{:S(2)}, u32[]{:S(2)}) collective-permute-start(f32[256,128]{1,0:T(8,128)S(1)} %coarse.11), channel_id=1, source_target_pairs={{0,16},{1,17},{2,18},{3,19},{4,20},{5,21},{6,22},{7,23},{8,24},{9,... | collective-permute-start | bytes 393224 | tf_op jit(solution)/shard_map/ppermute | solution.py:49
  26.3 22.2 %copy-start.29 = (f32[16,128]{1,0:T(8,128)}, f32[16,128]{1,0:T(8,128)S(1)}, u32[]{:S(2)}) copy-start(f32[16,128]{1,0:T(8,128)S(1)} %get-tuple-element.34.base) | copy-start | bytes 24580
  26.3 22.2 %copy-start.33 = (f32[16,128]{1,0:T(8,128)}, f32[16,128]{1,0:T(8,128)S(1)}, u32[]{:S(2)}) copy-start(f32[16,128]{1,0:T(8,128)S(1)} %get-tuple-element.45.ofsource) | copy-start | bytes 24580
  46.6 1.9 %collective-permute-start.2 = (f32[8,128,128]{2,1,0:T(8,128)S(1)}, f32[8,128,128]{2,1,0:T(8,128)S(1)}, u32[]{:S(2)}, u32[]{:S(2)}) collective-permute-start(f32[8,128,128]{2,1,0:T(8,128)S(1)} %all_to_all.25.mine), channel_id=1, source_target_pairs={{0,1},{1,0},{2,3},{3,2},{4,5},{5,4},{6,7},{7,6},{8,9},{9,8},{10,11... | collective-permute-start | bytes 1572872 | tf_op jit(solution)/shard_map/ppermute | solution.py:54
  51.7 11.2 %all-to-all-start.2 = ((f32[16,8,128]{2,1,0:T(8,128)}), f32[16,8,128]{2,1,0:T(8,128)}, u32[]{:S(2)}, u32[]{:S(2)}) async-start(f32[16,8,128]{2,1,0:T(8,128)} %copy-done.23), calls=%async_computation.2 | async-start | bytes 131072 | tf_op jit(solution)/shard_map/all_to_all | solution.py:63
  58.9 10.0 %collective-permute-start.4 = (f32[256,128]{1,0:T(8,128)}, f32[256,128]{1,0:T(8,128)}, u32[]{:S(2)}, u32[]{:S(2)}) collective-permute-start(f32[256,128]{1,0:T(8,128)} %chain.2), channel_id=1, source_target_pairs={{0,16},{1,17},{2,18},{3,19},{4,20},{5,21},{6,22},{7,23},{8,24},{9,... | collective-permute-start | bytes 393224 | tf_op jit(solution)/shard_map/ppermute | solution.py:49
  62.9 6.0 %copy-start.11 = (f32[2,256,128]{2,1,0:T(8,128)S(1)}, f32[2,256,128]{2,1,0:T(8,128)}, u32[]{:S(2)}) copy-start(f32[2,256,128]{2,1,0:T(8,128)} %copy-done.9) | copy-start | bytes 786436
  62.9 6.0 %copy-start.14 = (f32[2,256,128]{2,1,0:T(8,128)S(1)}, f32[2,256,128]{2,1,0:T(8,128)}, u32[]{:S(2)}) copy-start(f32[2,256,128]{2,1,0:T(8,128)} %copy-done.12) | copy-start | bytes 786436
  62.9 6.0 %copy-start.17 = (f32[2,256,128]{2,1,0:T(8,128)S(1)}, f32[2,256,128]{2,1,0:T(8,128)}, u32[]{:S(2)}) copy-start(f32[2,256,128]{2,1,0:T(8,128)} %copy-done.16) | copy-start | bytes 786436
  65.5 5.3 %collective-permute-start.3 = (f32[2,8,128]{2,1,0:T(8,128)S(1)}, f32[2,8,128]{2,1,0:T(8,128)S(1)}, u32[]{:S(2)}, u32[]{:S(2)}) collective-permute-start(f32[2,8,128]{2,1,0:T(8,128)S(1)} %get-tuple-element.39), channel_id=1, source_target_pairs={{0,16},{1,17},{2,18},{3,19},{4,20},{5,21},{6,22},{7,23},{8,24},{9,... | collective-permute-start | bytes 24584 | tf_op jit(solution)/shard_map/ppermute | solution.py:49
  70.7 13.4 %copy-start.3 = (f32[2,256,128]{2,1,0:T(8,128)}, f32[2,256,128]{2,1,0:T(8,128)S(1)}, u32[]{:S(2)}) copy-start(f32[2,256,128]{2,1,0:T(8,128)S(1)} %get-tuple-element.53.old) | copy-start | bytes 786436
  70.8 13.4 %copy-start.6 = (f32[2,256,128]{2,1,0:T(8,128)}, f32[2,256,128]{2,1,0:T(8,128)S(1)}, u32[]{:S(2)}) copy-start(f32[2,256,128]{2,1,0:T(8,128)S(1)} %get-tuple-element.54.fines) | copy-start | bytes 786436
  85.4 13.0 %all-to-all-start.4 = ((f32[16,8,128]{2,1,0:T(8,128)}), f32[16,8,128]{2,1,0:T(8,128)}, u32[]{:S(2)}, u32[]{:S(2)}) async-start(f32[16,8,128]{2,1,0:T(8,128)} %copy-done.22), calls=%async_computation.4 | async-start | bytes 131072 | tf_op jit(solution)/shard_map/all_to_all | solution.py:63
  92.5 11.4 %collective-permute-start.6 = (f32[256,128]{1,0:T(8,128)}, f32[256,128]{1,0:T(8,128)}, u32[]{:S(2)}, u32[]{:S(2)}) collective-permute-start(f32[256,128]{1,0:T(8,128)} %chain.3), channel_id=1, source_target_pairs={{0,16},{1,17},{2,18},{3,19},{4,20},{5,21},{6,22},{7,23},{8,24},{9,... | collective-permute-start | bytes 393224 | tf_op jit(solution)/shard_map/ppermute | solution.py:49
  98.3 5.6 %copy-start.8 = (f32[2,256,128]{2,1,0:T(8,128)S(1)}, f32[2,256,128]{2,1,0:T(8,128)}, u32[]{:S(2)}) copy-start(f32[2,256,128]{2,1,0:T(8,128)} %copy-done.6) | copy-start | bytes 786436
  102.2 3.1 %collective-permute-start.5 = (f32[2,8,128]{2,1,0:T(8,128)S(1)}, f32[2,8,128]{2,1,0:T(8,128)S(1)}, u32[]{:S(2)}, u32[]{:S(2)}) collective-permute-start(f32[2,8,128]{2,1,0:T(8,128)S(1)} %get-tuple-element.51), channel_id=1, source_target_pairs={{0,16},{1,17},{2,18},{3,19},{4,20},{5,21},{6,22},{7,23},{8,24},{9,... | collective-permute-start | bytes 24584 | tf_op jit(solution)/shard_map/ppermute | solution.py:49
  (25 other events, 37.1 us)

commit v3 on v2

--- a/solution.py
+++ b/solution.py
@@ -90,15 +90,33 @@
     return slice((d - 1) * width, d * width)
 
 
-def coarse_kernel(start, received, source, coarse, out):
-    slices, groups, width, _ = coarse.shape
-    per = start.shape[0] // groups
+def spread_counts(row):
+    per = row.shape[1]
+    return jnp.broadcast_to(row.astype(F32), (per, per)).T
+
+
+def lead_kernel(start, source, coarse, counts, sums, source_sums, end):
+    slices, groups, _, _ = coarse.shape
+    per = counts.shape[1]
     for g in range(groups):
         here = group_rows(g, per)
-        u = jnp.where(leading(), start[here], received[here])
+        k = counts[g:g + 1]
+        V = class_sums(start[here], k)
+        sums[g] = V
         for l in range(slices):
-            u = mul(u + source[l, here], stacked(coarse[l, g]))
-        out[here] = u
+            S = class_sums(source[l, here], k)
+            source_sums[l, g] = S
+            V = mul(V + S, stacked(coarse[l, g]))
+        end[g] = V
+
+
+def relay_kernel(start, received, source_sums, coarse, end):
+    slices, groups, _, _ = coarse.shape
+    for g in range(groups):
+        V = jnp.where(leading(), start[g], received[g])
+        for l in range(slices):
+            V = mul(V + source_sums[l, g], stacked(coarse[l, g]))
+        end[g] = V
 
 
 def setup_kernel(everyone, fine, rate, counts, own, other, powers, spread, active):
@@ -110,7 +128,7 @@
     alive = []
     for g in range(groups):
         k = counts[g:g + 1].astype(F32)
-        spread[group_rows(g, per)] = jnp.broadcast_to(k, (per, per)).T
+        spread[group_rows(g, per)] = spread_counts(k)
         rows = [
             jnp.sum((k >= q).astype(F32), axis=1, keepdims=True)
             for q in range(FINE_MIN, FINE_MAX + 1)
@@ -137,6 +155,7 @@
             powers[l, g, :, block(2, width)] = st2
             powers[l, g, :, block(3, width)] = stacked(w3)
             powers[l, g, :, block(4, width)] = st4
+            powers[l, g, :, block(FINE_MAX + 1, width)] = stacked((w1 + w2) + (w3 + w4))
             for i in range(4):
                 powers[l, g, :, block(5 + i, width)] = stacked(w58[i * width:(i + 1) * width])
             sums = [t + w for t, w in zip(sums, (w1, w2, w3, w4))]
@@ -200,91 +219,72 @@
     return out
 
 
-def fine_of_state(v, keep, powers, k, width):
-    return by_count(mul(v * keep, powers), k, FINE_MIN, width)
-
-
-def start_kernel(everyone, initial, received, source, coarse, powers, rate, counts, spread,
-                 base, ofsource, starts, fines, sourced):
+def base_kernel(everyone, sums, received, source_sums, coarse, powers, rate, base, ofsource):
     slices, groups, width, _ = coarse.shape
-    per = counts.shape[1]
     keep = 1.0 - rate[...]
-    states = [
-        jnp.where(leading(), initial[group_rows(g, per)], received[group_rows(g, per)])
-        for g in range(groups)
-    ]
+    states = [jnp.where(leading(), sums[g], received[g]) for g in range(groups)]
     for l in range(slices):
         rows, rows_source = 0.0, 0.0
         for g in range(groups):
-            here = group_rows(g, per)
-            k = counts[g:g + 1]
-            u, s, w = states[g], source[l, here], powers[l, g]
-            starts[l, here] = u
-            rows = rows + sums_of_state(class_sums(u, k), keep, w, width)
-            rows_source = rows_source + sums_of_source(class_sums(s, k), w, width)
+            V, S, w = states[g], source_sums[l, g], powers[l, g, :, :FINE_MAX * width]
+            rows = rows + sums_of_state(V, keep, w, width)
+            rows_source = rows_source + sums_of_source(S, w, width)
             if l + 1 < slices:
-                states[g] = mul(u + s, stacked(coarse[l, g]))
+                states[g] = mul(V + S, stacked(coarse[l, g]))
         rows_source = rows_source / everyone
         at = slice(l * ROWS, (l + 1) * ROWS)
         ofsource[at] = rows_source
         base[at] = rows / everyone + rows_source
-    for l in range(slices):
-        for g in range(groups):
-            here = group_rows(g, per)
-            n = spread[here]
-            w = powers[l, g]
-            x = mul(source[l, here], w)
-            total = x[:, block(1, width)]
-            for d in range(2, FINE_MIN + 1):
-                total = total + x[:, block(d, width)]
-            out = jnp.where(n == float(FINE_MIN), total, 0.0)
-            for d in range(FINE_MIN + 1, FINE_MAX + 1):
-                total = total + x[:, block(d, width)]
-                out = jnp.where(n == float(d), total, out)
-            sourced[l, here] = out
-            v = starts[l, here]
-            w = powers[l, g, :, (FINE_MIN - 1) * width:]
-            fines[l, here] = out + fine_of_state(v, keep, w, n, width)
-
-
-def chain_kernel(start, received, old, fines, coarse, out):
-    slices, groups, _, _ = coarse.shape
-    per = start.shape[0] // groups
-    for g in range(groups):
-        here = group_rows(g, per)
-        u = jnp.where(leading(), start[here], received[here])
-        for l in range(slices):
-            u = fines[l, here] + mul(u - old[l, here], stacked(coarse[l, g]))
-        out[here] = u
-
-
-def again_kernel(start, received, old, fines, sourced, coarse, powers, rate, counts, spread,
-                 starts, fines_out, sums):
+
+
+def sweep_kernel(first, last, *refs):
+    if first:
+        initial, source, coarse, powers, rate, spread, *outs = refs
+    else:
+        initial, received, source, coarse, powers, rate, spread, *outs = refs
     slices, groups, width, _ = coarse.shape
-    per = counts.shape[1]
+    per = spread.shape[0] // groups
     keep = 1.0 - rate[...]
     for g in range(groups):
         here = group_rows(g, per)
         n = spread[here]
-        u = jnp.where(leading(), start[here], received[here])
+        start = initial[here]
+        states = [start] * 3
+        if not first:
+            states = [jnp.where(leading(), start, received[i, here]) for i in range(3)]
         for l in range(slices):
-            starts[l, here] = u
-            sums[l, g] = class_sums(u, counts[g:g + 1])
-            w = powers[l, g, :, (FINE_MIN - 1) * width:]
-            fines_out[l, here] = sourced[l, here] + fine_of_state(u, keep, w, n, width)
-            if l + 1 < slices:
-                u = fines[l, here] + mul(u - old[l, here], stacked(coarse[l, g]))
-
-
-def ends_kernel(start, received, old, fines, coarse, out):
-    slices, groups, _, _ = coarse.shape
-    per = start.shape[0] // groups
-    for g in range(groups):
-        here = group_rows(g, per)
-        u = jnp.where(leading(), start[here], received[here])
-        for l in range(slices):
-            u = fines[l, here] + mul(u - old[l, here], stacked(coarse[l, g]))
-            out[l, here] = u
+            s = source[l, here]
+            if last is not None:
+                outs[0][l, g] = class_sums(states[1], last[g:g + 1])
+            w = powers[l, g, :, FINE_MIN * width:]
+            x = mul(s, w)
+            total = x[:, FINE_MIN * width:]
+            sourced = jnp.where(n == float(FINE_MIN), total, 0.0)
+            for i in range(CLASSES - 1):
+                total = total + x[:, i * width:(i + 1) * width]
+                sourced = jnp.where(n == float(FINE_MIN + 1 + i), total, sourced)
+            both = jnp.concatenate(states[:2], axis=0) * keep
+            x = mul(both, powers[l, g, :, (FINE_MIN - 1) * width:FINE_MAX * width])
+            moved = mul(
+                jnp.concatenate(
+                    [states[0] + s, states[1] - states[0], states[2] - states[1]], axis=0
+                ),
+                stacked(coarse[l, g]),
+            )
+            states = [
+                moved[:per],
+                sourced + by_count(x[:per], n, FINE_MIN, width) + moved[per:2 * per],
+                sourced + by_count(x[per:], n, FINE_MIN, width) + moved[2 * per:],
+            ]
+            if last is not None:
+                outs[1][l, here] = states[2]
+        if last is None:
+            for i in range(3):
+                outs[0][i, here] = states[i]
+
+
+def last_sweep_kernel(initial, received, source, coarse, powers, rate, counts, spread, *outs):
+    sweep_kernel(False, counts, initial, received, source, coarse, powers, rate, spread, *outs)
 
 
 def gather_kernel(parts, base, out):
@@ -333,7 +333,7 @@
     groups = powers.shape[1]
     rows = [0.0] * 3
     for g in range(groups):
-        h = folded(a, rate, powers[l, g], width)
+        h = folded(a, rate, powers[l, g, :, :FINE_MAX * width], width)
         total = per * h[4:5]
         for i in range(1, 4):
             total = total + active[g, i:i + 1] * (h[4 + i:5 + i] - h[3 + i:4 + i])
@@ -356,7 +356,7 @@
 def mixing_kernel(everyone, per, mine, theirs, base, powers, rate, active,
                   mixing, averages, out, held):
     slices, _, _, wider = powers.shape
-    width = wider // FINE_MAX
+    width = wider // (FINE_MAX + 1)
     half = slices // 2
     n, rows, _ = mine.shape
     rows -= slices * ROWS
@@ -379,7 +379,7 @@
 
 def first_kernel(everyone, per, received, base, mixing, powers, rate, active, averages, out):
     slices, _, _, wider = powers.shape
-    width = wider // FINE_MAX
+    width = wider // (FINE_MAX + 1)
     total = received[0]
     for p in range(1, received.shape[0]):
         total = total + received[p]
@@ -397,7 +397,7 @@
     else:
         plain, starts, pushes, end = refs
     slices, groups, _, wider = powers.shape
-    width = wider // FINE_MAX
+    width = wider // (FINE_MAX + 1)
     r = rate[...]
     total = received[0]
     for p in range(1, received.shape[0]):
@@ -413,7 +413,7 @@
         for m, row in ((5, a5), (6, a6), (7, a7)):
             a = jnp.where(row_is(m, a.shape), row, a)
         for g in range(groups):
-            h = folded(a, r, powers[l, g], width)[FINE_MIN:FINE_MIN + ROWS]
+            h = folded(a, r, powers[l, g, :, :FINE_MAX * width], width)[FINE_MIN:FINE_MIN + ROWS]
             if plain is not None:
                 h = h + plain[l, g]
             pushes[l, g] = h
@@ -451,7 +451,7 @@
             for i in reversed(range(CLASSES)):
                 tail = tail + weighted[i:i + 1]
                 V = jnp.where(row_is(i, V.shape), V + tail, V)
-            rows = rows + sums_of_state(V, keep, powers[l, g], width)
+            rows = rows + sums_of_state(V, keep, powers[l, g, :, :FINE_MAX * width], width)
             if l + 1 < slices:
                 x[g] = pushes[l, g] + mul(x[g], stacked(coarse[l, g]))
         at = slice(l * ROWS, (l + 1) * ROWS)
@@ -465,19 +465,19 @@
 
 def plain_kernel(starts, powers, rate, out):
     slices, groups, _, wider = powers.shape
-    width = wider // FINE_MAX
+    width = wider // (FINE_MAX + 1)
     keep = 1.0 - rate[...]
     for l in range(slices):
         for g in range(groups):
-            out[l, g] = picked(mul(starts[l, g] * keep, powers[l, g]), FINE_MIN, width)
-
-
-def finish_kernel(received, pushes, starts, coarse, ends, spread, out):
+            out[l, g] = picked(mul(starts[l, g] * keep, powers[l, g, :, :FINE_MAX * width]), FINE_MIN, width)
+
+
+def finish_kernel(received, pushes, starts, coarse, ends, counts, out):
     slices, groups, width, _ = coarse.shape
-    per = spread.shape[0] // groups
+    per = counts.shape[1]
     for g in range(groups):
         here = group_rows(g, per)
-        n = spread[here]
+        n = spread_counts(counts[g:g + 1])
         x = jnp.where(leading(), 0.0, received[g])
         for l in range(slices):
             x = pushes[l, g] + mul(x - starts[l, g], stacked(coarse[l, g]))
@@ -507,39 +507,48 @@
     rows4 = shape(n_cell, slices * 4, width)
     averages = shape(slices, ROWS, width)
 
-    def handed(first, advance):
-        received = first
-        for _ in range(turns):
-            received = from_behind(advance(received), "tm", 1)
-        return received
-
-    received = handed(
-        initial, lambda u: call(coarse_kernel, "coarse", [state], (initial, u, source, coarse))[0]
-    )
     mats = shape(half * MATS * width, width)
     own, other, powers, spread, active = call(
         functools.partial(setup_kernel, everyone), "setup",
-        [mats, mats, shape(slices, groups, 2 * width, FINE_MAX * width, dtype=BF16), state, vector],
+        [
+            mats, mats,
+            shape(slices, groups, 2 * width, (FINE_MAX + 1) * width, dtype=BF16),
+            state, vector,
+        ],
         (fine, rate, counts),
     )
+    sums0, source_sums, moved = call(
+        lead_kernel, "lead", [vector, vectors, vector], (initial, source, coarse, counts)
+    )
+    for turn in range(turns):
+        moved = from_behind(moved, "tm", 1)
+        if turn + 1 < turns:
+            moved, = call(relay_kernel, "relay", [vector], (sums0, moved, source_sums, coarse))
     mine = (own + swap_core(other)).reshape(peers, shard, width)
     parts = exchange(mine, same_core())
-    base, ofsource, starts0, fines1, sourced = call(
-        functools.partial(start_kernel, everyone), "start",
-        [rows8, rows8, states, states, states],
-        (initial, received, source, coarse, powers, rate, counts, spread),
-    )
+    base, ofsource = call(
+        functools.partial(base_kernel, everyone), "base", [rows8, rows8],
+        (sums0, moved, source_sums, coarse, powers, rate),
+    )
+    bundle = shape(3, cells, width)
+    sent, = call(
+        functools.partial(sweep_kernel, True, None), "sweep", [bundle],
+        (initial, source, coarse, powers, rate, spread),
+    )
+    for turn in range(turns):
+        sent = from_behind(sent, "tm", 1)
+        if turn + 1 < turns:
+            sent, = call(
+                functools.partial(sweep_kernel, False, None), "sweep", [bundle],
+                (initial, sent, source, coarse, powers, rate, spread),
+            )
     payload, = call(
         gather_kernel, "gather", [shape(peers, shard + slices * ROWS, width)], (parts, base)
     )
     gathered = exchange(payload, same_core())
-    received = handed(
-        initial,
-        lambda u: call(chain_kernel, "chain", [state], (initial, u, starts0, fines1, coarse))[0],
-    )
-    starts1, fines2, sums = call(
-        again_kernel, "again", [states, states, vectors],
-        (initial, received, starts0, fines1, sourced, coarse, powers, rate, counts, spread),
+    sums, ends = call(
+        last_sweep_kernel, "sweep", [vectors, states],
+        (initial, sent, source, coarse, powers, rate, counts, spread),
     )
     theirs = swap_core(gathered)
     mixing, first, out = call(
@@ -565,13 +574,6 @@
     )
     got = exchange(out)
     plain, = call(plain_kernel, "plain", [vectors], (moved1, powers, rate))
-    received = handed(
-        initial,
-        lambda u: call(chain_kernel, "chain", [state], (initial, u, starts1, fines2, coarse))[0],
-    )
-    ends, = call(
-        ends_kernel, "ends", [states], (initial, received, starts1, fines2, coarse)
-    )
     first, out = call(
         functools.partial(first_kernel, everyone, per), "first", [averages, rows4],
         (got, base, mixing, powers, rate, active),
@@ -586,7 +588,7 @@
         if turn + 1 < turns:
             moved, = call(vectors_kernel, "vectors", [vector], (moved, pushes2, moved1, coarse))
     out, = call(
-        finish_kernel, "finish", [states], (moved, pushes2, moved1, coarse, ends, spread)
+        finish_kernel, "finish", [states], (moved, pushes2, moved1, coarse, ends, counts)
     )
     return out
 

time: 107 us -> 105 us (0.981)
  blocking collectives: 29.7 us -> 39.2 us
  starting transfers between devices: 32.8 us -> 23.4 us
  waiting for transfers between devices: 8.28 us -> 16.1 us
  local copies, waits for them, and re-layouts: 15.5 us -> 9.22 us
  Pallas kernels: 18.7 us -> 15 us
    all_to_all x3 -> x2, waiting for transfers between devices: 2.16 us -> 12 us  [exchange(): return lax.all_to_all(block, 'cell', 0, 0, axis_index_groups=groups)]
    all_to_all x2 -> x3, blocking collectives: 29.7 us -> 39.2 us  [exchange(): return lax.all_to_all(block, 'cell', 0, 0, axis_index_groups=groups)]
    unnamed x78 -> x60, local copies, waits for them, and re-layouts: 15.5 us -> 9.22 us
    ppermute x5 -> x4, starting transfers between devices: 16.8 us -> 11.5 us  [from_behind(): return lax.ppermute(block, axis, route)]
    all_to_all x3 -> x2, starting transfers between devices: 15.5 us -> 11.3 us  [exchange(): return lax.all_to_all(block, 'cell', 0, 0, axis_index_groups=groups)]
    pallas_call x15 -> x13, Pallas kernels: 18.7 us -> 15 us  [call(): pl.pallas_call(kernel, out_shape=outs, in_specs=[pl.BlockSpec(memory_spac...]
    ppermute x2, waiting for transfers between devices: 3.35 us -> 1.45 us  [swap_core(): return lax.ppermute(block, 'cell', [(i, i ^ 1) for i in range(n)])]
    ppermute x5 -> x4, waiting for transfers between devices: 2.76 us -> 2.7 us  [from_behind(): return lax.ppermute(block, axis, route)]
  transfers between devices with their start and end apart: 10 -> 8, of which waited for: 4 -> 5; matrix products, arithmetic and copies ran while one was open for 0% -> 0% of each run, Pallas kernels for 11% -> 8%
where the time goes in v3:
time: 105 us; the launch traced here: 104 us
  blocking collectives  39.2 us (37%)
  starting transfers between devices  23.4 us (22%)
  waiting for transfers between devices  16.1 us (15%)
  Pallas kernels  15 us (14%)
  local copies, waits for them, and re-layouts  9.22 us (9%)
    all_to_all x3, blocking collectives, exchange(): return lax.all_to_all(block, 'cell', 0, 0, axis_index_groups=groups)  39.2 us
    pallas_call x13, Pallas kernels, call(): pl.pallas_call(kernel, out_shape=outs, in_specs=[pl.BlockSpec(memory_spac...  15 us
    all_to_all x2, waiting for transfers between devices, exchange(): return lax.all_to_all(block, 'cell', 0, 0, axis_index_groups=groups)  12 us
    ppermute x4, starting transfers between devices, from_behind(): return lax.ppermute(block, axis, route)  11.5 us
    all_to_all x2, starting transfers between devices, exchange(): return lax.all_to_all(block, 'cell', 0, 0, axis_index_groups=groups)  11.3 us
    unnamed x60, local copies, waits for them, and re-layouts  9.22 us
    ppermute x4, waiting for transfers between devices, from_behind(): return lax.ppermute(block, axis, route)  2.7 us
  transfers between devices with their start and end apart: 8, of which 5 were waited for; matrix products, arithmetic and copies ran while one was open for 0% of the time, Pallas kernels for 8%

profile of v3, /device:TPU:0, one launch (start us, length us, event | category | flops | bytes accessed | tf_op | source)
XLA Modules:
  0.0 104.1 jit_solution(4942942167078619842)
XLA Ops:
  0.0 1.0 copy-done.8
  2.4 2.6 %setup.1 = (f32[896,128]{1,0:T(8,128)S(1)}, f32[896,128]{1,0:T(8,128)S(1)}, bf16[2,2,256,1152]{3,2,1,0:T(8,128)(2,1)S(1)}, f32[256,128]{1,0:T(8,128)S(1)}, f32[2,8,128]{2,1,0:T(8,128)S(1)}) custom-call(f32[2,2,128,128]{3,2,1,0:T(8,128)S(1)} %copy-done.8, f32[1,128]{1,0:T(1,128)S(1)} %bitcast.3, s32[2,128]{1,0:T(2,128)S(1)} %bitcast.13), custom_call_target="tpu_custom_call" | custom-call | bytes 3679744 | tf_op jit(solution)/shard_map/setup/pallas_call | solution.py:69
  5.5 1.4 %collective-permute-done = f32[896,128]{1,0:T(8,128)S(1)} collective-permute-done((f32[896,128]{1,0:T(8,128)S(1)}, f32[896,128]{1,0:T(8,128)S(1)}, u32[]{:S(2)}, u32[]{:S(2)}) %collective-permute-start) | collective-permute-done | bytes 458784 | tf_op jit(solution)/shard_map/ppermute | solution.py:54
  7.8 7.2 %all-to-all-start = ((f32[8,112,128]{2,1,0:T(8,128)}), f32[8,112,128]{2,1,0:T(8,128)S(1)}, u32[]{:S(2)}, u32[]{:S(2)}) async-start(f32[8,112,128]{2,1,0:T(8,128)} %bitcast.17), calls=%async_computation | async-start | bytes 917504 | tf_op jit(solution)/shard_map/all_to_all | solution.py:63
  15.7 3.4 %collective-permute-start.1 = (f32[2,8,128]{2,1,0:T(8,128)S(1)}, f32[2,8,128]{2,1,0:T(8,128)S(1)}, u32[]{:S(2)}, u32[]{:S(2)}) collective-permute-start(f32[2,8,128]{2,1,0:T(8,128)S(1)} %get-tuple-element.32), channel_id=1, source_target_pairs={{0,16},{1,17},{2,18},{3,19},{4,20},{5,21},{6,22},{7,23},{8,24},{9,... | collective-permute-start | bytes 24584 | tf_op jit(solution)/shard_map/ppermute | solution.py:49
  19.1 1.3 %collective-permute-done.1.received = f32[2,8,128]{2,1,0:T(8,128)S(1)} collective-permute-done((f32[2,8,128]{2,1,0:T(8,128)S(1)}, f32[2,8,128]{2,1,0:T(8,128)S(1)}, u32[]{:S(2)}, u32[]{:S(2)}) %collective-permute-start.1) | collective-permute-done | bytes 8224 | tf_op jit(solution)/shard_map/ppermute | solution.py:49
  21.7 6.7 %all-to-all-done.parts = f32[8,112,128]{2,1,0:T(8,128)S(1)} async-done(((f32[8,112,128]{2,1,0:T(8,128)}), f32[8,112,128]{2,1,0:T(8,128)S(1)}, u32[]{:S(2)}, u32[]{:S(2)}) %all-to-all-start) | async-done | bytes 458784 | tf_op jit(solution)/shard_map/all_to_all | solution.py:63
  28.4 18.1 %all_to_all.25.mine = f32[8,128,128]{2,1,0:T(8,128)S(1)} all-to-all(f32[8,128,128]{2,1,0:T(8,128)S(1)} %gather.1), channel_id=1, replica_groups={{0,2,4,6,8,10,12,14},{1,3,5,7,9,11,13,15},{16,18,20,22,24,26,28,30},{17..., dimensions={0} | all-to-all | bytes 1048576 | tf_op jit(solution)/shard_map/all_to_all | solution.py:63
  46.5 0.9 copy-done.6
  47.4 1.8 %sweep.2 = f32[3,256,128]{2,1,0:T(8,128)S(1)} custom-call(f32[256,128]{1,0:T(8,128)S(1)} %copy-done.3, f32[2,256,128]{2,1,0:T(8,128)S(1)} %copy-done.1, f32[2,2,128,128]{3,2,1,0:T(8,128)S(1)} %copy-done, bf16[2,2,256,1152]{3,2,1,0:T(8,128)(2,1)S(1)} %get-tuple-element.34.powers.refs_3_, f32[1,128]{1,0:T(1,128)S(1)} %bitcast.5, f32[256,128]{1,0:T(8,128)S(1)} %copy-done.6), custom_call_target="tpu_custom_call" | custom-call | bytes 3539456 | tf_op jit(solution)/shard_map/sweep/pallas_call | solution.py:69
  49.3 3.4 %collective-permute-start.4 = (f32[3,256,128]{2,1,0:T(8,128)S(1)}, f32[3,256,128]{2,1,0:T(8,128)S(1)}, u32[]{:S(2)}, u32[]{:S(2)}) collective-permute-start(f32[3,256,128]{2,1,0:T(8,128)S(1)} %sweep.2), channel_id=1, source_target_pairs={{0,16},{1,17},{2,18},{3,19},{4,20},{5,21},{6,22},{7,23},{8,24},{9,... | collective-permute-start | bytes 1179656 | tf_op jit(solution)/shard_map/ppermute | solution.py:49
  53.4 1.3 %mixing.1 = (bf16[2,256,896]{2,1,0:T(8,128)(2,1)S(1)}, f32[2,8,128]{2,1,0:T(8,128)S(1)}, f32[16,8,128]{2,1,0:T(8,128)S(1)}) custom-call(f32[8,128,128]{2,1,0:T(8,128)S(1)} %all_to_all.25.mine, f32[8,128,128]{2,1,0:T(8,128)S(1)} %collective-permute-done.2.theirs, f32[16,128]{1,0:T(8,128)S(1)} %copy-done.22, ...), custom_call_target="tpu_custom_call" | custom-call | bytes 4416000 | tf_op jit(solution)/shard_map/mixing/pallas_call | solution.py:69
  54.8 10.6 %all_to_all.26.received = f32[16,8,128]{2,1,0:T(8,128)S(1)} all-to-all(f32[16,8,128]{2,1,0:T(8,128)S(1)} %get-tuple-element.37), channel_id=1, replica_groups=mesh['tm'=2,'cell'=16] {'cell'}, dimensions={0} | all-to-all | bytes 131072 | tf_op jit(solution)/shard_map/all_to_all | solution.py:63
  65.4 0.9 push.2
  66.3 1.5 %collective-permute-start.3 = (f32[2,8,128]{2,1,0:T(8,128)S(1)}, f32[2,8,128]{2,1,0:T(8,128)S(1)}, u32[]{:S(2)}, u32[]{:S(2)}) collective-permute-start(f32[2,8,128]{2,1,0:T(8,128)S(1)} %get-tuple-element.40), channel_id=1, source_target_pairs={{0,16},{1,17},{2,18},{3,19},{4,20},{5,21},{6,22},{7,23},{8,24},{9,... | collective-permute-start | bytes 24584 | tf_op jit(solution)/shard_map/ppermute | solution.py:49
  67.9 2.3 %sweep.3 = (f32[2,2,8,128]{3,2,1,0:T(8,128)S(1)}, f32[2,256,128]{2,1,0:T(8,128)S(1)}) custom-call(f32[256,128]{1,0:T(8,128)S(1)} %copy-done.4, f32[3,256,128]{2,1,0:T(8,128)S(1)} %collective-permute-done.4.received, f32[2,256,128]{2,1,0:T(8,128)S(1)} %copy-done.2, f32[2,2,128,128]{3,2,1,0:T(8,128)S(1)} %copy-done, ...), custom_call_target="tpu_custom_call" | custom-call | bytes 3819008 | tf_op jit(solution)/shard_map/sweep/pallas_call | solution.py:69
  70.7 10.5 %all_to_all.27.received = f32[16,10,128]{2,1,0:T(8,128)S(1)} all-to-all(f32[16,10,128]{2,1,0:T(8,128)S(1)} %get-tuple-element.45), channel_id=1, replica_groups=mesh['tm'=2,'cell'=16] {'cell'}, dimensions={0} | all-to-all | bytes 163840 | tf_op jit(solution)/shard_map/all_to_all | solution.py:63
  81.2 1.2 %first.1 = (f32[2,8,128]{2,1,0:T(8,128)S(1)}, f32[16,8,128]{2,1,0:T(8,128)S(1)}) custom-call(f32[16,10,128]{2,1,0:T(8,128)S(1)} %all_to_all.27.received, f32[16,128]{1,0:T(8,128)S(1)} %get-tuple-element.46.base, bf16[2,256,896]{2,1,0:T(8,128)(2,1)S(1)} %get-tuple-element.39.mixing, bf16[2,2,256,1152]{3,2,1,0:T(8,128)(2,1)S(1)} %get-tuple-element.34.powers.refs_3_, ...), custom_call_target="tpu_custom_call" | custom-call | bytes 3449344 | tf_op jit(solution)/shard_map/first/pallas_call | solution.py:69
  83.6 4.1 %all-to-all-start.4 = ((f32[16,8,128]{2,1,0:T(8,128)}), f32[16,8,128]{2,1,0:T(8,128)}, u32[]{:S(2)}, u32[]{:S(2)}) async-start(f32[16,8,128]{2,1,0:T(8,128)} %copy-done.15), calls=%async_computation.4 | async-start | bytes 131072 | tf_op jit(solution)/shard_map/all_to_all | solution.py:63
  89.3 5.3 %all-to-all-done.4.received = f32[16,8,128]{2,1,0:T(8,128)} async-done(((f32[16,8,128]{2,1,0:T(8,128)}), f32[16,8,128]{2,1,0:T(8,128)}, u32[]{:S(2)}, u32[]{:S(2)}) %all-to-all-start.4) | async-done | bytes 65568 | tf_op jit(solution)/shard_map/all_to_all | solution.py:63
  96.8 1.8 %push.3 = (f32[2,2,8,128]{3,2,1,0:T(8,128)S(1)}, f32[2,8,128]{2,1,0:T(8,128)S(1)}) custom-call(f32[16,8,128]{2,1,0:T(8,128)} %all-to-all-done.4.received, f32[2,8,128]{2,1,0:T(8,128)S(1)} %copy-done.29, bf16[2,256,896]{2,1,0:T(8,128)(2,1)S(1)} %get-tuple-element.39.mixing, bf16[2,2,256,1152]{3,2,1,0:T(8,128)(2,1)S(1)} %get-tuple-element.34.powers.refs_3_, ...), custom_call_target="tpu_custom_call" | custom-call | bytes 3670528 | tf_op jit(solution)/shard_map/push/pallas_call | solution.py:69
  98.5 3.2 %collective-permute-start.5 = (f32[2,8,128]{2,1,0:T(8,128)S(1)}, f32[2,8,128]{2,1,0:T(8,128)S(1)}, u32[]{:S(2)}, u32[]{:S(2)}) collective-permute-start(f32[2,8,128]{2,1,0:T(8,128)S(1)} %get-tuple-element.50), channel_id=1, source_target_pairs={{0,16},{1,17},{2,18},{3,19},{4,20},{5,21},{6,22},{7,23},{8,24},{9,... | collective-permute-start | bytes 24584 | tf_op jit(solution)/shard_map/ppermute | solution.py:49
  101.7 1.3 %collective-permute-done.5.received = f32[2,8,128]{2,1,0:T(8,128)S(1)} collective-permute-done((f32[2,8,128]{2,1,0:T(8,128)S(1)}, f32[2,8,128]{2,1,0:T(8,128)S(1)}, u32[]{:S(2)}, u32[]{:S(2)}) %collective-permute-start.5) | collective-permute-done | bytes 8224 | tf_op jit(solution)/shard_map/ppermute | solution.py:49
  103.1 1.0 finish.1
  (69 shorter events, 10.8 us)
Async XLA Ops:
  0.0 15.0 %copy-start.3 = (f32[256,128]{1,0:T(8,128)S(1)}, f32[256,128]{1,0:T(8,128)}, u32[]{:S(2)}) copy-start(f32[256,128]{1,0:T(8,128)} %initial.1) | copy-start | bytes 393220
  0.0 15.0 %copy-start.1 = (f32[2,256,128]{2,1,0:T(8,128)S(1)}, f32[2,256,128]{2,1,0:T(8,128)}, u32[]{:S(2)}) copy-start(f32[2,256,128]{2,1,0:T(8,128)} %source.3) | copy-start | bytes 786436
  0.0 15.0 %copy-start = (f32[2,2,128,128]{3,2,1,0:T(8,128)S(1)}, f32[2,2,128,128]{3,2,1,0:T(8,128)}, u32[]{:S(2)}) copy-start(f32[2,2,128,128]{3,2,1,0:T(8,128)} %coarse.13) | copy-start | bytes 786436
  2.4 12.7 %copy-start.24 = (s32[256]{0:T(256)S(1)}, s32[256]{0:T(256)}, u32[]{:S(2)}) copy-start(s32[256]{0:T(256)} %param.11) | copy-start | bytes 3076
  2.4 18.1 %copy-start.17 = (f32[128]{0:T(128)S(1)}, f32[128]{0:T(128)}, u32[]{:S(2)}) copy-start(f32[128]{0:T(128)} %param.8) | copy-start | bytes 1540
  5.0 47.7 %copy-start.11 = (f32[2,8,128]{2,1,0:T(8,128)}, f32[2,8,128]{2,1,0:T(8,128)S(1)}, u32[]{:S(2)}) copy-start(f32[2,8,128]{2,1,0:T(8,128)S(1)} %get-tuple-element.36.active) | copy-start | bytes 24580
  5.0 2.0 %collective-permute-start = (f32[896,128]{1,0:T(8,128)S(1)}, f32[896,128]{1,0:T(8,128)S(1)}, u32[]{:S(2)}, u32[]{:S(2)}) collective-permute-start(f32[896,128]{1,0:T(8,128)S(1)} %get-tuple-element.30), channel_id=1, source_target_pairs={{0,1},{1,0},{2,3},{3,2},{4,5},{5,4},{6,7},{7,6},{8,9},{9,8},{10,11... | collective-permute-start | bytes 1376264 | tf_op jit(solution)/shard_map/ppermute | solution.py:54
  7.8 20.6 %all-to-all-start = ((f32[8,112,128]{2,1,0:T(8,128)}), f32[8,112,128]{2,1,0:T(8,128)S(1)}, u32[]{:S(2)}, u32[]{:S(2)}) async-start(f32[8,112,128]{2,1,0:T(8,128)} %bitcast.17), calls=%async_computation | async-start | bytes 917504 | tf_op jit(solution)/shard_map/all_to_all | solution.py:63
  15.7 4.8 %collective-permute-start.1 = (f32[2,8,128]{2,1,0:T(8,128)S(1)}, f32[2,8,128]{2,1,0:T(8,128)S(1)}, u32[]{:S(2)}, u32[]{:S(2)}) collective-permute-start(f32[2,8,128]{2,1,0:T(8,128)S(1)} %get-tuple-element.32), channel_id=1, source_target_pairs={{0,16},{1,17},{2,18},{3,19},{4,20},{5,21},{6,22},{7,23},{8,24},{9,... | collective-permute-start | bytes 24584 | tf_op jit(solution)/shard_map/ppermute | solution.py:49
  21.7 27.5 %copy-start.21 = (f32[16,128]{1,0:T(8,128)}, f32[16,128]{1,0:T(8,128)S(1)}, u32[]{:S(2)}) copy-start(f32[16,128]{1,0:T(8,128)S(1)} %get-tuple-element.35.base) | copy-start | bytes 24580
  46.5 6.2 %collective-permute-start.2 = (f32[8,128,128]{2,1,0:T(8,128)S(1)}, f32[8,128,128]{2,1,0:T(8,128)S(1)}, u32[]{:S(2)}, u32[]{:S(2)}) collective-permute-start(f32[8,128,128]{2,1,0:T(8,128)S(1)} %all_to_all.25.mine), channel_id=1, source_target_pairs={{0,1},{1,0},{2,3},{3,2},{4,5},{5,4},{6,7},{7,6},{8,9},{9,8},{10,11... | collective-permute-start | bytes 1572872 | tf_op jit(solution)/shard_map/ppermute | solution.py:54
  49.3 18.6 %collective-permute-start.4 = (f32[3,256,128]{2,1,0:T(8,128)S(1)}, f32[3,256,128]{2,1,0:T(8,128)S(1)}, u32[]{:S(2)}, u32[]{:S(2)}) collective-permute-start(f32[3,256,128]{2,1,0:T(8,128)S(1)} %sweep.2), channel_id=1, source_target_pairs={{0,16},{1,17},{2,18},{3,19},{4,20},{5,21},{6,22},{7,23},{8,24},{9,... | collective-permute-start | bytes 1179656 | tf_op jit(solution)/shard_map/ppermute | solution.py:49
  54.8 13.1 %copy-start.2 = (f32[2,256,128]{2,1,0:T(8,128)S(1)}, f32[2,256,128]{2,1,0:T(8,128)}, u32[]{:S(2)}) copy-start(f32[2,256,128]{2,1,0:T(8,128)} %source.3) | copy-start | bytes 786436
  54.8 13.1 %copy-start.4 = (f32[256,128]{1,0:T(8,128)S(1)}, f32[256,128]{1,0:T(8,128)}, u32[]{:S(2)}) copy-start(f32[256,128]{1,0:T(8,128)} %initial.1) | copy-start | bytes 393220
  54.8 13.1 %copy-start.7 = (f32[256,128]{1,0:T(8,128)S(1)}, f32[256,128]{1,0:T(8,128)}, u32[]{:S(2)}) copy-start(f32[256,128]{1,0:T(8,128)} %copy-done.5) | copy-start | bytes 393220
  66.3 3.9 %copy-start.12 = (f32[2,8,128]{2,1,0:T(8,128)S(1)}, f32[2,8,128]{2,1,0:T(8,128)}, u32[]{:S(2)}) copy-start(f32[2,8,128]{2,1,0:T(8,128)} %copy-done.11) | copy-start | bytes 24580
  66.3 3.9 %copy-start.18 = (f32[128]{0:T(128)S(1)}, f32[128]{0:T(128)}, u32[]{:S(2)}) copy-start(f32[128]{0:T(128)} %param.8) | copy-start | bytes 1540
  66.3 3.9 %copy-start.27 = (f32[16,128]{1,0:T(8,128)S(1)}, f32[16,128]{1,0:T(8,128)}, u32[]{:S(2)}) copy-start(f32[16,128]{1,0:T(8,128)} %copy-done.26) | copy-start | bytes 24580
  66.3 3.8 %collective-permute-start.3 = (f32[2,8,128]{2,1,0:T(8,128)S(1)}, f32[2,8,128]{2,1,0:T(8,128)S(1)}, u32[]{:S(2)}, u32[]{:S(2)}) collective-permute-start(f32[2,8,128]{2,1,0:T(8,128)S(1)} %get-tuple-element.40), channel_id=1, source_target_pairs={{0,16},{1,17},{2,18},{3,19},{4,20},{5,21},{6,22},{7,23},{8,24},{9,... | collective-permute-start | bytes 24584 | tf_op jit(solution)/shard_map/ppermute | solution.py:49
  70.1 12.2 %copy-start.9 = (f32[2,256,128]{2,1,0:T(8,128)}, f32[2,256,128]{2,1,0:T(8,128)S(1)}, u32[]{:S(2)}) copy-start(f32[2,256,128]{2,1,0:T(8,128)S(1)} %get-tuple-element.52.ends) | copy-start | bytes 786436
  83.6 11.1 %all-to-all-start.4 = ((f32[16,8,128]{2,1,0:T(8,128)}), f32[16,8,128]{2,1,0:T(8,128)}, u32[]{:S(2)}, u32[]{:S(2)}) async-start(f32[16,8,128]{2,1,0:T(8,128)} %copy-done.15), calls=%async_computation.4 | async-start | bytes 131072 | tf_op jit(solution)/shard_map/all_to_all | solution.py:63
  94.7 8.4 %copy-start.10 = (f32[2,256,128]{2,1,0:T(8,128)S(1)}, f32[2,256,128]{2,1,0:T(8,128)}, u32[]{:S(2)}) copy-start(f32[2,256,128]{2,1,0:T(8,128)} %copy-done.9) | copy-start | bytes 786436
  96.8 6.3 %copy-start.25 = (s32[256]{0:T(256)S(1)}, s32[256]{0:T(256)}, u32[]{:S(2)}) copy-start(s32[256]{0:T(256)} %param.11) | copy-start | bytes 3076
  98.5 4.5 %collective-permute-start.5 = (f32[2,8,128]{2,1,0:T(8,128)S(1)}, f32[2,8,128]{2,1,0:T(8,128)S(1)}, u32[]{:S(2)}, u32[]{:S(2)}) collective-permute-start(f32[2,8,128]{2,1,0:T(8,128)S(1)} %get-tuple-element.50), channel_id=1, source_target_pairs={{0,16},{1,17},{2,18},{3,19},{4,20},{5,21},{6,22},{7,23},{8,24},{9,... | collective-permute-start | bytes 24584 | tf_op jit(solution)/shard_map/ppermute | solution.py:49
  (14 other events, 12.0 us)

commit v4 on v3

--- a/solution.py
+++ b/solution.py
@@ -12,6 +12,8 @@
 CLASSES = FINE_MAX - FINE_MIN + 1
 MATS = 7
 ROWS = 8
+COUNT_ROW = slice(6, 7)
+RATE_ROW = slice(7, 8)
 F32 = jnp.float32
 BF16 = jnp.bfloat16
 
@@ -54,22 +56,36 @@
     return lax.ppermute(block, "cell", [(i, i ^ 1) for i in range(n)])
 
 
-def same_core():
+def near_size():
     n = lax.axis_size("cell")
-    return [list(range(c, n, 2)) for c in range(2)]
+    return 4 if n % 8 == 0 else n // 2
+
+
+def near_groups():
+    n, near = lax.axis_size("cell"), near_size()
+    return [
+        [at + core + 2 * i for i in range(near)]
+        for at in range(0, n, 2 * near)
+        for core in range(2)
+    ]
+
+
+def far_swap(block, distance):
+    n = lax.axis_size("cell")
+    return lax.ppermute(block, "cell", [(i, i ^ distance) for i in range(n)])
 
 
 def exchange(block, groups=None):
     return lax.all_to_all(block, "cell", 0, 0, axis_index_groups=groups)
 
 
-def call(kernel, name, outs, args, scratch=(), flops=0):
+def call(kernel, name, outs, args, scratch=(), flops=0, space=pltpu.VMEM):
     size = sum(x.size * x.dtype.itemsize for x in args)
     size += sum(x.size * x.dtype.itemsize for x in outs)
     return pl.pallas_call(
         kernel,
         out_shape=outs,
-        in_specs=[pl.BlockSpec(memory_space=pltpu.VMEM)] * len(args),
+        in_specs=[pl.BlockSpec(memory_space=space)] * len(args),
         out_specs=[pl.BlockSpec(memory_space=pltpu.VMEM)] * len(outs),
         scratch_shapes=list(scratch),
         compiler_params=pltpu.CompilerParams(vmem_limit_bytes=24 << 20),
@@ -95,21 +111,6 @@
     return jnp.broadcast_to(row.astype(F32), (per, per)).T
 
 
-def lead_kernel(start, source, coarse, counts, sums, source_sums, end):
-    slices, groups, _, _ = coarse.shape
-    per = counts.shape[1]
-    for g in range(groups):
-        here = group_rows(g, per)
-        k = counts[g:g + 1]
-        V = class_sums(start[here], k)
-        sums[g] = V
-        for l in range(slices):
-            S = class_sums(source[l, here], k)
-            source_sums[l, g] = S
-            V = mul(V + S, stacked(coarse[l, g]))
-        end[g] = V
-
-
 def relay_kernel(start, received, source_sums, coarse, end):
     slices, groups, _, _ = coarse.shape
     for g in range(groups):
@@ -119,12 +120,21 @@
         end[g] = V
 
 
-def setup_kernel(everyone, fine, rate, counts, own, other, powers, spread, active):
+def setup_kernel(everyone, *refs):
+    outside, refs = refs[:6], refs[6:]
+    own, other, powers, spread, table, start_sums, source_sums, end = refs[:8]
+    held, arrived = refs[8:14], refs[14]
+    loads = [pltpu.make_async_copy(x, y, arrived.at[i]) for i, (x, y) in enumerate(zip(outside, held))]
+    for load in loads:
+        load.start()
+    fine, rate, counts, initial, source, coarse = held
     slices, groups, width, _ = fine.shape
     per = counts.shape[1]
     half = slices // 2
+    core = lax.rem(lax.axis_index("cell"), 2)
+    for load in loads[:3]:
+        load.wait()
     keep = 1.0 - rate[...]
-    core = lax.rem(lax.axis_index("cell"), 2)
     alive = []
     for g in range(groups):
         k = counts[g:g + 1].astype(F32)
@@ -135,9 +145,10 @@
         ]
         alive.append(rows)
         filled = jnp.zeros((ROWS, width), F32)
-        for i, n in enumerate(rows):
-            filled = jnp.where(row_is(i, filled.shape), n, filled)
-        active[g] = filled
+        for i, n in enumerate(rows + [None, k, rate[...]]):
+            if n is not None:
+                filled = jnp.where(row_is(i, filled.shape), n, filled)
+        table[g] = filled
     for l in range(slices):
         sums = [0.0] * 4
         e6, e7, e72 = 0.0, 0.0, 0.0
@@ -174,11 +185,27 @@
             @pl.when(core != l // half)
             def _():
                 other[at] = m
+    for load in loads[3:]:
+        load.wait()
+    for g in range(groups):
+        here = group_rows(g, per)
+        k = table[g, COUNT_ROW]
+        V = class_sums(initial[here], k)
+        start_sums[g] = V
+        for l in range(slices):
+            S = class_sums(source[l, here], k)
+            source_sums[l, g] = S
+            V = mul(V + S, stacked(coarse[l, g]))
+        end[g] = V
+
+
+def add_kernel(a, b, out):
+    out[...] = a[...] + b[...]
 
 
 def class_sums(state, k):
-    mask = k >= (FINE_MIN + lax.broadcasted_iota(jnp.int32, (ROWS, k.shape[1]), 0))
-    mask = mask.astype(F32)
+    least = (FINE_MIN + lax.broadcasted_iota(jnp.int32, (ROWS, k.shape[1]), 0)).astype(F32)
+    mask = (k >= least).astype(F32)
     left = jnp.concatenate([mask, mask], axis=1)
     left = jnp.concatenate([left, jnp.zeros_like(left)], axis=0).astype(BF16)
     return jnp.dot(left, stacked(state), preferred_element_type=F32)[:ROWS]
@@ -219,9 +246,9 @@
     return out
 
 
-def base_kernel(everyone, sums, received, source_sums, coarse, powers, rate, base, ofsource):
+def base_kernel(everyone, sums, received, source_sums, coarse, powers, table, base, ofsource):
     slices, groups, width, _ = coarse.shape
-    keep = 1.0 - rate[...]
+    keep = 1.0 - table[0, RATE_ROW]
     states = [jnp.where(leading(), sums[g], received[g]) for g in range(groups)]
     for l in range(slices):
         rows, rows_source = 0.0, 0.0
@@ -239,12 +266,12 @@
 
 def sweep_kernel(first, last, *refs):
     if first:
-        initial, source, coarse, powers, rate, spread, *outs = refs
+        initial, source, coarse, powers, table, spread, *outs = refs
     else:
-        initial, received, source, coarse, powers, rate, spread, *outs = refs
+        initial, received, source, coarse, powers, table, spread, *outs = refs
     slices, groups, width, _ = coarse.shape
     per = spread.shape[0] // groups
-    keep = 1.0 - rate[...]
+    keep = 1.0 - table[0, RATE_ROW]
     for g in range(groups):
         here = group_rows(g, per)
         n = spread[here]
@@ -254,8 +281,8 @@
             states = [jnp.where(leading(), start, received[i, here]) for i in range(3)]
         for l in range(slices):
             s = source[l, here]
-            if last is not None:
-                outs[0][l, g] = class_sums(states[1], last[g:g + 1])
+            if last:
+                outs[0][l, g] = class_sums(states[1], table[g, COUNT_ROW])
             w = powers[l, g, :, FINE_MIN * width:]
             x = mul(s, w)
             total = x[:, FINE_MIN * width:]
@@ -276,25 +303,26 @@
                 sourced + by_count(x[:per], n, FINE_MIN, width) + moved[per:2 * per],
                 sourced + by_count(x[per:], n, FINE_MIN, width) + moved[2 * per:],
             ]
-            if last is not None:
+            if last:
                 outs[1][l, here] = states[2]
-        if last is None:
+        if not last:
             for i in range(3):
                 outs[0][i, here] = states[i]
 
 
-def last_sweep_kernel(initial, received, source, coarse, powers, rate, counts, spread, *outs):
-    sweep_kernel(False, counts, initial, received, source, coarse, powers, rate, spread, *outs)
-
-
-def gather_kernel(parts, base, out):
+def middle_kernel(parts, base, out):
     n, rows, _ = parts.shape
     total = parts[0]
     for p in range(1, n):
         total = total + parts[p]
-    for p in range(n):
-        out[p, :rows] = total
-        out[p, rows:] = base[...]
+    out[:rows] = total
+    out[rows:] = base[...]
+
+
+def gather_kernel(a, b, out):
+    total = a[...] + b[...]
+    for p in range(out.shape[0]):
+        out[p] = total
 
 
 def wide(row):
@@ -320,11 +348,11 @@
     return assembled(known, width)
 
 
-def folded(a, rate, powers, width):
-    x = mul(a * rate, powers)
+def shifted(products, width):
     out = jnp.zeros((2 * ROWS, width), F32)
+    empty = jnp.zeros((ROWS, width), F32)
     for d in range(1, FINE_MAX + 1):
-        z = jnp.concatenate([x[:, block(d, width)], jnp.zeros((ROWS, width), F32)], axis=0)
+        z = jnp.concatenate([products[:, block(d, width)], empty], axis=0)
         out = out + pltpu.roll(z, d, 0)
     return out
 
@@ -333,7 +361,7 @@
     groups = powers.shape[1]
     rows = [0.0] * 3
     for g in range(groups):
-        h = folded(a, rate, powers[l, g, :, :FINE_MAX * width], width)
+        h = shifted(mul(a * rate, powers[l, g, :, :FINE_MAX * width]), width)
         total = per * h[4:5]
         for i in range(1, 4):
             total = total + active[g, i:i + 1] * (h[4 + i:5 + i] - h[3 + i:4 + i])
@@ -353,13 +381,14 @@
         out[p] = rows
 
 
-def mixing_kernel(everyone, per, mine, theirs, base, powers, rate, active,
+def mixing_kernel(everyone, per, mine, theirs, base, powers, table,
                   mixing, averages, out, held):
     slices, _, _, wider = powers.shape
     width = wider // (FINE_MAX + 1)
     half = slices // 2
     n, rows, _ = mine.shape
     rows -= slices * ROWS
+    rate = table[0, RATE_ROW]
     core = lax.rem(lax.axis_index("cell"), 2)
     mixed = 0.0
     for ref, at in ((mine, core), (theirs, 1 - core)):
@@ -372,33 +401,31 @@
         for i in range(MATS):
             at = (l * MATS + i) * width
             mixing[l, :, block(i + 1, width)] = stacked(held[at:at + width])
-        a.append(first_averages(mixed[l * ROWS:(l + 1) * ROWS], mixing[l], rate[...], width))
+        a.append(first_averages(mixed[l * ROWS:(l + 1) * ROWS], mixing[l], rate, width))
         averages[l] = a[-1]
-    send_rows(everyone, per, a, base, rate[...], powers, active, out, width)
-
-
-def first_kernel(everyone, per, received, base, mixing, powers, rate, active, averages, out):
+    send_rows(everyone, per, a, base, rate, powers, table, out, width)
+
+
+def first_kernel(everyone, per, received, base, mixing, powers, table, averages, out):
     slices, _, _, wider = powers.shape
     width = wider // (FINE_MAX + 1)
+    rate = table[0, RATE_ROW]
     total = received[0]
     for p in range(1, received.shape[0]):
         total = total + received[p]
     a = []
     for l in range(slices):
         rows = total[l * (FINE_MIN + 1):(l + 1) * (FINE_MIN + 1)]
-        a.append(first_averages(rows, mixing[l], rate[...], width))
+        a.append(first_averages(rows, mixing[l], rate, width))
         averages[l] = a[-1]
-    send_rows(everyone, per, a, base, rate[...], powers, active, out, width)
-
-
-def push_kernel(received, averages, mixing, powers, rate, coarse, *refs):
-    if len(refs) == 2:
-        plain, starts, (pushes, end) = None, None, refs
-    else:
-        plain, starts, pushes, end = refs
+    send_rows(everyone, per, a, base, rate, powers, table, out, width)
+
+
+def push_kernel(received, averages, mixing, powers, table, coarse, *refs):
+    starts, (pushes, end) = (None, refs) if len(refs) == 2 else (refs[0], refs[1:])
     slices, groups, _, wider = powers.shape
     width = wider // (FINE_MAX + 1)
-    r = rate[...]
+    r = table[0, RATE_ROW]
     total = received[0]
     for p in range(1, received.shape[0]):
         total = total + received[p]
@@ -413,11 +440,17 @@
         for m, row in ((5, a5), (6, a6), (7, a7)):
             a = jnp.where(row_is(m, a.shape), row, a)
         for g in range(groups):
-            h = folded(a, r, powers[l, g, :, :FINE_MAX * width], width)[FINE_MIN:FINE_MIN + ROWS]
-            if plain is not None:
-                h = h + plain[l, g]
+            w = powers[l, g, :, :FINE_MAX * width]
+            if starts is None:
+                h = shifted(mul(a * r, w), width)[FINE_MIN:FINE_MIN + ROWS]
+                old = x[g]
+            else:
+                both = jnp.concatenate([a * r, starts[l, g] * (1.0 - r)], axis=0)
+                z = mul(both, w)
+                h = shifted(z[:ROWS], width)[FINE_MIN:FINE_MIN + ROWS]
+                h = h + picked(z[ROWS:], FINE_MIN, width)
+                old = x[g] - starts[l, g]
             pushes[l, g] = h
-            old = x[g] if starts is None else x[g] - starts[l, g]
             x[g] = h + mul(old, stacked(coarse[l, g]))
     for g in range(groups):
         end[g] = x[g]
@@ -432,17 +465,17 @@
         end[g] = x
 
 
-def second_kernel(everyone, received, pushes, coarse, sums, active, powers, rate, ofsource,
+def second_kernel(everyone, received, pushes, coarse, sums, table, powers, ofsource,
                   starts, base, out):
     slices, groups, width, _ = coarse.shape
-    keep = 1.0 - rate[...]
+    keep = 1.0 - table[0, RATE_ROW]
     x = [jnp.where(leading(), 0.0, received[g]) for g in range(groups)]
     sent = []
     for l in range(slices):
         rows = 0.0
         for g in range(groups):
             starts[l, g] = x[g]
-            n = active[g]
+            n = table[g]
             exact = n - pltpu.roll(n, ROWS - 1, 0)
             exact = jnp.where(row_is(ROWS - 1, n.shape), 0.0, exact)
             weighted = exact * x[g]
@@ -463,21 +496,12 @@
         out[p] = sent
 
 
-def plain_kernel(starts, powers, rate, out):
-    slices, groups, _, wider = powers.shape
-    width = wider // (FINE_MAX + 1)
-    keep = 1.0 - rate[...]
-    for l in range(slices):
-        for g in range(groups):
-            out[l, g] = picked(mul(starts[l, g] * keep, powers[l, g, :, :FINE_MAX * width]), FINE_MIN, width)
-
-
-def finish_kernel(received, pushes, starts, coarse, ends, counts, out):
+def finish_kernel(received, pushes, starts, coarse, ends, table, out):
     slices, groups, width, _ = coarse.shape
-    per = counts.shape[1]
+    per = ends.shape[1] // groups
     for g in range(groups):
         here = group_rows(g, per)
-        n = spread_counts(counts[g:g + 1])
+        n = spread_counts(table[g, COUNT_ROW])
         x = jnp.where(leading(), 0.0, received[g])
         for l in range(slices):
             x = pushes[l, g] + mul(x - starts[l, g], stacked(coarse[l, g]))
@@ -495,8 +519,8 @@
     turns = lax.axis_size("tm") - 1
     everyone = cells * n_cell
     half = slices // 2
-    peers = n_cell // 2
-    shard = half * MATS * width // peers
+    near = near_size()
+    shard = half * MATS * width // near
     rate = mix_rate.reshape(1, width)
     counts = step_counts.reshape(groups, per)
     state = shape(cells, width)
@@ -506,60 +530,70 @@
     rows8 = shape(slices * ROWS, width)
     rows4 = shape(n_cell, slices * 4, width)
     averages = shape(slices, ROWS, width)
-
     mats = shape(half * MATS * width, width)
-    own, other, powers, spread, active = call(
+    inputs = (fine, rate, counts, initial, source, coarse)
+    own, other, powers, spread, table, sums0, source_sums, moved = call(
         functools.partial(setup_kernel, everyone), "setup",
         [
             mats, mats,
             shape(slices, groups, 2 * width, (FINE_MAX + 1) * width, dtype=BF16),
-            state, vector,
+            state, vector, vector, vectors, vector,
         ],
-        (fine, rate, counts),
-    )
-    sums0, source_sums, moved = call(
-        lead_kernel, "lead", [vector, vectors, vector], (initial, source, coarse, counts)
+        inputs,
+        scratch=[pltpu.VMEM(x.shape, x.dtype) for x in inputs]
+        + [pltpu.SemaphoreType.DMA((len(inputs),))],
+        space=pltpu.HBM,
     )
     for turn in range(turns):
         moved = from_behind(moved, "tm", 1)
         if turn + 1 < turns:
             moved, = call(relay_kernel, "relay", [vector], (sums0, moved, source_sums, coarse))
-    mine = (own + swap_core(other)).reshape(peers, shard, width)
-    parts = exchange(mine, same_core())
+    mine, = call(add_kernel, "add", [mats], (own, swap_core(other)))
+    parts = exchange(mine.reshape(near, shard, width), near_groups())
     base, ofsource = call(
         functools.partial(base_kernel, everyone), "base", [rows8, rows8],
-        (sums0, moved, source_sums, coarse, powers, rate),
+        (sums0, moved, source_sums, coarse, powers, table),
     )
     bundle = shape(3, cells, width)
     sent, = call(
-        functools.partial(sweep_kernel, True, None), "sweep", [bundle],
-        (initial, source, coarse, powers, rate, spread),
+        functools.partial(sweep_kernel, True, False), "sweep", [bundle],
+        (initial, source, coarse, powers, table, spread),
     )
     for turn in range(turns):
         sent = from_behind(sent, "tm", 1)
         if turn + 1 < turns:
             sent, = call(
-                functools.partial(sweep_kernel, False, None), "sweep", [bundle],
-                (initial, sent, source, coarse, powers, rate, spread),
+                functools.partial(sweep_kernel, False, False), "sweep", [bundle],
+                (initial, sent, source, coarse, powers, table, spread),
             )
+    block, = call(
+        middle_kernel, "middle", [shape(shard + slices * ROWS, width)], (parts, base)
+    )
+    far = jnp.zeros_like(block)
+    distance = 2 * near
+    while distance < n_cell:
+        far = far_swap(block, distance)
+        distance *= 2
+        if distance < n_cell:
+            block = block + far
     payload, = call(
-        gather_kernel, "gather", [shape(peers, shard + slices * ROWS, width)], (parts, base)
-    )
-    gathered = exchange(payload, same_core())
+        gather_kernel, "gather", [shape(near, shard + slices * ROWS, width)], (block, far)
+    )
+    gathered = exchange(payload, near_groups())
     sums, ends = call(
-        last_sweep_kernel, "sweep", [vectors, states],
-        (initial, sent, source, coarse, powers, rate, counts, spread),
+        functools.partial(sweep_kernel, False, True), "sweep", [vectors, states],
+        (initial, sent, source, coarse, powers, table, spread),
     )
     theirs = swap_core(gathered)
     mixing, first, out = call(
         functools.partial(mixing_kernel, everyone, per), "mixing",
         [shape(slices, 2 * width, MATS * width, dtype=BF16), averages, rows4],
-        (gathered, theirs, base, powers, rate, active),
+        (gathered, theirs, base, powers, table),
         scratch=[pltpu.VMEM((slices * MATS * width, width), F32)],
     )
     pushes1, end = call(
         push_kernel, "push", [vectors, vector],
-        (exchange(out), first, mixing, powers, rate, coarse),
+        (exchange(out), first, mixing, powers, table, coarse),
     )
     nothing = jnp.zeros(vectors.shape, F32)
     moved = end
@@ -570,17 +604,15 @@
     moved1, base, out = call(
         functools.partial(second_kernel, everyone), "second",
         [vectors, rows8, shape(n_cell, slices * (FINE_MIN + 1), width)],
-        (moved, pushes1, coarse, sums, active, powers, rate, ofsource),
-    )
-    got = exchange(out)
-    plain, = call(plain_kernel, "plain", [vectors], (moved1, powers, rate))
+        (moved, pushes1, coarse, sums, table, powers, ofsource),
+    )
     first, out = call(
         functools.partial(first_kernel, everyone, per), "first", [averages, rows4],
-        (got, base, mixing, powers, rate, active),
+        (exchange(out), base, mixing, powers, table),
     )
     pushes2, end = call(
         push_kernel, "push", [vectors, vector],
-        (exchange(out), first, mixing, powers, rate, coarse, plain, moved1),
+        (exchange(out), first, mixing, powers, table, coarse, moved1),
     )
     moved = end
     for turn in range(turns):
@@ -588,7 +620,7 @@
         if turn + 1 < turns:
             moved, = call(vectors_kernel, "vectors", [vector], (moved, pushes2, moved1, coarse))
     out, = call(
-        finish_kernel, "finish", [states], (moved, pushes2, moved1, coarse, ends, counts)
+        finish_kernel, "finish", [states], (moved, pushes2, moved1, coarse, ends, table)
     )
     return out
 

time: 105 us -> 94.2 us (0.90)
  waiting for transfers between devices: 16.1 us -> 12.1 us
  starting transfers between devices: 23.4 us -> 19.8 us
  local copies, waits for them, and re-layouts: 9.22 us -> 5.89 us
  blocking collectives: 39.2 us -> 41.8 us
    all_to_all x2 -> x1, waiting for transfers between devices: 12 us -> 2.2 us  [exchange(): return lax.all_to_all(block, 'cell', 0, 0, axis_index_groups=groups)]
    all_to_all x2 -> x1, starting transfers between devices: 11.3 us -> 5.16 us  [exchange(): return lax.all_to_all(block, 'cell', 0, 0, axis_index_groups=groups)]
    ppermute x0 -> x1, waiting for transfers between devices: none -> 5.72 us  [far_swap(): return lax.ppermute(block, 'cell', [(i, i ^ distance) for i in range(n)])]
    unnamed x60 -> x24, local copies, waits for them, and re-layouts: 9.22 us -> 5.89 us
    ppermute x0 -> x1, starting transfers between devices: none -> 2.66 us  [far_swap(): return lax.ppermute(block, 'cell', [(i, i ^ distance) for i in range(n)])]
    all_to_all x3 -> x4, blocking collectives: 39.2 us -> 41.8 us  [exchange(): return lax.all_to_all(block, 'cell', 0, 0, axis_index_groups=groups)]
  transfers between devices with their start and end apart: 8 -> 8, of which waited for: 5 -> 5; matrix products, arithmetic and copies ran while one was open for 0% -> 0% of each run, Pallas kernels for 8% -> 7%
where the time goes in v4:
time: 94.2 us; the launch traced here: 93.7 us
  blocking collectives  41.8 us (44%)
  starting transfers between devices  19.8 us (21%)
  Pallas kernels  14 us (15%)
  waiting for transfers between devices  12.1 us (13%)
  local copies, waits for them, and re-layouts  5.89 us (6%)
    all_to_all x4, blocking collectives, exchange(): return lax.all_to_all(block, 'cell', 0, 0, axis_index_groups=groups)  41.8 us
    pallas_call x13, Pallas kernels, call(): pl.pallas_call(kernel, out_shape=outs, in_specs=[pl.BlockSpec(memory_spac...  14 us
    ppermute x4, starting transfers between devices, from_behind(): return lax.ppermute(block, axis, route)  11.4 us
    unnamed x24, local copies, waits for them, and re-layouts  5.89 us
    ppermute x1, waiting for transfers between devices, far_swap(): return lax.ppermute(block, 'cell', [(i, i ^ distance) for i in range(n)])  5.72 us
    all_to_all x1, starting transfers between devices, exchange(): return lax.all_to_all(block, 'cell', 0, 0, axis_index_groups=groups)  5.16 us
    ppermute x4, waiting for transfers between devices, from_behind(): return lax.ppermute(block, axis, route)  2.7 us
    ppermute x1, starting transfers between devices, far_swap(): return lax.ppermute(block, 'cell', [(i, i ^ distance) for i in range(n)])  2.66 us
  transfers between devices with their start and end apart: 8, of which 5 were waited for; matrix products, arithmetic and copies ran while one was open for 0% of the time, Pallas kernels for 7%

profile of v4, /device:TPU:0, one launch (start us, length us, event | category | flops | bytes accessed | tf_op | source)
XLA Modules:
  0.0 93.7 jit_solution(12421400989988034076)
XLA Ops:
  0.0 0.9 %copy-done = f32[2,2,128,128]{3,2,1,0:T(8,128)S(1)} copy-done((f32[2,2,128,128]{3,2,1,0:T(8,128)S(1)}, f32[2,2,128,128]{3,2,1,0:T(8,128)}, u32[]{:S(2)}) %copy-start) | copy-done | bytes 262168
  1.0 0.9 %copy-done.2 = f32[2,256,128]{2,1,0:T(8,128)S(1)} copy-done((f32[2,256,128]{2,1,0:T(8,128)S(1)}, f32[2,256,128]{2,1,0:T(8,128)}, u32[]{:S(2)}) %copy-start.2) | copy-done | bytes 262168
  2.8 0.9 %copy-done.9 = f32[2,2,128,128]{3,2,1,0:T(8,128)S(1)} copy-done((f32[2,2,128,128]{3,2,1,0:T(8,128)S(1)}, f32[2,2,128,128]{3,2,1,0:T(8,128)}, u32[]{:S(2)}) %copy-start.9) | copy-done | bytes 262168
  5.1 3.3 %setup.1 = (f32[896,128]{1,0:T(8,128)S(1)}, f32[896,128]{1,0:T(8,128)S(1)}, bf16[2,2,256,1152]{3,2,1,0:T(8,128)(2,1)S(1)}, f32[256,128]{1,0:T(8,128)S(1)}, f32[2...) custom-call(f32[2,2,128,128]{3,2,1,0:T(8,128)S(1)} %copy-done.9, ...), custom_call_target="tpu_custom_call" | custom-call | bytes 4367872 | tf_op jit(solution)/shard_map/setup/pallas_call | solution.py:85
  9.0 1.4 %collective-permute-done.b = f32[896,128]{1,0:T(8,128)S(1)} collective-permute-done((f32[896,128]{1,0:T(8,128)S(1)}, f32[896,128]{1,0:T(8,128)S(1)}, u32[]{:S(2)}, u32[]{:S(2)}) %collective-permute-start) | collective-permute-done | bytes 458784 | tf_op jit(solution)/shard_map/ppermute | solution.py:56
  11.3 5.2 %all-to-all-start = ((f32[4,224,128]{2,1,0:T(8,128)}), f32[4,224,128]{2,1,0:T(8,128)S(1)}, u32[]{:S(2)}, u32[]{:S(2)}) async-start(f32[4,224,128]{2,1,0:T(8,128)} %bitcast.3), calls=%async_computation | async-start | bytes 917504 | tf_op jit(solution)/shard_map/all_to_all | solution.py:79
  16.4 3.4 %collective-permute-start.1 = (f32[2,8,128]{2,1,0:T(8,128)S(1)}, f32[2,8,128]{2,1,0:T(8,128)S(1)}, u32[]{:S(2)}, u32[]{:S(2)}) collective-permute-start(f32[2,8,128]{2,1,0:T(8,128)S(1)} %get-tuple-element.32), channel_id=1, source_target_pairs={{0,16},{1,17},{2,18},{3,19},{4,20},{5,21},{6,22},{7,23},{8,24},{9,... | collective-permute-start | bytes 24584 | tf_op jit(solution)/shard_map/ppermute | solution.py:51
  19.8 1.3 %collective-permute-done.1.received = f32[2,8,128]{2,1,0:T(8,128)S(1)} collective-permute-done((f32[2,8,128]{2,1,0:T(8,128)S(1)}, f32[2,8,128]{2,1,0:T(8,128)S(1)}, u32[]{:S(2)}, u32[]{:S(2)}) %collective-permute-start.1) | collective-permute-done | bytes 8224 | tf_op jit(solution)/shard_map/ppermute | solution.py:51
  21.8 2.2 %all-to-all-done.parts = f32[4,224,128]{2,1,0:T(8,128)S(1)} async-done(((f32[4,224,128]{2,1,0:T(8,128)}), f32[4,224,128]{2,1,0:T(8,128)S(1)}, u32[]{:S(2)}, u32[]{:S(2)}) %all-to-all-start) | async-done | bytes 458784 | tf_op jit(solution)/shard_map/all_to_all | solution.py:79
  24.1 2.7 %collective-permute-start.2 = (f32[240,128]{1,0:T(8,128)S(1)}, f32[240,128]{1,0:T(8,128)S(1)}, u32[]{:S(2)}, u32[]{:S(2)}) collective-permute-start(f32[240,128]{1,0:T(8,128)S(1)} %middle.1.a), channel_id=1, source_target_pairs={{0,8},{1,9},{2,10},{3,11},{4,12},{5,13},{6,14},{7,15},{8,0},{9,1},... | collective-permute-start | bytes 368648 | tf_op jit(solution)/shard_map/ppermute | solution.py:75
  26.7 5.7 %collective-permute-done.2.b = f32[240,128]{1,0:T(8,128)S(1)} collective-permute-done((f32[240,128]{1,0:T(8,128)S(1)}, f32[240,128]{1,0:T(8,128)S(1)}, u32[]{:S(2)}, u32[]{:S(2)}) %collective-permute-start.2) | collective-permute-done | bytes 122912 | tf_op jit(solution)/shard_map/ppermute | solution.py:75
  32.5 10.1 %all_to_all.25.mine = f32[4,240,128]{2,1,0:T(8,128)S(1)} all-to-all(f32[4,240,128]{2,1,0:T(8,128)S(1)} %gather.1), channel_id=1, replica_groups={{0,2,4,6},{1,3,5,7},{8,10,12,14},{9,11,13,15},{16,18,20,22},{17,19,21,2..., dimensions={0} | all-to-all | bytes 983040 | tf_op jit(solution)/shard_map/all_to_all | solution.py:79
  42.6 1.8 %sweep.2 = f32[3,256,128]{2,1,0:T(8,128)S(1)} custom-call(f32[256,128]{1,0:T(8,128)S(1)} %copy-done.6, f32[2,256,128]{2,1,0:T(8,128)S(1)} %copy-done.3, f32[2,2,128,128]{3,2,1,0:T(8,128)S(1)} %copy-done.1, bf16[2,2,256,1152]{3,2,1,0:T(8,128)(2,1)S(1)} %get-tuple-element.34.powers.refs_3_.refs_4_, f32[2,8,128]{2,1,0:T(8,128)S(1)} %get-tuple-element.35.table.refs_4_.refs_5_, ...), custom_call_target="tpu_custom_call" | custom-call | bytes 3547136 | tf_op jit(solution)/shard_map/sweep/pallas_call | solution.py:85
  44.4 3.4 %collective-permute-start.5 = (f32[3,256,128]{2,1,0:T(8,128)S(1)}, f32[3,256,128]{2,1,0:T(8,128)S(1)}, u32[]{:S(2)}, u32[]{:S(2)}) collective-permute-start(f32[3,256,128]{2,1,0:T(8,128)S(1)} %sweep.2), channel_id=1, source_target_pairs={{0,16},{1,17},{2,18},{3,19},{4,20},{5,21},{6,22},{7,23},{8,24},{9,... | collective-permute-start | bytes 1179656 | tf_op jit(solution)/shard_map/ppermute | solution.py:51
  47.8 1.4 %mixing.1 = (bf16[2,256,896]{2,1,0:T(8,128)(2,1)S(1)}, f32[2,8,128]{2,1,0:T(8,128)S(1)}, f32[16,8,128]{2,1,0:T(8,128)S(1)}) custom-call(f32[4,240,128]{2,1,0:T(8,128)S(1)} %all_to_all.25.mine, f32[4,240,128]{2,1,0:T(8,128)S(1)} %collective-permute-done.3.theirs, f32[16,128]{1,0:T(8,128)S(1)} %get-tuple-element.36.base, ...), custom_call_target="tpu_custom_call" | custom-call | bytes 4349952 | tf_op jit(solution)/shard_map/mixing/pallas_call | solution.py:85
  49.2 11.7 %all_to_all.26.received = f32[16,8,128]{2,1,0:T(8,128)S(1)} all-to-all(f32[16,8,128]{2,1,0:T(8,128)S(1)} %get-tuple-element.37), channel_id=1, replica_groups=mesh['tm'=2,'cell'=16] {'cell'}, dimensions={0} | all-to-all | bytes 131072 | tf_op jit(solution)/shard_map/all_to_all | solution.py:79
  61.8 1.4 %collective-permute-start.4 = (f32[2,8,128]{2,1,0:T(8,128)S(1)}, f32[2,8,128]{2,1,0:T(8,128)S(1)}, u32[]{:S(2)}, u32[]{:S(2)}) collective-permute-start(f32[2,8,128]{2,1,0:T(8,128)S(1)} %get-tuple-element.40), channel_id=1, source_target_pairs={{0,16},{1,17},{2,18},{3,19},{4,20},{5,21},{6,22},{7,23},{8,24},{9,... | collective-permute-start | bytes 24584 | tf_op jit(solution)/shard_map/ppermute | solution.py:51
  63.2 2.3 %sweep.3 = (f32[2,2,8,128]{3,2,1,0:T(8,128)S(1)}, f32[2,256,128]{2,1,0:T(8,128)S(1)}) custom-call(f32[256,128]{1,0:T(8,128)S(1)} %copy-done.6, f32[3,256,128]{2,1,0:T(8,128)S(1)} %collective-permute-done.5.refs_1_, f32[2,256,128]{2,1,0:T(8,128)S(1)} %copy-done.3, f32[2,2,128,128]{3,2,1,0:T(8,128)S(1)} %copy-done.1, ...), custom_call_target="tpu_custom_call" | custom-call | bytes 3825664 | tf_op jit(solution)/shard_map/sweep/pallas_call | solution.py:85
  65.9 10.5 %all_to_all.27.received = f32[16,10,128]{2,1,0:T(8,128)S(1)} all-to-all(f32[16,10,128]{2,1,0:T(8,128)S(1)} %get-tuple-element.45), channel_id=1, replica_groups=mesh['tm'=2,'cell'=16] {'cell'}, dimensions={0} | all-to-all | bytes 163840 | tf_op jit(solution)/shard_map/all_to_all | solution.py:79
  76.4 1.2 %first.1 = (f32[2,8,128]{2,1,0:T(8,128)S(1)}, f32[16,8,128]{2,1,0:T(8,128)S(1)}) custom-call(f32[16,10,128]{2,1,0:T(8,128)S(1)} %all_to_all.27.received, f32[16,128]{1,0:T(8,128)S(1)} %get-tuple-element.46.base, bf16[2,256,896]{2,1,0:T(8,128)(2,1)S(1)} %get-tuple-element.39.mixing, bf16[2,2,256,1152]{3,2,1,0:T(8,128)(2,1)S(1)} %get-tuple-element.34.powers.refs_3_.refs_4_, ...), custom_call_target="tpu_custom_call" | custom-call | bytes 3448832 | tf_op jit(solution)/shard_map/first/pallas_call | solution.py:85
  77.6 9.5 %all_to_all.28.received = f32[16,8,128]{2,1,0:T(8,128)S(1)} all-to-all(f32[16,8,128]{2,1,0:T(8,128)S(1)} %get-tuple-element.47), channel_id=1, replica_groups=mesh['tm'=2,'cell'=16] {'cell'}, dimensions={0} | all-to-all | bytes 131072 | tf_op jit(solution)/shard_map/all_to_all | solution.py:79
  88.1 3.2 %collective-permute-start.6 = (f32[2,8,128]{2,1,0:T(8,128)S(1)}, f32[2,8,128]{2,1,0:T(8,128)S(1)}, u32[]{:S(2)}, u32[]{:S(2)}) collective-permute-start(f32[2,8,128]{2,1,0:T(8,128)S(1)} %get-tuple-element.50), channel_id=1, source_target_pairs={{0,16},{1,17},{2,18},{3,19},{4,20},{5,21},{6,22},{7,23},{8,24},{9,... | collective-permute-start | bytes 24584 | tf_op jit(solution)/shard_map/ppermute | solution.py:51
  91.3 1.3 %collective-permute-done.6.received = f32[2,8,128]{2,1,0:T(8,128)S(1)} collective-permute-done((f32[2,8,128]{2,1,0:T(8,128)S(1)}, f32[2,8,128]{2,1,0:T(8,128)S(1)}, u32[]{:S(2)}, u32[]{:S(2)}) %collective-permute-start.6) | collective-permute-done | bytes 8224 | tf_op jit(solution)/shard_map/ppermute | solution.py:51
  92.7 1.0 %finish.1 = f32[2,256,128]{2,1,0:T(8,128)} custom-call(f32[2,8,128]{2,1,0:T(8,128)S(1)} %collective-permute-done.6.received, f32[2,2,8,128]{3,2,1,0:T(8,128)S(1)} %get-tuple-element.51.pushes, f32[2,2,8,128]{3,2,1,0:T(8,128)S(1)} %get-tuple-element.49.refs_0_.starts, f32[2,2,128,128]{3,2,1,0:T(8,128)S(1)} %copy-done.1, ...), custom_call_target="tpu_custom_call" | custom-call | bytes 835584 | tf_op jit(solution)/shard_map/finish/pallas_call | solution.py:85
  (33 shorter events, 6.7 us)
Async XLA Ops:
  0.0 0.9 %copy-start = (f32[2,2,128,128]{3,2,1,0:T(8,128)S(1)}, f32[2,2,128,128]{3,2,1,0:T(8,128)}, u32[]{:S(2)}) copy-start(f32[2,2,128,128]{3,2,1,0:T(8,128)} %coarse.9) | copy-start | bytes 786436
  1.0 0.9 %copy-start.2 = (f32[2,256,128]{2,1,0:T(8,128)S(1)}, f32[2,256,128]{2,1,0:T(8,128)}, u32[]{:S(2)}) copy-start(f32[2,256,128]{2,1,0:T(8,128)} %refs_2_.3) | copy-start | bytes 786436
  1.9 0.9 copy-start.5
  2.8 0.9 %copy-start.9 = (f32[2,2,128,128]{3,2,1,0:T(8,128)S(1)}, f32[2,2,128,128]{3,2,1,0:T(8,128)}, u32[]{:S(2)}) copy-start(f32[2,2,128,128]{3,2,1,0:T(8,128)} %refs_0_.3) | copy-start | bytes 786436
  3.8 0.7 copy-start.10
  4.4 0.7 copy-start.11
  5.1 16.1 %copy-start.1 = (f32[2,2,128,128]{3,2,1,0:T(8,128)S(1)}, f32[2,2,128,128]{3,2,1,0:T(8,128)}, u32[]{:S(2)}) copy-start(f32[2,2,128,128]{3,2,1,0:T(8,128)} %coarse.9) | copy-start | bytes 786436
  8.4 2.1 %copy-start.7 = (f32[256,128]{1,0:T(8,128)}, f32[256,128]{1,0:T(8,128)S(1)}, u32[]{:S(2)}) copy-start(f32[256,128]{1,0:T(8,128)S(1)} %get-tuple-element.42.refs_5_.refs_6_) | copy-start | bytes 393220
  8.4 2.0 %collective-permute-start = (f32[896,128]{1,0:T(8,128)S(1)}, f32[896,128]{1,0:T(8,128)S(1)}, u32[]{:S(2)}, u32[]{:S(2)}) collective-permute-start(f32[896,128]{1,0:T(8,128)S(1)} %get-tuple-element.30), channel_id=1, source_target_pairs={{0,1},{1,0},{2,3},{3,2},{4,5},{5,4},{6,7},{7,6},{8,9},{9,8},{10,11... | collective-permute-start | bytes 1376264 | tf_op jit(solution)/shard_map/ppermute | solution.py:56
  10.5 0.8 copy-start.4
  11.3 12.8 %all-to-all-start = ((f32[4,224,128]{2,1,0:T(8,128)}), f32[4,224,128]{2,1,0:T(8,128)S(1)}, u32[]{:S(2)}, u32[]{:S(2)}) async-start(f32[4,224,128]{2,1,0:T(8,128)} %bitcast.3), calls=%async_computation | async-start | bytes 917504 | tf_op jit(solution)/shard_map/all_to_all | solution.py:79
  16.4 4.7 %collective-permute-start.1 = (f32[2,8,128]{2,1,0:T(8,128)S(1)}, f32[2,8,128]{2,1,0:T(8,128)S(1)}, u32[]{:S(2)}, u32[]{:S(2)}) collective-permute-start(f32[2,8,128]{2,1,0:T(8,128)S(1)} %get-tuple-element.32), channel_id=1, source_target_pairs={{0,16},{1,17},{2,18},{3,19},{4,20},{5,21},{6,22},{7,23},{8,24},{9,... | collective-permute-start | bytes 24584 | tf_op jit(solution)/shard_map/ppermute | solution.py:51
  21.2 21.4 %copy-start.3 = (f32[2,256,128]{2,1,0:T(8,128)S(1)}, f32[2,256,128]{2,1,0:T(8,128)}, u32[]{:S(2)}) copy-start(f32[2,256,128]{2,1,0:T(8,128)} %refs_2_.3) | copy-start | bytes 786436
  21.2 21.4 %copy-start.6 = (f32[256,128]{1,0:T(8,128)S(1)}, f32[256,128]{1,0:T(8,128)}, u32[]{:S(2)}) copy-start(f32[256,128]{1,0:T(8,128)} %refs_0_.5) | copy-start | bytes 393220
  24.0 18.5 %copy-start.8 = (f32[256,128]{1,0:T(8,128)S(1)}, f32[256,128]{1,0:T(8,128)}, u32[]{:S(2)}) copy-start(f32[256,128]{1,0:T(8,128)} %copy-done.7) | copy-start | bytes 393220
  24.1 8.4 %collective-permute-start.2 = (f32[240,128]{1,0:T(8,128)S(1)}, f32[240,128]{1,0:T(8,128)S(1)}, u32[]{:S(2)}, u32[]{:S(2)}) collective-permute-start(f32[240,128]{1,0:T(8,128)S(1)} %middle.1.a), channel_id=1, source_target_pairs={{0,8},{1,9},{2,10},{3,11},{4,12},{5,13},{6,14},{7,15},{8,0},{9,1},... | collective-permute-start | bytes 368648 | tf_op jit(solution)/shard_map/ppermute | solution.py:75
  42.6 5.3 %collective-permute-start.3 = (f32[4,240,128]{2,1,0:T(8,128)S(1)}, f32[4,240,128]{2,1,0:T(8,128)S(1)}, u32[]{:S(2)}, u32[]{:S(2)}) collective-permute-start(f32[4,240,128]{2,1,0:T(8,128)S(1)} %all_to_all.25.mine), channel_id=1, source_target_pairs={{0,1},{1,0},{2,3},{3,2},{4,5},{5,4},{6,7},{7,6},{8,9},{9,8},{10,11... | collective-permute-start | bytes 1474568 | tf_op jit(solution)/shard_map/ppermute | solution.py:56
  44.4 18.8 %collective-permute-start.5 = (f32[3,256,128]{2,1,0:T(8,128)S(1)}, f32[3,256,128]{2,1,0:T(8,128)S(1)}, u32[]{:S(2)}, u32[]{:S(2)}) collective-permute-start(f32[3,256,128]{2,1,0:T(8,128)S(1)} %sweep.2), channel_id=1, source_target_pairs={{0,16},{1,17},{2,18},{3,19},{4,20},{5,21},{6,22},{7,23},{8,24},{9,... | collective-permute-start | bytes 1179656 | tf_op jit(solution)/shard_map/ppermute | solution.py:51
  61.8 3.7 %collective-permute-start.4 = (f32[2,8,128]{2,1,0:T(8,128)S(1)}, f32[2,8,128]{2,1,0:T(8,128)S(1)}, u32[]{:S(2)}, u32[]{:S(2)}) collective-permute-start(f32[2,8,128]{2,1,0:T(8,128)S(1)} %get-tuple-element.40), channel_id=1, source_target_pairs={{0,16},{1,17},{2,18},{3,19},{4,20},{5,21},{6,22},{7,23},{8,24},{9,... | collective-permute-start | bytes 24584 | tf_op jit(solution)/shard_map/ppermute | solution.py:51
  88.1 4.6 %collective-permute-start.6 = (f32[2,8,128]{2,1,0:T(8,128)S(1)}, f32[2,8,128]{2,1,0:T(8,128)S(1)}, u32[]{:S(2)}, u32[]{:S(2)}) collective-permute-start(f32[2,8,128]{2,1,0:T(8,128)S(1)} %get-tuple-element.50), channel_id=1, source_target_pairs={{0,16},{1,17},{2,18},{3,19},{4,20},{5,21},{6,22},{7,23},{8,24},{9,... | collective-permute-start | bytes 24584 | tf_op jit(solution)/shard_map/ppermute | solution.py:51

commit v5 on v4

--- a/solution.py
+++ b/solution.py
@@ -79,13 +79,13 @@
     return lax.all_to_all(block, "cell", 0, 0, axis_index_groups=groups)
 
 
-def call(kernel, name, outs, args, scratch=(), flops=0, space=pltpu.VMEM):
+def call(kernel, name, outs, args, scratch=(), flops=0):
     size = sum(x.size * x.dtype.itemsize for x in args)
     size += sum(x.size * x.dtype.itemsize for x in outs)
     return pl.pallas_call(
         kernel,
         out_shape=outs,
-        in_specs=[pl.BlockSpec(memory_space=space)] * len(args),
+        in_specs=[pl.BlockSpec(memory_space=pltpu.VMEM)] * len(args),
         out_specs=[pl.BlockSpec(memory_space=pltpu.VMEM)] * len(outs),
         scratch_shapes=list(scratch),
         compiler_params=pltpu.CompilerParams(vmem_limit_bytes=24 << 20),
@@ -120,25 +120,15 @@
         end[g] = V
 
 
-def setup_kernel(everyone, *refs):
-    outside, refs = refs[:6], refs[6:]
-    own, other, powers, spread, table, start_sums, source_sums, end = refs[:8]
-    held, arrived = refs[8:14], refs[14]
-    loads = [pltpu.make_async_copy(x, y, arrived.at[i]) for i, (x, y) in enumerate(zip(outside, held))]
-    for load in loads:
-        load.start()
-    fine, rate, counts, initial, source, coarse = held
+def setup_kernel(everyone, fine, rate, counts, own, other, lows, table):
     slices, groups, width, _ = fine.shape
     per = counts.shape[1]
     half = slices // 2
     core = lax.rem(lax.axis_index("cell"), 2)
-    for load in loads[:3]:
-        load.wait()
     keep = 1.0 - rate[...]
     alive = []
     for g in range(groups):
         k = counts[g:g + 1].astype(F32)
-        spread[group_rows(g, per)] = spread_counts(k)
         rows = [
             jnp.sum((k >= q).astype(F32), axis=1, keepdims=True)
             for q in range(FINE_MIN, FINE_MAX + 1)
@@ -154,21 +144,12 @@
         e6, e7, e72 = 0.0, 0.0, 0.0
         for g in range(groups):
             w1 = fine[l, g]
-            st1 = stacked(w1)
-            w2 = mul(w1 * keep, st1)
-            st2 = stacked(w2)
+            w2 = mul(w1 * keep, stacked(w1))
             first = jnp.concatenate([w1, w2], axis=0)
-            w34 = mul(first * keep, st2)
+            w34 = mul(first * keep, stacked(w2))
             w3, w4 = w34[:width], w34[width:]
-            st4 = stacked(w4)
-            w58 = mul(jnp.concatenate([first, w34], axis=0) * keep, st4)
-            powers[l, g, :, block(1, width)] = st1
-            powers[l, g, :, block(2, width)] = st2
-            powers[l, g, :, block(3, width)] = stacked(w3)
-            powers[l, g, :, block(4, width)] = st4
-            powers[l, g, :, block(FINE_MAX + 1, width)] = stacked((w1 + w2) + (w3 + w4))
-            for i in range(4):
-                powers[l, g, :, block(5 + i, width)] = stacked(w58[i * width:(i + 1) * width])
+            lows[l, g, :2 * width] = first
+            lows[l, g, 2 * width:] = w34
             sums = [t + w for t, w in zip(sums, (w1, w2, w3, w4))]
             e6 = e6 + alive[g][2] * w1
             e7 = e7 + alive[g][3] * w1
@@ -185,8 +166,24 @@
             @pl.when(core != l // half)
             def _():
                 other[at] = m
-    for load in loads[3:]:
-        load.wait()
+
+
+def extend_kernel(lows, table, powers):
+    slices, groups, _, width = lows.shape
+    keep = 1.0 - table[0, RATE_ROW]
+    for l in range(slices):
+        for g in range(groups):
+            ws = [lows[l, g, i * width:(i + 1) * width] for i in range(4)]
+            w58 = mul(lows[l, g] * keep, stacked(ws[3]))
+            ws += [w58[i * width:(i + 1) * width] for i in range(4)]
+            ws.append((ws[0] + ws[1]) + (ws[2] + ws[3]))
+            for i, w in enumerate(ws):
+                powers[l, g, :, block(i + 1, width)] = stacked(w)
+
+
+def lead_kernel(table, initial, source, coarse, start_sums, source_sums, end):
+    slices, groups, _, _ = coarse.shape
+    per = initial.shape[0] // groups
     for g in range(groups):
         here = group_rows(g, per)
         k = table[g, COUNT_ROW]
@@ -266,15 +263,15 @@
 
 def sweep_kernel(first, last, *refs):
     if first:
-        initial, source, coarse, powers, table, spread, *outs = refs
+        initial, source, coarse, powers, table, *outs = refs
     else:
-        initial, received, source, coarse, powers, table, spread, *outs = refs
+        initial, received, source, coarse, powers, table, *outs = refs
     slices, groups, width, _ = coarse.shape
-    per = spread.shape[0] // groups
+    per = initial.shape[0] // groups
     keep = 1.0 - table[0, RATE_ROW]
     for g in range(groups):
         here = group_rows(g, per)
-        n = spread[here]
+        n = spread_counts(table[g, COUNT_ROW])
         start = initial[here]
         states = [start] * 3
         if not first:
@@ -531,43 +528,38 @@
     rows4 = shape(n_cell, slices * 4, width)
     averages = shape(slices, ROWS, width)
     mats = shape(half * MATS * width, width)
-    inputs = (fine, rate, counts, initial, source, coarse)
-    own, other, powers, spread, table, sums0, source_sums, moved = call(
+    own, other, lows, table = call(
         functools.partial(setup_kernel, everyone), "setup",
-        [
-            mats, mats,
-            shape(slices, groups, 2 * width, (FINE_MAX + 1) * width, dtype=BF16),
-            state, vector, vector, vectors, vector,
-        ],
-        inputs,
-        scratch=[pltpu.VMEM(x.shape, x.dtype) for x in inputs]
-        + [pltpu.SemaphoreType.DMA((len(inputs),))],
-        space=pltpu.HBM,
+        [mats, mats, shape(slices, groups, 4 * width, width), vector],
+        (fine, rate, counts),
+    )
+    swapped = swap_core(other)
+    powers, = call(
+        extend_kernel, "extend",
+        [shape(slices, groups, 2 * width, (FINE_MAX + 1) * width, dtype=BF16)], (lows, table),
+    )
+    swapped, powers = lax.optimization_barrier((swapped, powers))
+    sums0, source_sums, moved = call(
+        lead_kernel, "lead", [vector, vectors, vector], (table, initial, source, coarse)
     )
     for turn in range(turns):
         moved = from_behind(moved, "tm", 1)
         if turn + 1 < turns:
             moved, = call(relay_kernel, "relay", [vector], (sums0, moved, source_sums, coarse))
-    mine, = call(add_kernel, "add", [mats], (own, swap_core(other)))
+    mine, = call(add_kernel, "add", [mats], (own, swapped))
     parts = exchange(mine.reshape(near, shard, width), near_groups())
     base, ofsource = call(
         functools.partial(base_kernel, everyone), "base", [rows8, rows8],
         (sums0, moved, source_sums, coarse, powers, table),
     )
+    block, = call(
+        middle_kernel, "middle", [shape(shard + slices * ROWS, width)], (parts, base)
+    )
+    block, later = lax.optimization_barrier((block, initial))
     bundle = shape(3, cells, width)
     sent, = call(
         functools.partial(sweep_kernel, True, False), "sweep", [bundle],
-        (initial, source, coarse, powers, table, spread),
-    )
-    for turn in range(turns):
-        sent = from_behind(sent, "tm", 1)
-        if turn + 1 < turns:
-            sent, = call(
-                functools.partial(sweep_kernel, False, False), "sweep", [bundle],
-                (initial, sent, source, coarse, powers, table, spread),
-            )
-    block, = call(
-        middle_kernel, "middle", [shape(shard + slices * ROWS, width)], (parts, base)
+        (later, source, coarse, powers, table),
     )
     far = jnp.zeros_like(block)
     distance = 2 * near
@@ -576,13 +568,21 @@
         distance *= 2
         if distance < n_cell:
             block = block + far
+    far, sent = lax.optimization_barrier((far, sent))
+    for turn in range(turns):
+        sent = from_behind(sent, "tm", 1)
+        if turn + 1 < turns:
+            sent, = call(
+                functools.partial(sweep_kernel, False, False), "sweep", [bundle],
+                (initial, sent, source, coarse, powers, table),
+            )
     payload, = call(
         gather_kernel, "gather", [shape(near, shard + slices * ROWS, width)], (block, far)
     )
     gathered = exchange(payload, near_groups())
     sums, ends = call(
         functools.partial(sweep_kernel, False, True), "sweep", [vectors, states],
-        (initial, sent, source, coarse, powers, table, spread),
+        (initial, sent, source, coarse, powers, table),
     )
     theirs = swap_core(gathered)
     mixing, first, out = call(

time: 94.2 us -> 87.4 us (0.928)
  waiting for transfers between devices: 12.1 us -> 8.81 us
  local copies, waits for them, and re-layouts: 5.89 us -> 3.06 us
    unnamed x24 -> x14, local copies, waits for them, and re-layouts: 5.89 us -> 3.06 us
    ppermute x1, waiting for transfers between devices: 5.72 us -> 3.91 us  [far_swap(): return lax.ppermute(block, 'cell', [(i, i ^ distance) for i in range(n)])]
    pallas_call x13 -> x15, Pallas kernels: 14 us -> 13.3 us  [call(): pl.pallas_call(kernel, out_shape=outs, in_specs=[pl.BlockSpec(memory_spac...]
  transfers between devices with their start and end apart: 8 -> 8, of which waited for: 5 -> 5; matrix products, arithmetic and copies ran while one was open for 0% -> 0% of each run, Pallas kernels for 7% -> 10%
where the time goes in v5:
time: 87.4 us; the launch traced here: 87 us
  blocking collectives  41.7 us (48%)
  starting transfers between devices  20 us (23%)
  Pallas kernels  13.3 us (15%)
  waiting for transfers between devices  8.81 us (10%)
  local copies, waits for them, and re-layouts  3.06 us (4%)
    all_to_all x4, blocking collectives, exchange(): return lax.all_to_all(block, 'cell', 0, 0, axis_index_groups=groups)  41.7 us
    pallas_call x15, Pallas kernels, call(): pl.pallas_call(kernel, out_shape=outs, in_specs=[pl.BlockSpec(memory_spac...  13.3 us
    ppermute x4, starting transfers between devices, from_behind(): return lax.ppermute(block, axis, route)  11.6 us
    all_to_all x1, starting transfers between devices, exchange(): return lax.all_to_all(block, 'cell', 0, 0, axis_index_groups=groups)  5.16 us
    ppermute x1, waiting for transfers between devices, far_swap(): return lax.ppermute(block, 'cell', [(i, i ^ distance) for i in range(n)])  3.91 us
    unnamed x14, local copies, waits for them, and re-layouts  3.06 us
    ppermute x4, waiting for transfers between devices, from_behind(): return lax.ppermute(block, axis, route)  2.7 us
    ppermute x1, starting transfers between devices, far_swap(): return lax.ppermute(block, 'cell', [(i, i ^ distance) for i in range(n)])  2.66 us
  transfers between devices with their start and end apart: 8, of which 5 were waited for; matrix products, arithmetic and copies ran while one was open for 0% of the time, Pallas kernels for 10%

profile of v5, /device:TPU:0, one launch (start us, length us, event | category | flops | bytes accessed | tf_op | source)
XLA Modules:
  0.0 87.0 jit_solution(8070866499966706186)
XLA Ops:
  0.0 0.9 %copy-done.4 = f32[2,2,128,128]{3,2,1,0:T(8,128)S(1)} copy-done((f32[2,2,128,128]{3,2,1,0:T(8,128)S(1)}, f32[2,2,128,128]{3,2,1,0:T(8,128)}, u32[]{:S(2)}) %copy-start.4) | copy-done | bytes 262168
  2.3 1.1 %setup.1 = (f32[896,128]{1,0:T(8,128)S(1)}, f32[896,128]{1,0:T(8,128)S(1)}, f32[2,2,512,128]{3,2,1,0:T(8,128)S(1)}, f32[2,8,128]{2,1,0:T(8,128)S(1)}) custom-call(f32[2,2,128,128]{3,2,1,0:T(8,128)S(1)} %copy-done.4, f32[1,128]{1,0:T(1,128)S(1)} %bitcast.5, s32[2,128]{1,0:T(2,128)S(1)} %bitcast.4), custom_call_target="tpu_custom_call" | custom-call | bytes 2237952 | tf_op jit(solution)/shard_map/setup/pallas_call | solution.py:85
  4.0 0.8 extend.1.powers.refs_3_.refs_4_
  6.2 5.2 %all-to-all-start = ((f32[4,224,128]{2,1,0:T(8,128)}), f32[4,224,128]{2,1,0:T(8,128)S(1)}, u32[]{:S(2)}, u32[]{:S(2)}) async-start(f32[4,224,128]{2,1,0:T(8,128)} %bitcast.3), calls=%async_computation | async-start | bytes 917504 | tf_op jit(solution)/shard_map/all_to_all | solution.py:79
  12.0 3.4 %collective-permute-start.1 = (f32[2,8,128]{2,1,0:T(8,128)S(1)}, f32[2,8,128]{2,1,0:T(8,128)S(1)}, u32[]{:S(2)}, u32[]{:S(2)}) collective-permute-start(f32[2,8,128]{2,1,0:T(8,128)S(1)} %get-tuple-element.40), channel_id=1, source_target_pairs={{0,16},{1,17},{2,18},{3,19},{4,20},{5,21},{6,22},{7,23},{8,24},{9,... | collective-permute-start | bytes 24584 | tf_op jit(solution)/shard_map/ppermute | solution.py:51
  15.5 1.3 %collective-permute-done.1.received = f32[2,8,128]{2,1,0:T(8,128)S(1)} collective-permute-done((f32[2,8,128]{2,1,0:T(8,128)S(1)}, f32[2,8,128]{2,1,0:T(8,128)S(1)}, u32[]{:S(2)}, u32[]{:S(2)}) %collective-permute-start.1) | collective-permute-done | bytes 8224 | tf_op jit(solution)/shard_map/ppermute | solution.py:51
  17.5 1.6 %all-to-all-done.parts = f32[4,224,128]{2,1,0:T(8,128)S(1)} async-done(((f32[4,224,128]{2,1,0:T(8,128)}), f32[4,224,128]{2,1,0:T(8,128)S(1)}, u32[]{:S(2)}, u32[]{:S(2)}) %all-to-all-start) | async-done | bytes 458784 | tf_op jit(solution)/shard_map/all_to_all | solution.py:79
  19.1 2.7 %collective-permute-start.2 = (f32[240,128]{1,0:T(8,128)S(1)}, f32[240,128]{1,0:T(8,128)S(1)}, u32[]{:S(2)}, u32[]{:S(2)}) collective-permute-start(f32[240,128]{1,0:T(8,128)S(1)} %middle.1.a), channel_id=1, source_target_pairs={{0,8},{1,9},{2,10},{3,11},{4,12},{5,13},{6,14},{7,15},{8,0},{9,1},... | collective-permute-start | bytes 368648 | tf_op jit(solution)/shard_map/ppermute | solution.py:75
  21.7 1.8 %sweep.2 = f32[3,256,128]{2,1,0:T(8,128)S(1)} custom-call(f32[256,128]{1,0:T(8,128)S(1)} %copy-done.3, f32[2,256,128]{2,1,0:T(8,128)S(1)} %copy-done.1, f32[2,2,128,128]{3,2,1,0:T(8,128)S(1)} %copy-done, bf16[2,2,256,1152]{3,2,1,0:T(8,128)(2,1)S(1)} %extend.1.powers.refs_3_.refs_4_, f32[2,8,128]{2,1,0:T(8,128)S(1)} %get-tuple-element.37.table.refs_4_.refs_5_), custom_call_target="tpu_custom_call" | custom-call | bytes 3416064 | tf_op jit(solution)/shard_map/sweep/pallas_call | solution.py:85
  23.5 3.9 %collective-permute-done.2.b = f32[240,128]{1,0:T(8,128)S(1)} collective-permute-done((f32[240,128]{1,0:T(8,128)S(1)}, f32[240,128]{1,0:T(8,128)S(1)}, u32[]{:S(2)}, u32[]{:S(2)}) %collective-permute-start.2) | collective-permute-done | bytes 122912 | tf_op jit(solution)/shard_map/ppermute | solution.py:75
  27.5 10.1 %all_to_all.25.mine = f32[4,240,128]{2,1,0:T(8,128)S(1)} all-to-all(f32[4,240,128]{2,1,0:T(8,128)S(1)} %gather.1), channel_id=1, replica_groups={{0,2,4,6},{1,3,5,7},{8,10,12,14},{9,11,13,15},{16,18,20,22},{17,19,21,2..., dimensions={0} | all-to-all | bytes 983040 | tf_op jit(solution)/shard_map/all_to_all | solution.py:79
  37.5 3.1 %collective-permute-start.5 = (f32[3,256,128]{2,1,0:T(8,128)S(1)}, f32[3,256,128]{2,1,0:T(8,128)S(1)}, u32[]{:S(2)}, u32[]{:S(2)}) collective-permute-start(f32[3,256,128]{2,1,0:T(8,128)S(1)} %sweep.2), channel_id=1, source_target_pairs={{0,16},{1,17},{2,18},{3,19},{4,20},{5,21},{6,22},{7,23},{8,24},{9,... | collective-permute-start | bytes 1179656 | tf_op jit(solution)/shard_map/ppermute | solution.py:51
  40.7 1.4 %mixing.1 = (bf16[2,256,896]{2,1,0:T(8,128)(2,1)S(1)}, f32[2,8,128]{2,1,0:T(8,128)S(1)}, f32[16,8,128]{2,1,0:T(8,128)S(1)}) custom-call(f32[4,240,128]{2,1,0:T(8,128)S(1)} %all_to_all.25.mine, f32[4,240,128]{2,1,0:T(8,128)S(1)} %collective-permute-done.3.theirs, f32[16,128]{1,0:T(8,128)S(1)} %get-tuple-element.43.base, ...), custom_call_target="tpu_custom_call" | custom-call | bytes 4349952 | tf_op jit(solution)/shard_map/mixing/pallas_call | solution.py:85
  42.1 11.6 %all_to_all.26.received = f32[16,8,128]{2,1,0:T(8,128)S(1)} all-to-all(f32[16,8,128]{2,1,0:T(8,128)S(1)} %get-tuple-element.47), channel_id=1, replica_groups=mesh['tm'=2,'cell'=16] {'cell'}, dimensions={0} | all-to-all | bytes 131072 | tf_op jit(solution)/shard_map/all_to_all | solution.py:79
  53.7 0.9 %push.2 = (f32[2,2,8,128]{3,2,1,0:T(8,128)S(1)}, f32[2,8,128]{2,1,0:T(8,128)S(1)}) custom-call(f32[16,8,128]{2,1,0:T(8,128)S(1)} %all_to_all.26.received, f32[2,8,128]{2,1,0:T(8,128)S(1)} %get-tuple-element.48.averages, bf16[2,256,896]{2,1,0:T(8,128)(2,1)S(1)} %get-tuple-element.49.mixing, bf16[2,2,256,1152]{3,2,1,0:T(8,128)(2,1)S(1)} %extend.1.powers.refs_3_.refs_4_, ...), custom_call_target="tpu_custom_call" | custom-call | bytes 3645440 | tf_op jit(solution)/shard_map/push/pallas_call | solution.py:85
  54.6 1.8 %collective-permute-start.4 = (f32[2,8,128]{2,1,0:T(8,128)S(1)}, f32[2,8,128]{2,1,0:T(8,128)S(1)}, u32[]{:S(2)}, u32[]{:S(2)}) collective-permute-start(f32[2,8,128]{2,1,0:T(8,128)S(1)} %get-tuple-element.50), channel_id=1, source_target_pairs={{0,16},{1,17},{2,18},{3,19},{4,20},{5,21},{6,22},{7,23},{8,24},{9,... | collective-permute-start | bytes 24584 | tf_op jit(solution)/shard_map/ppermute | solution.py:51
  56.5 2.3 %sweep.3 = (f32[2,2,8,128]{3,2,1,0:T(8,128)S(1)}, f32[2,256,128]{2,1,0:T(8,128)S(1)}) custom-call(f32[256,128]{1,0:T(8,128)S(1)} %copy-done.3, f32[3,256,128]{2,1,0:T(8,128)S(1)} %collective-permute-done.5.refs_1_, f32[2,256,128]{2,1,0:T(8,128)S(1)} %copy-done.1, f32[2,2,128,128]{3,2,1,0:T(8,128)S(1)} %copy-done, ...), custom_call_target="tpu_custom_call" | custom-call | bytes 3694592 | tf_op jit(solution)/shard_map/sweep/pallas_call | solution.py:85
  59.2 10.5 %all_to_all.27.received = f32[16,10,128]{2,1,0:T(8,128)S(1)} all-to-all(f32[16,10,128]{2,1,0:T(8,128)S(1)} %get-tuple-element.55), channel_id=1, replica_groups=mesh['tm'=2,'cell'=16] {'cell'}, dimensions={0} | all-to-all | bytes 163840 | tf_op jit(solution)/shard_map/all_to_all | solution.py:79
  69.7 1.2 %first.1 = (f32[2,8,128]{2,1,0:T(8,128)S(1)}, f32[16,8,128]{2,1,0:T(8,128)S(1)}) custom-call(f32[16,10,128]{2,1,0:T(8,128)S(1)} %all_to_all.27.received, f32[16,128]{1,0:T(8,128)S(1)} %get-tuple-element.56.base, bf16[2,256,896]{2,1,0:T(8,128)(2,1)S(1)} %get-tuple-element.49.mixing, bf16[2,2,256,1152]{3,2,1,0:T(8,128)(2,1)S(1)} %extend.1.powers.refs_3_.refs_4_, ...), custom_call_target="tpu_custom_call" | custom-call | bytes 3448832 | tf_op jit(solution)/shard_map/first/pallas_call | solution.py:85
  70.9 9.5 %all_to_all.28.received = f32[16,8,128]{2,1,0:T(8,128)S(1)} all-to-all(f32[16,8,128]{2,1,0:T(8,128)S(1)} %get-tuple-element.57), channel_id=1, replica_groups=mesh['tm'=2,'cell'=16] {'cell'}, dimensions={0} | all-to-all | bytes 131072 | tf_op jit(solution)/shard_map/all_to_all | solution.py:79
  80.4 0.9 %push.3 = (f32[2,2,8,128]{3,2,1,0:T(8,128)S(1)}, f32[2,8,128]{2,1,0:T(8,128)S(1)}) custom-call(f32[16,8,128]{2,1,0:T(8,128)S(1)} %all_to_all.28.received, f32[2,8,128]{2,1,0:T(8,128)S(1)} %get-tuple-element.58.averages, bf16[2,256,896]{2,1,0:T(8,128)(2,1)S(1)} %get-tuple-element.49.mixing, bf16[2,2,256,1152]{3,2,1,0:T(8,128)(2,1)S(1)} %extend.1.powers.refs_3_.refs_4_, ...), custom_call_target="tpu_custom_call" | custom-call | bytes 3661824 | tf_op jit(solution)/shard_map/push/pallas_call | solution.py:85
  81.3 3.3 %collective-permute-start.6 = (f32[2,8,128]{2,1,0:T(8,128)S(1)}, f32[2,8,128]{2,1,0:T(8,128)S(1)}, u32[]{:S(2)}, u32[]{:S(2)}) collective-permute-start(f32[2,8,128]{2,1,0:T(8,128)S(1)} %get-tuple-element.60), channel_id=1, source_target_pairs={{0,16},{1,17},{2,18},{3,19},{4,20},{5,21},{6,22},{7,23},{8,24},{9,... | collective-permute-start | bytes 24584 | tf_op jit(solution)/shard_map/ppermute | solution.py:51
  84.6 1.3 %collective-permute-done.6.received = f32[2,8,128]{2,1,0:T(8,128)S(1)} collective-permute-done((f32[2,8,128]{2,1,0:T(8,128)S(1)}, f32[2,8,128]{2,1,0:T(8,128)S(1)}, u32[]{:S(2)}, u32[]{:S(2)}) %collective-permute-start.6) | collective-permute-done | bytes 8224 | tf_op jit(solution)/shard_map/ppermute | solution.py:51
  85.9 1.0 %finish.1 = f32[2,256,128]{2,1,0:T(8,128)} custom-call(f32[2,8,128]{2,1,0:T(8,128)S(1)} %collective-permute-done.6.received, f32[2,2,8,128]{3,2,1,0:T(8,128)S(1)} %get-tuple-element.61.pushes, f32[2,2,8,128]{3,2,1,0:T(8,128)S(1)} %get-tuple-element.59.refs_0_.starts, f32[2,2,128,128]{3,2,1,0:T(8,128)S(1)} %copy-done, ...), custom_call_target="tpu_custom_call" | custom-call | bytes 835584 | tf_op jit(solution)/shard_map/finish/pallas_call | solution.py:85
  (25 shorter events, 5.2 us)
Async XLA Ops:
  0.0 0.9 %copy-start.4 = (f32[2,2,128,128]{3,2,1,0:T(8,128)S(1)}, f32[2,2,128,128]{3,2,1,0:T(8,128)}, u32[]{:S(2)}) copy-start(f32[2,2,128,128]{3,2,1,0:T(8,128)} %fine.1) | copy-start | bytes 786436
  1.0 0.7 copy-start.5
  1.6 0.7 copy-start.6
  3.4 2.0 %collective-permute-start = (f32[896,128]{1,0:T(8,128)S(1)}, f32[896,128]{1,0:T(8,128)S(1)}, u32[]{:S(2)}, u32[]{:S(2)}) collective-permute-start(f32[896,128]{1,0:T(8,128)S(1)} %get-tuple-element.35), channel_id=1, source_target_pairs={{0,1},{1,0},{2,3},{3,2},{4,5},{5,4},{6,7},{7,6},{8,9},{9,8},{10,11... | collective-permute-start | bytes 1376264 | tf_op jit(solution)/shard_map/ppermute | solution.py:56
  4.0 7.4 %copy-start = (f32[2,2,128,128]{3,2,1,0:T(8,128)S(1)}, f32[2,2,128,128]{3,2,1,0:T(8,128)}, u32[]{:S(2)}) copy-start(f32[2,2,128,128]{3,2,1,0:T(8,128)} %coarse.11) | copy-start | bytes 786436
  4.0 7.4 %copy-start.1 = (f32[2,256,128]{2,1,0:T(8,128)S(1)}, f32[2,256,128]{2,1,0:T(8,128)}, u32[]{:S(2)}) copy-start(f32[2,256,128]{2,1,0:T(8,128)} %refs_2_.3) | copy-start | bytes 786436
  4.0 7.4 %copy-start.3 = (f32[256,128]{1,0:T(8,128)S(1)}, f32[256,128]{1,0:T(8,128)}, u32[]{:S(2)}) copy-start(f32[256,128]{1,0:T(8,128)} %refs_0_.2) | copy-start | bytes 393220
  5.5 0.8 copy-start.2
  6.2 12.8 %all-to-all-start = ((f32[4,224,128]{2,1,0:T(8,128)}), f32[4,224,128]{2,1,0:T(8,128)S(1)}, u32[]{:S(2)}, u32[]{:S(2)}) async-start(f32[4,224,128]{2,1,0:T(8,128)} %bitcast.3), calls=%async_computation | async-start | bytes 917504 | tf_op jit(solution)/shard_map/all_to_all | solution.py:79
  12.0 4.8 %collective-permute-start.1 = (f32[2,8,128]{2,1,0:T(8,128)S(1)}, f32[2,8,128]{2,1,0:T(8,128)S(1)}, u32[]{:S(2)}, u32[]{:S(2)}) collective-permute-start(f32[2,8,128]{2,1,0:T(8,128)S(1)} %get-tuple-element.40), channel_id=1, source_target_pairs={{0,16},{1,17},{2,18},{3,19},{4,20},{5,21},{6,22},{7,23},{8,24},{9,... | collective-permute-start | bytes 24584 | tf_op jit(solution)/shard_map/ppermute | solution.py:51
  19.1 8.4 %collective-permute-start.2 = (f32[240,128]{1,0:T(8,128)S(1)}, f32[240,128]{1,0:T(8,128)S(1)}, u32[]{:S(2)}, u32[]{:S(2)}) collective-permute-start(f32[240,128]{1,0:T(8,128)S(1)} %middle.1.a), channel_id=1, source_target_pairs={{0,8},{1,9},{2,10},{3,11},{4,12},{5,13},{6,14},{7,15},{8,0},{9,1},... | collective-permute-start | bytes 368648 | tf_op jit(solution)/shard_map/ppermute | solution.py:75
  37.5 3.2 %collective-permute-start.3 = (f32[4,240,128]{2,1,0:T(8,128)S(1)}, f32[4,240,128]{2,1,0:T(8,128)S(1)}, u32[]{:S(2)}, u32[]{:S(2)}) collective-permute-start(f32[4,240,128]{2,1,0:T(8,128)S(1)} %all_to_all.25.mine), channel_id=1, source_target_pairs={{0,1},{1,0},{2,3},{3,2},{4,5},{5,4},{6,7},{7,6},{8,9},{9,8},{10,11... | collective-permute-start | bytes 1474568 | tf_op jit(solution)/shard_map/ppermute | solution.py:56
  37.5 18.9 %collective-permute-start.5 = (f32[3,256,128]{2,1,0:T(8,128)S(1)}, f32[3,256,128]{2,1,0:T(8,128)S(1)}, u32[]{:S(2)}, u32[]{:S(2)}) collective-permute-start(f32[3,256,128]{2,1,0:T(8,128)S(1)} %sweep.2), channel_id=1, source_target_pairs={{0,16},{1,17},{2,18},{3,19},{4,20},{5,21},{6,22},{7,23},{8,24},{9,... | collective-permute-start | bytes 1179656 | tf_op jit(solution)/shard_map/ppermute | solution.py:51
  54.6 4.1 %collective-permute-start.4 = (f32[2,8,128]{2,1,0:T(8,128)S(1)}, f32[2,8,128]{2,1,0:T(8,128)S(1)}, u32[]{:S(2)}, u32[]{:S(2)}) collective-permute-start(f32[2,8,128]{2,1,0:T(8,128)S(1)} %get-tuple-element.50), channel_id=1, source_target_pairs={{0,16},{1,17},{2,18},{3,19},{4,20},{5,21},{6,22},{7,23},{8,24},{9,... | collective-permute-start | bytes 24584 | tf_op jit(solution)/shard_map/ppermute | solution.py:51
  81.3 4.6 %collective-permute-start.6 = (f32[2,8,128]{2,1,0:T(8,128)S(1)}, f32[2,8,128]{2,1,0:T(8,128)S(1)}, u32[]{:S(2)}, u32[]{:S(2)}) collective-permute-start(f32[2,8,128]{2,1,0:T(8,128)S(1)} %get-tuple-element.60), channel_id=1, source_target_pairs={{0,16},{1,17},{2,18},{3,19},{4,20},{5,21},{6,22},{7,23},{8,24},{9,... | collective-permute-start | bytes 24584 | tf_op jit(solution)/shard_map/ppermute | solution.py:51

commit v6 on v5

--- a/solution.py
+++ b/solution.py
@@ -12,6 +12,7 @@
 CLASSES = FINE_MAX - FINE_MIN + 1
 MATS = 7
 ROWS = 8
+OPENING_FLOPS = 10**9
 COUNT_ROW = slice(6, 7)
 RATE_ROW = slice(7, 8)
 F32 = jnp.float32
@@ -120,7 +121,11 @@
         end[g] = V
 
 
-def setup_kernel(everyone, fine, rate, counts, own, other, lows, table):
+def opening_kernel(out):
+    out[...] = jnp.zeros_like(out)
+
+
+def setup_kernel(everyone, fine, rate, counts, opened, own, other, lows, table):
     slices, groups, width, _ = fine.shape
     per = counts.shape[1]
     half = slices // 2
@@ -528,10 +533,11 @@
     rows4 = shape(n_cell, slices * 4, width)
     averages = shape(slices, ROWS, width)
     mats = shape(half * MATS * width, width)
+    opened, = call(opening_kernel, "opening", [shape(ROWS, width)], (), flops=OPENING_FLOPS)
     own, other, lows, table = call(
         functools.partial(setup_kernel, everyone), "setup",
         [mats, mats, shape(slices, groups, 4 * width, width), vector],
-        (fine, rate, counts),
+        (fine, rate, counts, opened),
     )
     swapped = swap_core(other)
     powers, = call(

time: 87.4 us -> 86.1 us (0.985)
  local copies, waits for them, and re-layouts: 3.06 us -> 1.74 us
    unnamed x14, local copies, waits for them, and re-layouts: 3.06 us -> 1.74 us
    pallas_call x15 -> x16, Pallas kernels: 13.3 us -> 13.3 us  [call(): pl.pallas_call(kernel, out_shape=outs, in_specs=[pl.BlockSpec(memory_spac...]
where the time goes in v6:
time: 86.1 us; the launch traced here: 85.7 us
  blocking collectives  41.7 us (48%)
  starting transfers between devices  20 us (23%)
  Pallas kernels  13.3 us (15%)
  waiting for transfers between devices  8.82 us (10%)
  local copies, waits for them, and re-layouts  1.74 us (2%)
    all_to_all x4, blocking collectives, exchange(): return lax.all_to_all(block, 'cell', 0, 0, axis_index_groups=groups)  41.7 us
    pallas_call x16, Pallas kernels, call(): pl.pallas_call(kernel, out_shape=outs, in_specs=[pl.BlockSpec(memory_spac...  13.3 us
    ppermute x4, starting transfers between devices, from_behind(): return lax.ppermute(block, axis, route)  11.6 us
    all_to_all x1, starting transfers between devices, exchange(): return lax.all_to_all(block, 'cell', 0, 0, axis_index_groups=groups)  5.16 us
    ppermute x1, waiting for transfers between devices, far_swap(): return lax.ppermute(block, 'cell', [(i, i ^ distance) for i in range(n)])  3.92 us
    ppermute x4, waiting for transfers between devices, from_behind(): return lax.ppermute(block, axis, route)  2.7 us
    ppermute x1, starting transfers between devices, far_swap(): return lax.ppermute(block, 'cell', [(i, i ^ distance) for i in range(n)])  2.65 us
    unnamed x14, local copies, waits for them, and re-layouts  1.74 us
  transfers between devices with their start and end apart: 8, of which 5 were waited for; matrix products, arithmetic and copies ran while one was open for 0% of the time, Pallas kernels for 10%

profile of v6, /device:TPU:0, one launch (start us, length us, event | category | flops | bytes accessed | tf_op | source)
XLA Modules:
  0.0 85.7 jit_solution(11725327916295240323)
XLA Ops:
  1.0 1.1 %setup.1 = (f32[896,128]{1,0:T(8,128)S(1)}, f32[896,128]{1,0:T(8,128)S(1)}, f32[2,2,512,128]{3,2,1,0:T(8,128)S(1)}, f32[2,8,128]{2,1,0:T(8,128)S(1)}) custom-call(f32[2,2,128,128]{3,2,1,0:T(8,128)S(1)} %copy-done.4, f32[1,128]{1,0:T(1,128)S(1)} %bitcast.5, s32[2,128]{1,0:T(2,128)S(1)} %bitcast.4, f32[8,128]{1,0:T(8,128)S(1)} %opening.1.opened), custom_call_target="tpu_custom_call" | custom-call | bytes 2242048 | tf_op jit(solution)/shard_map/setup/pallas_call | solution.py:86
  2.7 0.8 extend.1.powers.refs_3_.refs_4_
  4.2 0.8 copy-done.2
  4.9 5.2 %all-to-all-start = ((f32[4,224,128]{2,1,0:T(8,128)}), f32[4,224,128]{2,1,0:T(8,128)S(1)}, u32[]{:S(2)}, u32[]{:S(2)}) async-start(f32[4,224,128]{2,1,0:T(8,128)} %bitcast.3), calls=%async_computation | async-start | bytes 917504 | tf_op jit(solution)/shard_map/all_to_all | solution.py:80
  10.7 3.4 %collective-permute-start.1 = (f32[2,8,128]{2,1,0:T(8,128)S(1)}, f32[2,8,128]{2,1,0:T(8,128)S(1)}, u32[]{:S(2)}, u32[]{:S(2)}) collective-permute-start(f32[2,8,128]{2,1,0:T(8,128)S(1)} %get-tuple-element.40), channel_id=1, source_target_pairs={{0,16},{1,17},{2,18},{3,19},{4,20},{5,21},{6,22},{7,23},{8,24},{9,... | collective-permute-start | bytes 24584 | tf_op jit(solution)/shard_map/ppermute | solution.py:52
  14.1 1.3 %collective-permute-done.1.received = f32[2,8,128]{2,1,0:T(8,128)S(1)} collective-permute-done((f32[2,8,128]{2,1,0:T(8,128)S(1)}, f32[2,8,128]{2,1,0:T(8,128)S(1)}, u32[]{:S(2)}, u32[]{:S(2)}) %collective-permute-start.1) | collective-permute-done | bytes 8224 | tf_op jit(solution)/shard_map/ppermute | solution.py:52
  16.2 1.6 %all-to-all-done.parts = f32[4,224,128]{2,1,0:T(8,128)S(1)} async-done(((f32[4,224,128]{2,1,0:T(8,128)}), f32[4,224,128]{2,1,0:T(8,128)S(1)}, u32[]{:S(2)}, u32[]{:S(2)}) %all-to-all-start) | async-done | bytes 458784 | tf_op jit(solution)/shard_map/all_to_all | solution.py:80
  17.7 2.7 %collective-permute-start.2 = (f32[240,128]{1,0:T(8,128)S(1)}, f32[240,128]{1,0:T(8,128)S(1)}, u32[]{:S(2)}, u32[]{:S(2)}) collective-permute-start(f32[240,128]{1,0:T(8,128)S(1)} %middle.1.a), channel_id=1, source_target_pairs={{0,8},{1,9},{2,10},{3,11},{4,12},{5,13},{6,14},{7,15},{8,0},{9,1},... | collective-permute-start | bytes 368648 | tf_op jit(solution)/shard_map/ppermute | solution.py:76
  20.4 1.8 %sweep.2 = f32[3,256,128]{2,1,0:T(8,128)S(1)} custom-call(f32[256,128]{1,0:T(8,128)S(1)} %copy-done.3, f32[2,256,128]{2,1,0:T(8,128)S(1)} %copy-done.1, f32[2,2,128,128]{3,2,1,0:T(8,128)S(1)} %copy-done, bf16[2,2,256,1152]{3,2,1,0:T(8,128)(2,1)S(1)} %extend.1.powers.refs_3_.refs_4_, f32[2,8,128]{2,1,0:T(8,128)S(1)} %get-tuple-element.37.table.refs_4_.refs_5_), custom_call_target="tpu_custom_call" | custom-call | bytes 3416064 | tf_op jit(solution)/shard_map/sweep/pallas_call | solution.py:86
  22.2 3.9 %collective-permute-done.2.b = f32[240,128]{1,0:T(8,128)S(1)} collective-permute-done((f32[240,128]{1,0:T(8,128)S(1)}, f32[240,128]{1,0:T(8,128)S(1)}, u32[]{:S(2)}, u32[]{:S(2)}) %collective-permute-start.2) | collective-permute-done | bytes 122912 | tf_op jit(solution)/shard_map/ppermute | solution.py:76
  26.2 10.1 %all_to_all.25.mine = f32[4,240,128]{2,1,0:T(8,128)S(1)} all-to-all(f32[4,240,128]{2,1,0:T(8,128)S(1)} %gather.1), channel_id=1, replica_groups={{0,2,4,6},{1,3,5,7},{8,10,12,14},{9,11,13,15},{16,18,20,22},{17,19,21,2..., dimensions={0} | all-to-all | bytes 983040 | tf_op jit(solution)/shard_map/all_to_all | solution.py:80
  36.2 3.1 %collective-permute-start.5 = (f32[3,256,128]{2,1,0:T(8,128)S(1)}, f32[3,256,128]{2,1,0:T(8,128)S(1)}, u32[]{:S(2)}, u32[]{:S(2)}) collective-permute-start(f32[3,256,128]{2,1,0:T(8,128)S(1)} %sweep.2), channel_id=1, source_target_pairs={{0,16},{1,17},{2,18},{3,19},{4,20},{5,21},{6,22},{7,23},{8,24},{9,... | collective-permute-start | bytes 1179656 | tf_op jit(solution)/shard_map/ppermute | solution.py:52
  39.4 1.4 %mixing.1 = (bf16[2,256,896]{2,1,0:T(8,128)(2,1)S(1)}, f32[2,8,128]{2,1,0:T(8,128)S(1)}, f32[16,8,128]{2,1,0:T(8,128)S(1)}) custom-call(f32[4,240,128]{2,1,0:T(8,128)S(1)} %all_to_all.25.mine, f32[4,240,128]{2,1,0:T(8,128)S(1)} %collective-permute-done.3.theirs, f32[16,128]{1,0:T(8,128)S(1)} %get-tuple-element.43.base, ...), custom_call_target="tpu_custom_call" | custom-call | bytes 4349952 | tf_op jit(solution)/shard_map/mixing/pallas_call | solution.py:86
  40.7 11.6 %all_to_all.26.received = f32[16,8,128]{2,1,0:T(8,128)S(1)} all-to-all(f32[16,8,128]{2,1,0:T(8,128)S(1)} %get-tuple-element.47), channel_id=1, replica_groups=mesh['tm'=2,'cell'=16] {'cell'}, dimensions={0} | all-to-all | bytes 131072 | tf_op jit(solution)/shard_map/all_to_all | solution.py:80
  52.4 0.9 %push.2 = (f32[2,2,8,128]{3,2,1,0:T(8,128)S(1)}, f32[2,8,128]{2,1,0:T(8,128)S(1)}) custom-call(f32[16,8,128]{2,1,0:T(8,128)S(1)} %all_to_all.26.received, f32[2,8,128]{2,1,0:T(8,128)S(1)} %get-tuple-element.48.averages, bf16[2,256,896]{2,1,0:T(8,128)(2,1)S(1)} %get-tuple-element.49.mixing, bf16[2,2,256,1152]{3,2,1,0:T(8,128)(2,1)S(1)} %extend.1.powers.refs_3_.refs_4_, ...), custom_call_target="tpu_custom_call" | custom-call | bytes 3645440 | tf_op jit(solution)/shard_map/push/pallas_call | solution.py:86
  53.3 1.8 %collective-permute-start.4 = (f32[2,8,128]{2,1,0:T(8,128)S(1)}, f32[2,8,128]{2,1,0:T(8,128)S(1)}, u32[]{:S(2)}, u32[]{:S(2)}) collective-permute-start(f32[2,8,128]{2,1,0:T(8,128)S(1)} %get-tuple-element.50), channel_id=1, source_target_pairs={{0,16},{1,17},{2,18},{3,19},{4,20},{5,21},{6,22},{7,23},{8,24},{9,... | collective-permute-start | bytes 24584 | tf_op jit(solution)/shard_map/ppermute | solution.py:52
  55.1 2.3 %sweep.3 = (f32[2,2,8,128]{3,2,1,0:T(8,128)S(1)}, f32[2,256,128]{2,1,0:T(8,128)S(1)}) custom-call(f32[256,128]{1,0:T(8,128)S(1)} %copy-done.3, f32[3,256,128]{2,1,0:T(8,128)S(1)} %collective-permute-done.5.refs_1_, f32[2,256,128]{2,1,0:T(8,128)S(1)} %copy-done.1, f32[2,2,128,128]{3,2,1,0:T(8,128)S(1)} %copy-done, ...), custom_call_target="tpu_custom_call" | custom-call | bytes 3694592 | tf_op jit(solution)/shard_map/sweep/pallas_call | solution.py:86
  57.9 10.5 %all_to_all.27.received = f32[16,10,128]{2,1,0:T(8,128)S(1)} all-to-all(f32[16,10,128]{2,1,0:T(8,128)S(1)} %get-tuple-element.55), channel_id=1, replica_groups=mesh['tm'=2,'cell'=16] {'cell'}, dimensions={0} | all-to-all | bytes 163840 | tf_op jit(solution)/shard_map/all_to_all | solution.py:80
  68.4 1.2 %first.1 = (f32[2,8,128]{2,1,0:T(8,128)S(1)}, f32[16,8,128]{2,1,0:T(8,128)S(1)}) custom-call(f32[16,10,128]{2,1,0:T(8,128)S(1)} %all_to_all.27.received, f32[16,128]{1,0:T(8,128)S(1)} %get-tuple-element.56.base, bf16[2,256,896]{2,1,0:T(8,128)(2,1)S(1)} %get-tuple-element.49.mixing, bf16[2,2,256,1152]{3,2,1,0:T(8,128)(2,1)S(1)} %extend.1.powers.refs_3_.refs_4_, ...), custom_call_target="tpu_custom_call" | custom-call | bytes 3448832 | tf_op jit(solution)/shard_map/first/pallas_call | solution.py:86
  69.6 9.5 %all_to_all.28.received = f32[16,8,128]{2,1,0:T(8,128)S(1)} all-to-all(f32[16,8,128]{2,1,0:T(8,128)S(1)} %get-tuple-element.57), channel_id=1, replica_groups=mesh['tm'=2,'cell'=16] {'cell'}, dimensions={0} | all-to-all | bytes 131072 | tf_op jit(solution)/shard_map/all_to_all | solution.py:80
  79.1 0.9 %push.3 = (f32[2,2,8,128]{3,2,1,0:T(8,128)S(1)}, f32[2,8,128]{2,1,0:T(8,128)S(1)}) custom-call(f32[16,8,128]{2,1,0:T(8,128)S(1)} %all_to_all.28.received, f32[2,8,128]{2,1,0:T(8,128)S(1)} %get-tuple-element.58.averages, bf16[2,256,896]{2,1,0:T(8,128)(2,1)S(1)} %get-tuple-element.49.mixing, bf16[2,2,256,1152]{3,2,1,0:T(8,128)(2,1)S(1)} %extend.1.powers.refs_3_.refs_4_, ...), custom_call_target="tpu_custom_call" | custom-call | bytes 3661824 | tf_op jit(solution)/shard_map/push/pallas_call | solution.py:86
  80.0 3.3 %collective-permute-start.6 = (f32[2,8,128]{2,1,0:T(8,128)S(1)}, f32[2,8,128]{2,1,0:T(8,128)S(1)}, u32[]{:S(2)}, u32[]{:S(2)}) collective-permute-start(f32[2,8,128]{2,1,0:T(8,128)S(1)} %get-tuple-element.60), channel_id=1, source_target_pairs={{0,16},{1,17},{2,18},{3,19},{4,20},{5,21},{6,22},{7,23},{8,24},{9,... | collective-permute-start | bytes 24584 | tf_op jit(solution)/shard_map/ppermute | solution.py:52
  83.3 1.3 %collective-permute-done.6.received = f32[2,8,128]{2,1,0:T(8,128)S(1)} collective-permute-done((f32[2,8,128]{2,1,0:T(8,128)S(1)}, f32[2,8,128]{2,1,0:T(8,128)S(1)}, u32[]{:S(2)}, u32[]{:S(2)}) %collective-permute-start.6) | collective-permute-done | bytes 8224 | tf_op jit(solution)/shard_map/ppermute | solution.py:52
  84.6 1.0 %finish.1 = f32[2,256,128]{2,1,0:T(8,128)} custom-call(f32[2,8,128]{2,1,0:T(8,128)S(1)} %collective-permute-done.6.received, f32[2,2,8,128]{3,2,1,0:T(8,128)S(1)} %get-tuple-element.61.pushes, f32[2,2,8,128]{3,2,1,0:T(8,128)S(1)} %get-tuple-element.59.refs_0_.starts, f32[2,2,128,128]{3,2,1,0:T(8,128)S(1)} %copy-done, ...), custom_call_target="tpu_custom_call" | custom-call | bytes 835584 | tf_op jit(solution)/shard_map/finish/pallas_call | solution.py:86
  (26 shorter events, 4.1 us)
Async XLA Ops:
  0.0 0.7 copy-start.5
  0.0 1.0 %copy-start.4 = (f32[2,2,128,128]{3,2,1,0:T(8,128)S(1)}, f32[2,2,128,128]{3,2,1,0:T(8,128)}, u32[]{:S(2)}) copy-start(f32[2,2,128,128]{3,2,1,0:T(8,128)} %fine.1) | copy-start | bytes 786436
  0.0 1.0 %copy-start.6 = (f32[128]{0:T(128)S(1)}, f32[128]{0:T(128)}, u32[]{:S(2)}) copy-start(f32[128]{0:T(128)} %param.8) | copy-start | bytes 1540
  2.1 2.0 %collective-permute-start = (f32[896,128]{1,0:T(8,128)S(1)}, f32[896,128]{1,0:T(8,128)S(1)}, u32[]{:S(2)}, u32[]{:S(2)}) collective-permute-start(f32[896,128]{1,0:T(8,128)S(1)} %get-tuple-element.35), channel_id=1, source_target_pairs={{0,1},{1,0},{2,3},{3,2},{4,5},{5,4},{6,7},{7,6},{8,9},{9,8},{10,11... | collective-permute-start | bytes 1376264 | tf_op jit(solution)/shard_map/ppermute | solution.py:57
  2.7 7.4 %copy-start = (f32[2,2,128,128]{3,2,1,0:T(8,128)S(1)}, f32[2,2,128,128]{3,2,1,0:T(8,128)}, u32[]{:S(2)}) copy-start(f32[2,2,128,128]{3,2,1,0:T(8,128)} %coarse.11) | copy-start | bytes 786436
  2.7 7.4 %copy-start.1 = (f32[2,256,128]{2,1,0:T(8,128)S(1)}, f32[2,256,128]{2,1,0:T(8,128)}, u32[]{:S(2)}) copy-start(f32[2,256,128]{2,1,0:T(8,128)} %refs_2_.3) | copy-start | bytes 786436
  2.7 7.4 %copy-start.3 = (f32[256,128]{1,0:T(8,128)S(1)}, f32[256,128]{1,0:T(8,128)}, u32[]{:S(2)}) copy-start(f32[256,128]{1,0:T(8,128)} %refs_0_.2) | copy-start | bytes 393220
  4.2 0.8 copy-start.2
  4.9 12.8 %all-to-all-start = ((f32[4,224,128]{2,1,0:T(8,128)}), f32[4,224,128]{2,1,0:T(8,128)S(1)}, u32[]{:S(2)}, u32[]{:S(2)}) async-start(f32[4,224,128]{2,1,0:T(8,128)} %bitcast.3), calls=%async_computation | async-start | bytes 917504 | tf_op jit(solution)/shard_map/all_to_all | solution.py:80
  10.7 4.7 %collective-permute-start.1 = (f32[2,8,128]{2,1,0:T(8,128)S(1)}, f32[2,8,128]{2,1,0:T(8,128)S(1)}, u32[]{:S(2)}, u32[]{:S(2)}) collective-permute-start(f32[2,8,128]{2,1,0:T(8,128)S(1)} %get-tuple-element.40), channel_id=1, source_target_pairs={{0,16},{1,17},{2,18},{3,19},{4,20},{5,21},{6,22},{7,23},{8,24},{9,... | collective-permute-start | bytes 24584 | tf_op jit(solution)/shard_map/ppermute | solution.py:52
  17.7 8.4 %collective-permute-start.2 = (f32[240,128]{1,0:T(8,128)S(1)}, f32[240,128]{1,0:T(8,128)S(1)}, u32[]{:S(2)}, u32[]{:S(2)}) collective-permute-start(f32[240,128]{1,0:T(8,128)S(1)} %middle.1.a), channel_id=1, source_target_pairs={{0,8},{1,9},{2,10},{3,11},{4,12},{5,13},{6,14},{7,15},{8,0},{9,1},... | collective-permute-start | bytes 368648 | tf_op jit(solution)/shard_map/ppermute | solution.py:76
  36.2 3.2 %collective-permute-start.3 = (f32[4,240,128]{2,1,0:T(8,128)S(1)}, f32[4,240,128]{2,1,0:T(8,128)S(1)}, u32[]{:S(2)}, u32[]{:S(2)}) collective-permute-start(f32[4,240,128]{2,1,0:T(8,128)S(1)} %all_to_all.25.mine), channel_id=1, source_target_pairs={{0,1},{1,0},{2,3},{3,2},{4,5},{5,4},{6,7},{7,6},{8,9},{9,8},{10,11... | collective-permute-start | bytes 1474568 | tf_op jit(solution)/shard_map/ppermute | solution.py:57
  36.2 18.9 %collective-permute-start.5 = (f32[3,256,128]{2,1,0:T(8,128)S(1)}, f32[3,256,128]{2,1,0:T(8,128)S(1)}, u32[]{:S(2)}, u32[]{:S(2)}) collective-permute-start(f32[3,256,128]{2,1,0:T(8,128)S(1)} %sweep.2), channel_id=1, source_target_pairs={{0,16},{1,17},{2,18},{3,19},{4,20},{5,21},{6,22},{7,23},{8,24},{9,... | collective-permute-start | bytes 1179656 | tf_op jit(solution)/shard_map/ppermute | solution.py:52
  53.3 4.1 %collective-permute-start.4 = (f32[2,8,128]{2,1,0:T(8,128)S(1)}, f32[2,8,128]{2,1,0:T(8,128)S(1)}, u32[]{:S(2)}, u32[]{:S(2)}) collective-permute-start(f32[2,8,128]{2,1,0:T(8,128)S(1)} %get-tuple-element.50), channel_id=1, source_target_pairs={{0,16},{1,17},{2,18},{3,19},{4,20},{5,21},{6,22},{7,23},{8,24},{9,... | collective-permute-start | bytes 24584 | tf_op jit(solution)/shard_map/ppermute | solution.py:52
  80.0 4.6 %collective-permute-start.6 = (f32[2,8,128]{2,1,0:T(8,128)S(1)}, f32[2,8,128]{2,1,0:T(8,128)S(1)}, u32[]{:S(2)}, u32[]{:S(2)}) collective-permute-start(f32[2,8,128]{2,1,0:T(8,128)S(1)} %get-tuple-element.60), channel_id=1, source_target_pairs={{0,16},{1,17},{2,18},{3,19},{4,20},{5,21},{6,22},{7,23},{8,24},{9,... | collective-permute-start | bytes 24584 | tf_op jit(solution)/shard_map/ppermute | solution.py:52

commit v7 on v6

--- a/solution.py
+++ b/solution.py
@@ -47,9 +47,8 @@
 
 
 def from_behind(block, axis, distance):
-    devices = range(lax.axis_size(axis))
-    route = [(i - distance, i) for i in devices if i - distance in devices]
-    return lax.ppermute(block, axis, route)
+    n = lax.axis_size(axis)
+    return lax.ppermute(block, axis, [(i, (i + distance) % n) for i in range(n)])
 
 
 def swap_core(block):
@@ -186,12 +185,12 @@
                 powers[l, g, :, block(i + 1, width)] = stacked(w)
 
 
-def lead_kernel(table, initial, source, coarse, start_sums, source_sums, end):
+def lead_kernel(counts, initial, source, coarse, opened, start_sums, source_sums, end):
     slices, groups, _, _ = coarse.shape
     per = initial.shape[0] // groups
     for g in range(groups):
         here = group_rows(g, per)
-        k = table[g, COUNT_ROW]
+        k = counts[g:g + 1].astype(F32)
         V = class_sums(initial[here], k)
         start_sums[g] = V
         for l in range(slices):
@@ -534,6 +533,14 @@
     averages = shape(slices, ROWS, width)
     mats = shape(half * MATS * width, width)
     opened, = call(opening_kernel, "opening", [shape(ROWS, width)], (), flops=OPENING_FLOPS)
+    sums0, source_sums, moved = call(
+        lead_kernel, "lead", [vector, vectors, vector], (counts, initial, source, coarse, opened)
+    )
+    for turn in range(turns):
+        moved = from_behind(moved, "tm", 1)
+        if turn + 1 < turns:
+            moved, = call(relay_kernel, "relay", [vector], (sums0, moved, source_sums, coarse))
+    fine, sums0 = lax.optimization_barrier((fine, sums0))
     own, other, lows, table = call(
         functools.partial(setup_kernel, everyone), "setup",
         [mats, mats, shape(slices, groups, 4 * width, width), vector],
@@ -544,20 +551,13 @@
         extend_kernel, "extend",
         [shape(slices, groups, 2 * width, (FINE_MAX + 1) * width, dtype=BF16)], (lows, table),
     )
-    swapped, powers = lax.optimization_barrier((swapped, powers))
-    sums0, source_sums, moved = call(
-        lead_kernel, "lead", [vector, vectors, vector], (table, initial, source, coarse)
-    )
-    for turn in range(turns):
-        moved = from_behind(moved, "tm", 1)
-        if turn + 1 < turns:
-            moved, = call(relay_kernel, "relay", [vector], (sums0, moved, source_sums, coarse))
-    mine, = call(add_kernel, "add", [mats], (own, swapped))
-    parts = exchange(mine.reshape(near, shard, width), near_groups())
     base, ofsource = call(
         functools.partial(base_kernel, everyone), "base", [rows8, rows8],
         (sums0, moved, source_sums, coarse, powers, table),
     )
+    swapped, base = lax.optimization_barrier((swapped, base))
+    mine, = call(add_kernel, "add", [mats], (own, swapped))
+    parts = exchange(mine.reshape(near, shard, width), near_groups())
     block, = call(
         middle_kernel, "middle", [shape(shard + slices * ROWS, width)], (parts, base)
     )

time: 86.1 us -> 82.6 us (0.959)
  starting transfers between devices: 20 us -> 10.3 us
  blocking collectives: 41.7 us -> 51.3 us
  waiting for transfers between devices: 8.82 us -> 6.07 us
    all_to_all x4 -> x5, blocking collectives: 41.7 us -> 51.3 us  [exchange(): return lax.all_to_all(block, 'cell', 0, 0, axis_index_groups=groups)]
    all_to_all x1 -> x0, starting transfers between devices: 5.16 us -> none  [exchange(): return lax.all_to_all(block, 'cell', 0, 0, axis_index_groups=groups)]
    ppermute x4, starting transfers between devices: 11.6 us -> 6.99 us  [from_behind(): lax.ppermute(block, axis, [(i, (i + distance) % n) for i in range(n)])]
    all_to_all x1 -> x0, waiting for transfers between devices: 1.55 us -> none  [exchange(): return lax.all_to_all(block, 'cell', 0, 0, axis_index_groups=groups)]
    ppermute x1, waiting for transfers between devices: 3.92 us -> 2.54 us  [far_swap(): return lax.ppermute(block, 'cell', [(i, i ^ distance) for i in range(n)])]
    unnamed x14 -> x12, local copies, waits for them, and re-layouts: 1.74 us -> 1.04 us
  transfers between devices with their start and end apart: 8 -> 7, of which waited for: 5 -> 4; matrix products, arithmetic and copies ran while one was open for 0% -> 0% of each run, Pallas kernels for 10% -> 10%
where the time goes in v7:
time: 82.6 us; the launch traced here: 82.3 us
  blocking collectives  51.3 us (62%)
  Pallas kernels  13.4 us (16%)
  starting transfers between devices  10.3 us (12%)
  waiting for transfers between devices  6.07 us (7%)
  local copies, waits for them, and re-layouts  1.04 us (1%)
    all_to_all x5, blocking collectives, exchange(): return lax.all_to_all(block, 'cell', 0, 0, axis_index_groups=groups)  51.3 us
    pallas_call x16, Pallas kernels, call(): pl.pallas_call(kernel, out_shape=outs, in_specs=[pl.BlockSpec(memory_spac...  13.4 us
    ppermute x4, starting transfers between devices, from_behind(): lax.ppermute(block, axis, [(i, (i + distance) % n) for i in range(n)])  6.99 us
    ppermute x4, waiting for transfers between devices, from_behind(): lax.ppermute(block, axis, [(i, (i + distance) % n) for i in range(n)])  3.15 us
    ppermute x1, starting transfers between devices, far_swap(): return lax.ppermute(block, 'cell', [(i, i ^ distance) for i in range(n)])  2.78 us
    ppermute x1, waiting for transfers between devices, far_swap(): return lax.ppermute(block, 'cell', [(i, i ^ distance) for i in range(n)])  2.54 us
  transfers between devices with their start and end apart: 7, of which 4 were waited for; matrix products, arithmetic and copies ran while one was open for 0% of the time, Pallas kernels for 10%

profile of v7, /device:TPU:0, one launch (start us, length us, event | category | flops | bytes accessed | tf_op | source)
XLA Modules:
  0.0 82.3 jit_solution(5293176910657346911)
XLA Ops:
  0.0 0.9 %copy-done = f32[2,2,128,128]{3,2,1,0:T(8,128)S(1)} copy-done((f32[2,2,128,128]{3,2,1,0:T(8,128)S(1)}, f32[2,2,128,128]{3,2,1,0:T(8,128)}, u32[]{:S(2)}) %copy-start) | copy-done | bytes 262168
  1.7 1.1 %setup.1 = (f32[896,128]{1,0:T(8,128)S(1)}, f32[896,128]{1,0:T(8,128)S(1)}, f32[2,2,512,128]{3,2,1,0:T(8,128)S(1)}, f32[2,8,128]{2,1,0:T(8,128)S(1)}) custom-call(f32[2,2,128,128]{3,2,1,0:T(8,128)S(1)} %copy-done.3, f32[1,128]{1,0:T(1,128)S(1)} %bitcast.6, s32[2,128]{1,0:T(2,128)S(1)} %bitcast.5, f32[8,128]{1,0:T(8,128)S(1)} %opening.1.opened), custom_call_target="tpu_custom_call" | custom-call | bytes 2242048 | tf_op jit(solution)/shard_map/setup/pallas_call | solution.py:85
  3.4 2.5 %collective-permute-start.1 = (f32[2,8,128]{2,1,0:T(8,128)S(1)}, f32[2,8,128]{2,1,0:T(8,128)S(1)}, u32[]{:S(2)}, u32[]{:S(2)}) collective-permute-start(f32[2,8,128]{2,1,0:T(8,128)S(1)} %get-tuple-element.41), channel_id=1, source_target_pairs={{0,16},{16,0},{1,17},{17,1},{2,18},{18,2},{3,19},{19,3},{4,20},{20... | collective-permute-start | bytes 24584 | tf_op jit(solution)/shard_map/ppermute | solution.py:51
  6.0 0.8 extend.1.powers.refs_3_.refs_4_
  6.8 0.8 %collective-permute-done.1.received = f32[2,8,128]{2,1,0:T(8,128)S(1)} collective-permute-done((f32[2,8,128]{2,1,0:T(8,128)S(1)}, f32[2,8,128]{2,1,0:T(8,128)S(1)}, u32[]{:S(2)}, u32[]{:S(2)}) %collective-permute-start.1) | collective-permute-done | bytes 8224 | tf_op jit(solution)/shard_map/ppermute | solution.py:51
  7.6 0.7 base.1
  8.3 11.6 %all_to_all.25.parts = f32[4,224,128]{2,1,0:T(8,128)S(1)} all-to-all(f32[4,224,128]{2,1,0:T(8,128)S(1)} %bitcast.3), channel_id=1, replica_groups={{0,2,4,6},{1,3,5,7},{8,10,12,14},{9,11,13,15},{16,18,20,22},{17,19,21,2..., dimensions={0} | all-to-all | bytes 917504 | tf_op jit(solution)/shard_map/all_to_all | solution.py:79
  19.9 2.8 %collective-permute-start.2 = (f32[240,128]{1,0:T(8,128)S(1)}, f32[240,128]{1,0:T(8,128)S(1)}, u32[]{:S(2)}, u32[]{:S(2)}) collective-permute-start(f32[240,128]{1,0:T(8,128)S(1)} %middle.1.a), channel_id=1, source_target_pairs={{0,8},{1,9},{2,10},{3,11},{4,12},{5,13},{6,14},{7,15},{8,0},{9,1},... | collective-permute-start | bytes 368648 | tf_op jit(solution)/shard_map/ppermute | solution.py:75
  22.7 1.8 %sweep.2 = f32[3,256,128]{2,1,0:T(8,128)S(1)} custom-call(f32[256,128]{1,0:T(8,128)S(1)} %copy-done.2, f32[2,256,128]{2,1,0:T(8,128)S(1)} %copy-done.1, f32[2,2,128,128]{3,2,1,0:T(8,128)S(1)} %copy-done, bf16[2,2,256,1152]{3,2,1,0:T(8,128)(2,1)S(1)} %extend.1.powers.refs_3_.refs_4_, f32[2,8,128]{2,1,0:T(8,128)S(1)} %get-tuple-element.44.table.refs_4_.refs_5_), custom_call_target="tpu_custom_call" | custom-call | bytes 3416064 | tf_op jit(solution)/shard_map/sweep/pallas_call | solution.py:85
  24.6 2.5 %collective-permute-done.2.b = f32[240,128]{1,0:T(8,128)S(1)} collective-permute-done((f32[240,128]{1,0:T(8,128)S(1)}, f32[240,128]{1,0:T(8,128)S(1)}, u32[]{:S(2)}, u32[]{:S(2)}) %collective-permute-start.2) | collective-permute-done | bytes 122912 | tf_op jit(solution)/shard_map/ppermute | solution.py:75
  27.1 9.4 %all_to_all.26.mine = f32[4,240,128]{2,1,0:T(8,128)S(1)} all-to-all(f32[4,240,128]{2,1,0:T(8,128)S(1)} %gather.1), channel_id=1, replica_groups={{0,2,4,6},{1,3,5,7},{8,10,12,14},{9,11,13,15},{16,18,20,22},{17,19,21,2..., dimensions={0} | all-to-all | bytes 983040 | tf_op jit(solution)/shard_map/all_to_all | solution.py:79
  36.6 1.5 %collective-permute-start.5 = (f32[3,256,128]{2,1,0:T(8,128)S(1)}, f32[3,256,128]{2,1,0:T(8,128)S(1)}, u32[]{:S(2)}, u32[]{:S(2)}) collective-permute-start(f32[3,256,128]{2,1,0:T(8,128)S(1)} %sweep.2), channel_id=1, source_target_pairs={{0,16},{16,0},{1,17},{17,1},{2,18},{18,2},{3,19},{19,3},{4,20},{20... | collective-permute-start | bytes 1179656 | tf_op jit(solution)/shard_map/ppermute | solution.py:51
  38.4 1.3 %mixing.1 = (bf16[2,256,896]{2,1,0:T(8,128)(2,1)S(1)}, f32[2,8,128]{2,1,0:T(8,128)S(1)}, f32[16,8,128]{2,1,0:T(8,128)S(1)}) custom-call(f32[4,240,128]{2,1,0:T(8,128)S(1)} %all_to_all.26.mine, f32[4,240,128]{2,1,0:T(8,128)S(1)} %collective-permute-done.3.theirs, f32[16,128]{1,0:T(8,128)S(1)} %get-tuple-element.47.base, ...), custom_call_target="tpu_custom_call" | custom-call | bytes 4349952 | tf_op jit(solution)/shard_map/mixing/pallas_call | solution.py:85
  39.8 10.4 %all_to_all.27.received = f32[16,8,128]{2,1,0:T(8,128)S(1)} all-to-all(f32[16,8,128]{2,1,0:T(8,128)S(1)} %get-tuple-element.51), channel_id=1, replica_groups=mesh['tm'=2,'cell'=16] {'cell'}, dimensions={0} | all-to-all | bytes 131072 | tf_op jit(solution)/shard_map/all_to_all | solution.py:79
  50.1 0.9 %push.2 = (f32[2,2,8,128]{3,2,1,0:T(8,128)S(1)}, f32[2,8,128]{2,1,0:T(8,128)S(1)}) custom-call(f32[16,8,128]{2,1,0:T(8,128)S(1)} %all_to_all.27.received, f32[2,8,128]{2,1,0:T(8,128)S(1)} %get-tuple-element.52.averages, bf16[2,256,896]{2,1,0:T(8,128)(2,1)S(1)} %get-tuple-element.53.mixing, bf16[2,2,256,1152]{3,2,1,0:T(8,128)(2,1)S(1)} %extend.1.powers.refs_3_.refs_4_, ...), custom_call_target="tpu_custom_call" | custom-call | bytes 3645440 | tf_op jit(solution)/shard_map/push/pallas_call | solution.py:85
  51.1 1.6 %collective-permute-start.4 = (f32[2,8,128]{2,1,0:T(8,128)S(1)}, f32[2,8,128]{2,1,0:T(8,128)S(1)}, u32[]{:S(2)}, u32[]{:S(2)}) collective-permute-start(f32[2,8,128]{2,1,0:T(8,128)S(1)} %get-tuple-element.54), channel_id=1, source_target_pairs={{0,16},{16,0},{1,17},{17,1},{2,18},{18,2},{3,19},{19,3},{4,20},{20... | collective-permute-start | bytes 24584 | tf_op jit(solution)/shard_map/ppermute | solution.py:51
  52.6 2.3 %sweep.3 = (f32[2,2,8,128]{3,2,1,0:T(8,128)S(1)}, f32[2,256,128]{2,1,0:T(8,128)S(1)}) custom-call(f32[256,128]{1,0:T(8,128)S(1)} %copy-done.2, f32[3,256,128]{2,1,0:T(8,128)S(1)} %collective-permute-done.5.refs_1_, f32[2,256,128]{2,1,0:T(8,128)S(1)} %copy-done.1, f32[2,2,128,128]{3,2,1,0:T(8,128)S(1)} %copy-done, ...), custom_call_target="tpu_custom_call" | custom-call | bytes 3694592 | tf_op jit(solution)/shard_map/sweep/pallas_call | solution.py:85
  55.4 10.5 %all_to_all.28.received = f32[16,10,128]{2,1,0:T(8,128)S(1)} all-to-all(f32[16,10,128]{2,1,0:T(8,128)S(1)} %get-tuple-element.59), channel_id=1, replica_groups=mesh['tm'=2,'cell'=16] {'cell'}, dimensions={0} | all-to-all | bytes 163840 | tf_op jit(solution)/shard_map/all_to_all | solution.py:79
  65.9 1.2 %first.1 = (f32[2,8,128]{2,1,0:T(8,128)S(1)}, f32[16,8,128]{2,1,0:T(8,128)S(1)}) custom-call(f32[16,10,128]{2,1,0:T(8,128)S(1)} %all_to_all.28.received, f32[16,128]{1,0:T(8,128)S(1)} %get-tuple-element.60.base, bf16[2,256,896]{2,1,0:T(8,128)(2,1)S(1)} %get-tuple-element.53.mixing, bf16[2,2,256,1152]{3,2,1,0:T(8,128)(2,1)S(1)} %extend.1.powers.refs_3_.refs_4_, ...), custom_call_target="tpu_custom_call" | custom-call | bytes 3448832 | tf_op jit(solution)/shard_map/first/pallas_call | solution.py:85
  67.1 9.5 %all_to_all.29.received = f32[16,8,128]{2,1,0:T(8,128)S(1)} all-to-all(f32[16,8,128]{2,1,0:T(8,128)S(1)} %get-tuple-element.61), channel_id=1, replica_groups=mesh['tm'=2,'cell'=16] {'cell'}, dimensions={0} | all-to-all | bytes 131072 | tf_op jit(solution)/shard_map/all_to_all | solution.py:79
  76.6 0.9 %push.3 = (f32[2,2,8,128]{3,2,1,0:T(8,128)S(1)}, f32[2,8,128]{2,1,0:T(8,128)S(1)}) custom-call(f32[16,8,128]{2,1,0:T(8,128)S(1)} %all_to_all.29.received, f32[2,8,128]{2,1,0:T(8,128)S(1)} %get-tuple-element.62.averages, bf16[2,256,896]{2,1,0:T(8,128)(2,1)S(1)} %get-tuple-element.53.mixing, bf16[2,2,256,1152]{3,2,1,0:T(8,128)(2,1)S(1)} %extend.1.powers.refs_3_.refs_4_, ...), custom_call_target="tpu_custom_call" | custom-call | bytes 3661824 | tf_op jit(solution)/shard_map/push/pallas_call | solution.py:85
  77.5 1.4 %collective-permute-start.6 = (f32[2,8,128]{2,1,0:T(8,128)S(1)}, f32[2,8,128]{2,1,0:T(8,128)S(1)}, u32[]{:S(2)}, u32[]{:S(2)}) collective-permute-start(f32[2,8,128]{2,1,0:T(8,128)S(1)} %get-tuple-element.64), channel_id=1, source_target_pairs={{0,16},{16,0},{1,17},{17,1},{2,18},{18,2},{3,19},{19,3},{4,20},{20... | collective-permute-start | bytes 24584 | tf_op jit(solution)/shard_map/ppermute | solution.py:51
  78.9 2.3 %collective-permute-done.6.received = f32[2,8,128]{2,1,0:T(8,128)S(1)} collective-permute-done((f32[2,8,128]{2,1,0:T(8,128)S(1)}, f32[2,8,128]{2,1,0:T(8,128)S(1)}, u32[]{:S(2)}, u32[]{:S(2)}) %collective-permute-start.6) | collective-permute-done | bytes 8224 | tf_op jit(solution)/shard_map/ppermute | solution.py:51
  81.2 1.0 %finish.1 = f32[2,256,128]{2,1,0:T(8,128)} custom-call(f32[2,8,128]{2,1,0:T(8,128)S(1)} %collective-permute-done.6.received, f32[2,2,8,128]{3,2,1,0:T(8,128)S(1)} %get-tuple-element.65.pushes, f32[2,2,8,128]{3,2,1,0:T(8,128)S(1)} %get-tuple-element.63.refs_0_.starts, f32[2,2,128,128]{3,2,1,0:T(8,128)S(1)} %copy-done, ...), custom_call_target="tpu_custom_call" | custom-call | bytes 835584 | tf_op jit(solution)/shard_map/finish/pallas_call | solution.py:85
  (23 shorter events, 2.3 us)
Async XLA Ops:
  0.0 0.9 %copy-start = (f32[2,2,128,128]{3,2,1,0:T(8,128)S(1)}, f32[2,2,128,128]{3,2,1,0:T(8,128)}, u32[]{:S(2)}) copy-start(f32[2,2,128,128]{3,2,1,0:T(8,128)} %coarse.11) | copy-start | bytes 786436
  0.0 1.0 %copy-start.1 = (f32[2,256,128]{2,1,0:T(8,128)S(1)}, f32[2,256,128]{2,1,0:T(8,128)}, u32[]{:S(2)}) copy-start(f32[2,256,128]{2,1,0:T(8,128)} %refs_2_.3) | copy-start | bytes 786436
  0.0 1.1 %copy-start.2 = (f32[256,128]{1,0:T(8,128)S(1)}, f32[256,128]{1,0:T(8,128)}, u32[]{:S(2)}) copy-start(f32[256,128]{1,0:T(8,128)} %refs_0_.2) | copy-start | bytes 393220
  0.0 1.1 %copy-start.4 = (s32[256]{0:T(256)S(1)}, s32[256]{0:T(256)}, u32[]{:S(2)}) copy-start(s32[256]{0:T(256)} %param.11) | copy-start | bytes 3076
  0.0 1.7 %copy-start.3 = (f32[2,2,128,128]{3,2,1,0:T(8,128)S(1)}, f32[2,2,128,128]{3,2,1,0:T(8,128)}, u32[]{:S(2)}) copy-start(f32[2,2,128,128]{3,2,1,0:T(8,128)} %fine) | copy-start | bytes 786436
  0.0 1.7 %copy-start.5 = (f32[128]{0:T(128)S(1)}, f32[128]{0:T(128)}, u32[]{:S(2)}) copy-start(f32[128]{0:T(128)} %param.8) | copy-start | bytes 1540
  2.9 5.4 %collective-permute-start = (f32[896,128]{1,0:T(8,128)S(1)}, f32[896,128]{1,0:T(8,128)S(1)}, u32[]{:S(2)}, u32[]{:S(2)}) collective-permute-start(f32[896,128]{1,0:T(8,128)S(1)} %get-tuple-element.39), channel_id=1, source_target_pairs={{0,1},{1,0},{2,3},{3,2},{4,5},{5,4},{6,7},{7,6},{8,9},{9,8},{10,11... | collective-permute-start | bytes 1376264 | tf_op jit(solution)/shard_map/ppermute | solution.py:56
  3.4 4.2 %collective-permute-start.1 = (f32[2,8,128]{2,1,0:T(8,128)S(1)}, f32[2,8,128]{2,1,0:T(8,128)S(1)}, u32[]{:S(2)}, u32[]{:S(2)}) collective-permute-start(f32[2,8,128]{2,1,0:T(8,128)S(1)} %get-tuple-element.41), channel_id=1, source_target_pairs={{0,16},{16,0},{1,17},{17,1},{2,18},{18,2},{3,19},{19,3},{4,20},{20... | collective-permute-start | bytes 24584 | tf_op jit(solution)/shard_map/ppermute | solution.py:51
  19.9 7.2 %collective-permute-start.2 = (f32[240,128]{1,0:T(8,128)S(1)}, f32[240,128]{1,0:T(8,128)S(1)}, u32[]{:S(2)}, u32[]{:S(2)}) collective-permute-start(f32[240,128]{1,0:T(8,128)S(1)} %middle.1.a), channel_id=1, source_target_pairs={{0,8},{1,9},{2,10},{3,11},{4,12},{5,13},{6,14},{7,15},{8,0},{9,1},... | collective-permute-start | bytes 368648 | tf_op jit(solution)/shard_map/ppermute | solution.py:75
  36.6 1.9 %collective-permute-start.3 = (f32[4,240,128]{2,1,0:T(8,128)S(1)}, f32[4,240,128]{2,1,0:T(8,128)S(1)}, u32[]{:S(2)}, u32[]{:S(2)}) collective-permute-start(f32[4,240,128]{2,1,0:T(8,128)S(1)} %all_to_all.26.mine), channel_id=1, source_target_pairs={{0,1},{1,0},{2,3},{3,2},{4,5},{5,4},{6,7},{7,6},{8,9},{9,8},{10,11... | collective-permute-start | bytes 1474568 | tf_op jit(solution)/shard_map/ppermute | solution.py:56
  36.6 16.0 %collective-permute-start.5 = (f32[3,256,128]{2,1,0:T(8,128)S(1)}, f32[3,256,128]{2,1,0:T(8,128)S(1)}, u32[]{:S(2)}, u32[]{:S(2)}) collective-permute-start(f32[3,256,128]{2,1,0:T(8,128)S(1)} %sweep.2), channel_id=1, source_target_pairs={{0,16},{16,0},{1,17},{17,1},{2,18},{18,2},{3,19},{19,3},{4,20},{20... | collective-permute-start | bytes 1179656 | tf_op jit(solution)/shard_map/ppermute | solution.py:51
  51.1 3.9 %collective-permute-start.4 = (f32[2,8,128]{2,1,0:T(8,128)S(1)}, f32[2,8,128]{2,1,0:T(8,128)S(1)}, u32[]{:S(2)}, u32[]{:S(2)}) collective-permute-start(f32[2,8,128]{2,1,0:T(8,128)S(1)} %get-tuple-element.54), channel_id=1, source_target_pairs={{0,16},{16,0},{1,17},{17,1},{2,18},{18,2},{3,19},{19,3},{4,20},{20... | collective-permute-start | bytes 24584 | tf_op jit(solution)/shard_map/ppermute | solution.py:51
  77.5 3.7 %collective-permute-start.6 = (f32[2,8,128]{2,1,0:T(8,128)S(1)}, f32[2,8,128]{2,1,0:T(8,128)S(1)}, u32[]{:S(2)}, u32[]{:S(2)}) collective-permute-start(f32[2,8,128]{2,1,0:T(8,128)S(1)} %get-tuple-element.64), channel_id=1, source_target_pairs={{0,16},{16,0},{1,17},{17,1},{2,18},{18,2},{3,19},{19,3},{4,20},{20... | collective-permute-start | bytes 24584 | tf_op jit(solution)/shard_map/ppermute | solution.py:51

commit v8 on v7

--- a/solution.py
+++ b/solution.py
@@ -340,7 +340,7 @@
 def first_averages(rows, mixing, rate, width):
     known, sent = [], []
     for m in range(FINE_MIN + 1):
-        a = wide(rows[m:m + 1])
+        a = wide(rows[m])
         for j in range(m):
             a = a + sent[j][:, block(m - j, width)]
         known.append(a)
@@ -352,38 +352,48 @@
 def shifted(products, width):
     out = jnp.zeros((2 * ROWS, width), F32)
     empty = jnp.zeros((ROWS, width), F32)
-    for d in range(1, FINE_MAX + 1):
+    for d in range(1, products.shape[1] // width + 1):
         z = jnp.concatenate([products[:, block(d, width)], empty], axis=0)
         out = out + pltpu.roll(z, d, 0)
     return out
 
 
-def second_rows(everyone, per, a, base, rate, powers, active, l, width):
+def second_rows(everyone, per, a, base, rate, powers, table, partial, l, width):
     groups = powers.shape[1]
     rows = [0.0] * 3
     for g in range(groups):
         h = shifted(mul(a * rate, powers[l, g, :, :FINE_MAX * width]), width)
+        partial[l, g] = h
         total = per * h[4:5]
         for i in range(1, 4):
-            total = total + active[g, i:i + 1] * (h[4 + i:5 + i] - h[3 + i:4 + i])
+            total = total + table[g, i:i + 1] * (h[4 + i:5 + i] - h[3 + i:4 + i])
             rows[i - 1] = rows[i - 1] + total
     at = l * ROWS + FINE_MIN + 1
     return [rows[i] / everyone + base[at + i:at + i + 1] for i in range(3)]
 
 
-def send_rows(everyone, per, a, base, rate, powers, active, out, width):
-    slices = powers.shape[0]
+def send_line(rows, out):
+    line = jnp.concatenate(rows, axis=1)
+    for p in range(out.shape[0]):
+        out[p] = line
+
+
+def received_rows(received, width):
+    total = received[0]
+    for p in range(1, received.shape[0]):
+        total = total + received[p]
+    return [total[:, i:i + width] for i in range(0, total.shape[1], width)]
+
+
+def send_rows(everyone, per, a, base, rate, powers, table, partial, out, width):
     rows = []
-    for l in range(slices):
-        rows += second_rows(everyone, per, a[l], base, rate, powers, active, l, width)
-        rows.append(jnp.zeros((1, width), F32))
-    rows = jnp.concatenate(rows, axis=0)
-    for p in range(out.shape[0]):
-        out[p] = rows
+    for l in range(powers.shape[0]):
+        rows += second_rows(everyone, per, a[l], base, rate, powers, table, partial, l, width)
+    send_line(rows, out)
 
 
 def mixing_kernel(everyone, per, mine, theirs, base, powers, table,
-                  mixing, averages, out, held):
+                  mixing, partial, out, held):
     slices, _, _, wider = powers.shape
     width = wider // (FINE_MAX + 1)
     half = slices // 2
@@ -402,54 +412,46 @@
         for i in range(MATS):
             at = (l * MATS + i) * width
             mixing[l, :, block(i + 1, width)] = stacked(held[at:at + width])
-        a.append(first_averages(mixed[l * ROWS:(l + 1) * ROWS], mixing[l], rate, width))
-        averages[l] = a[-1]
-    send_rows(everyone, per, a, base, rate, powers, table, out, width)
-
-
-def first_kernel(everyone, per, received, base, mixing, powers, table, averages, out):
+        rows = [mixed[l * ROWS + m:l * ROWS + m + 1] for m in range(FINE_MIN + 1)]
+        a.append(first_averages(rows, mixing[l], rate, width))
+    send_rows(everyone, per, a, base, rate, powers, table, partial, out, width)
+
+
+def first_kernel(everyone, per, received, base, mixing, powers, table, partial, out):
     slices, _, _, wider = powers.shape
     width = wider // (FINE_MAX + 1)
     rate = table[0, RATE_ROW]
-    total = received[0]
-    for p in range(1, received.shape[0]):
-        total = total + received[p]
-    a = []
-    for l in range(slices):
-        rows = total[l * (FINE_MIN + 1):(l + 1) * (FINE_MIN + 1)]
-        a.append(first_averages(rows, mixing[l], rate, width))
-        averages[l] = a[-1]
-    send_rows(everyone, per, a, base, rate, powers, table, out, width)
-
-
-def push_kernel(received, averages, mixing, powers, table, coarse, *refs):
+    rows = received_rows(received, width)
+    known = FINE_MIN + 1
+    a = [
+        first_averages(rows[l * known:(l + 1) * known], mixing[l], rate, width)
+        for l in range(slices)
+    ]
+    send_rows(everyone, per, a, base, rate, powers, table, partial, out, width)
+
+
+def push_kernel(received, partial, mixing, powers, table, coarse, *refs):
     starts, (pushes, end) = (None, refs) if len(refs) == 2 else (refs[0], refs[1:])
     slices, groups, _, wider = powers.shape
     width = wider // (FINE_MAX + 1)
     r = table[0, RATE_ROW]
-    total = received[0]
-    for p in range(1, received.shape[0]):
-        total = total + received[p]
+    rows = received_rows(received, width)
     x = [jnp.zeros((ROWS, width), F32) for _ in range(groups)]
     for l in range(slices):
-        a5 = wide(total[l * 4:l * 4 + 1])
+        a5, a6, a7 = (wide(row) for row in rows[3 * l:3 * l + 3])
         z = mul(a5 * r, mixing[l, :, 4 * width:6 * width])
-        a6 = wide(total[l * 4 + 1:l * 4 + 2]) + z[:, :width]
-        a7 = wide(total[l * 4 + 2:l * 4 + 3]) + z[:, width:]
-        a7 = a7 + mul(a6 * r, mixing[l, :, 6 * width:])
-        a = averages[l]
+        a6 = a6 + z[:, :width]
+        a7 = a7 + z[:, width:] + mul(a6 * r, mixing[l, :, 6 * width:])
+        a = jnp.zeros((ROWS, width), F32)
         for m, row in ((5, a5), (6, a6), (7, a7)):
             a = jnp.where(row_is(m, a.shape), row, a)
         for g in range(groups):
-            w = powers[l, g, :, :FINE_MAX * width]
-            if starts is None:
-                h = shifted(mul(a * r, w), width)[FINE_MIN:FINE_MIN + ROWS]
-                old = x[g]
-            else:
-                both = jnp.concatenate([a * r, starts[l, g] * (1.0 - r)], axis=0)
-                z = mul(both, w)
-                h = shifted(z[:ROWS], width)[FINE_MIN:FINE_MIN + ROWS]
-                h = h + picked(z[ROWS:], FINE_MIN, width)
+            z = mul(a * r, powers[l, g, :, :3 * width])
+            h = (partial[l, g] + shifted(z, width))[FINE_MIN:FINE_MIN + ROWS]
+            old = x[g]
+            if starts is not None:
+                w = powers[l, g, :, (FINE_MIN - 1) * width:FINE_MAX * width]
+                h = h + picked(mul(starts[l, g] * (1.0 - r), w), 1, width)
                 old = x[g] - starts[l, g]
             pushes[l, g] = h
             x[g] = h + mul(old, stacked(coarse[l, g]))
@@ -491,10 +493,8 @@
         at = slice(l * ROWS, (l + 1) * ROWS)
         rows = rows / everyone + ofsource[at]
         base[at] = rows
-        sent.append(rows[:FINE_MIN + 1])
-    sent = jnp.concatenate(sent, axis=0)
-    for p in range(out.shape[0]):
-        out[p] = sent
+        sent += [rows[m:m + 1] for m in range(FINE_MIN + 1)]
+    send_line(sent, out)
 
 
 def finish_kernel(received, pushes, starts, coarse, ends, table, out):
@@ -529,8 +529,9 @@
     vectors = shape(slices, groups, ROWS, width)
     vector = shape(groups, ROWS, width)
     rows8 = shape(slices * ROWS, width)
-    rows4 = shape(n_cell, slices * 4, width)
-    averages = shape(slices, ROWS, width)
+    line3 = shape(n_cell, 1, slices * 3 * width)
+    line5 = shape(n_cell, 1, slices * (FINE_MIN + 1) * width)
+    partial = shape(slices, groups, 2 * ROWS, width)
     mats = shape(half * MATS * width, width)
     opened, = call(opening_kernel, "opening", [shape(ROWS, width)], (), flops=OPENING_FLOPS)
     sums0, source_sums, moved = call(
@@ -593,7 +594,7 @@
     theirs = swap_core(gathered)
     mixing, first, out = call(
         functools.partial(mixing_kernel, everyone, per), "mixing",
-        [shape(slices, 2 * width, MATS * width, dtype=BF16), averages, rows4],
+        [shape(slices, 2 * width, MATS * width, dtype=BF16), partial, line3],
         (gathered, theirs, base, powers, table),
         scratch=[pltpu.VMEM((slices * MATS * width, width), F32)],
     )
@@ -609,11 +610,11 @@
             moved, = call(vectors_kernel, "vectors", [vector], (moved, pushes1, nothing, coarse))
     moved1, base, out = call(
         functools.partial(second_kernel, everyone), "second",
-        [vectors, rows8, shape(n_cell, slices * (FINE_MIN + 1), width)],
+        [vectors, rows8, line5],
         (moved, pushes1, coarse, sums, table, powers, ofsource),
     )
     first, out = call(
-        functools.partial(first_kernel, everyone, per), "first", [averages, rows4],
+        functools.partial(first_kernel, everyone, per), "first", [partial, line3],
         (exchange(out), base, mixing, powers, table),
     )
     pushes2, end = call(

time: 82.6 us -> 81.3 us (0.984)
  blocking collectives: 51.3 us -> 50.3 us
    all_to_all x5, blocking collectives: 51.3 us -> 50.3 us  [exchange(): return lax.all_to_all(block, 'cell', 0, 0, axis_index_groups=groups)]
  transfers between devices with their start and end apart: 7 -> 7, of which waited for: 4 -> 4; matrix products, arithmetic and copies ran while one was open for 0% -> 0% of each run, Pallas kernels for 10% -> 9%
where the time goes in v8:
time: 81.3 us; the launch traced here: 81 us
  blocking collectives  50.3 us (62%)
  Pallas kernels  13.2 us (16%)
  starting transfers between devices  10.4 us (13%)
  waiting for transfers between devices  6.06 us (7%)
  local copies, waits for them, and re-layouts  1.04 us (1%)
    all_to_all x5, blocking collectives, exchange(): return lax.all_to_all(block, 'cell', 0, 0, axis_index_groups=groups)  50.3 us
    pallas_call x16, Pallas kernels, call(): pl.pallas_call(kernel, out_shape=outs, in_specs=[pl.BlockSpec(memory_spac...  13.2 us
    ppermute x4, starting transfers between devices, from_behind(): lax.ppermute(block, axis, [(i, (i + distance) % n) for i in range(n)])  7.03 us
    ppermute x4, waiting for transfers between devices, from_behind(): lax.ppermute(block, axis, [(i, (i + distance) % n) for i in range(n)])  3.13 us
    ppermute x1, starting transfers between devices, far_swap(): return lax.ppermute(block, 'cell', [(i, i ^ distance) for i in range(n)])  2.78 us
    ppermute x1, waiting for transfers between devices, far_swap(): return lax.ppermute(block, 'cell', [(i, i ^ distance) for i in range(n)])  2.57 us
  transfers between devices with their start and end apart: 7, of which 4 were waited for; matrix products, arithmetic and copies ran while one was open for 0% of the time, Pallas kernels for 9%

profile of v8, /device:TPU:0, one launch (start us, length us, event | category | flops | bytes accessed | tf_op | source)
XLA Modules:
  0.0 81.0 jit_solution(6969171481437425661)
XLA Ops:
  0.0 0.9 %copy-done = f32[2,2,128,128]{3,2,1,0:T(8,128)S(1)} copy-done((f32[2,2,128,128]{3,2,1,0:T(8,128)S(1)}, f32[2,2,128,128]{3,2,1,0:T(8,128)}, u32[]{:S(2)}) %copy-start) | copy-done | bytes 262168
  1.7 1.1 %setup.1 = (f32[896,128]{1,0:T(8,128)S(1)}, f32[896,128]{1,0:T(8,128)S(1)}, f32[2,2,512,128]{3,2,1,0:T(8,128)S(1)}, f32[2,8,128]{2,1,0:T(8,128)S(1)}) custom-call(f32[2,2,128,128]{3,2,1,0:T(8,128)S(1)} %copy-done.3, f32[1,128]{1,0:T(1,128)S(1)} %bitcast.6, s32[2,128]{1,0:T(2,128)S(1)} %bitcast.5, f32[8,128]{1,0:T(8,128)S(1)} %opening.1.opened), custom_call_target="tpu_custom_call" | custom-call | bytes 2242048 | tf_op jit(solution)/shard_map/setup/pallas_call | solution.py:85
  3.4 2.6 %collective-permute-start.1 = (f32[2,8,128]{2,1,0:T(8,128)S(1)}, f32[2,8,128]{2,1,0:T(8,128)S(1)}, u32[]{:S(2)}, u32[]{:S(2)}) collective-permute-start(f32[2,8,128]{2,1,0:T(8,128)S(1)} %get-tuple-element.41), channel_id=1, source_target_pairs={{0,16},{16,0},{1,17},{17,1},{2,18},{18,2},{3,19},{19,3},{4,20},{20... | collective-permute-start | bytes 24584 | tf_op jit(solution)/shard_map/ppermute | solution.py:51
  6.0 0.8 extend.1.powers.refs_3_.refs_4_
  6.8 0.8 %collective-permute-done.1.received = f32[2,8,128]{2,1,0:T(8,128)S(1)} collective-permute-done((f32[2,8,128]{2,1,0:T(8,128)S(1)}, f32[2,8,128]{2,1,0:T(8,128)S(1)}, u32[]{:S(2)}, u32[]{:S(2)}) %collective-permute-start.1) | collective-permute-done | bytes 8224 | tf_op jit(solution)/shard_map/ppermute | solution.py:51
  7.6 0.7 base.1
  8.3 11.6 %all_to_all.25.parts = f32[4,224,128]{2,1,0:T(8,128)S(1)} all-to-all(f32[4,224,128]{2,1,0:T(8,128)S(1)} %bitcast.3), channel_id=1, replica_groups={{0,2,4,6},{1,3,5,7},{8,10,12,14},{9,11,13,15},{16,18,20,22},{17,19,21,2..., dimensions={0} | all-to-all | bytes 917504 | tf_op jit(solution)/shard_map/all_to_all | solution.py:79
  19.9 2.8 %collective-permute-start.2 = (f32[240,128]{1,0:T(8,128)S(1)}, f32[240,128]{1,0:T(8,128)S(1)}, u32[]{:S(2)}, u32[]{:S(2)}) collective-permute-start(f32[240,128]{1,0:T(8,128)S(1)} %middle.1.a), channel_id=1, source_target_pairs={{0,8},{1,9},{2,10},{3,11},{4,12},{5,13},{6,14},{7,15},{8,0},{9,1},... | collective-permute-start | bytes 368648 | tf_op jit(solution)/shard_map/ppermute | solution.py:75
  22.7 1.8 %sweep.2 = f32[3,256,128]{2,1,0:T(8,128)S(1)} custom-call(f32[256,128]{1,0:T(8,128)S(1)} %copy-done.2, f32[2,256,128]{2,1,0:T(8,128)S(1)} %copy-done.1, f32[2,2,128,128]{3,2,1,0:T(8,128)S(1)} %copy-done, bf16[2,2,256,1152]{3,2,1,0:T(8,128)(2,1)S(1)} %extend.1.powers.refs_3_.refs_4_, f32[2,8,128]{2,1,0:T(8,128)S(1)} %get-tuple-element.44.table.refs_4_.refs_5_), custom_call_target="tpu_custom_call" | custom-call | bytes 3416064 | tf_op jit(solution)/shard_map/sweep/pallas_call | solution.py:85
  24.5 2.6 %collective-permute-done.2.b = f32[240,128]{1,0:T(8,128)S(1)} collective-permute-done((f32[240,128]{1,0:T(8,128)S(1)}, f32[240,128]{1,0:T(8,128)S(1)}, u32[]{:S(2)}, u32[]{:S(2)}) %collective-permute-start.2) | collective-permute-done | bytes 122912 | tf_op jit(solution)/shard_map/ppermute | solution.py:75
  27.1 9.4 %all_to_all.26.mine = f32[4,240,128]{2,1,0:T(8,128)S(1)} all-to-all(f32[4,240,128]{2,1,0:T(8,128)S(1)} %gather.1), channel_id=1, replica_groups={{0,2,4,6},{1,3,5,7},{8,10,12,14},{9,11,13,15},{16,18,20,22},{17,19,21,2..., dimensions={0} | all-to-all | bytes 983040 | tf_op jit(solution)/shard_map/all_to_all | solution.py:79
  36.6 1.5 %collective-permute-start.5 = (f32[3,256,128]{2,1,0:T(8,128)S(1)}, f32[3,256,128]{2,1,0:T(8,128)S(1)}, u32[]{:S(2)}, u32[]{:S(2)}) collective-permute-start(f32[3,256,128]{2,1,0:T(8,128)S(1)} %sweep.2), channel_id=1, source_target_pairs={{0,16},{16,0},{1,17},{17,1},{2,18},{18,2},{3,19},{19,3},{4,20},{20... | collective-permute-start | bytes 1179656 | tf_op jit(solution)/shard_map/ppermute | solution.py:51
  38.4 1.4 %mixing.1 = (bf16[2,256,896]{2,1,0:T(8,128)(2,1)S(1)}, f32[2,2,16,128]{3,2,1,0:T(8,128)S(1)}, f32[16,1,768]{2,1,0:T(1,128)S(1)}) custom-call(f32[4,240,128]{2,1,0:T(8,128)S(1)} %all_to_all.26.mine, f32[4,240,128]{2,1,0:T(8,128)S(1)} %collective-permute-done.3.theirs, f32[16,128]{1,0:T(8,128)S(1)} %get-tuple-element.47.base, ...), custom_call_target="tpu_custom_call" | custom-call | bytes 4358144 | tf_op jit(solution)/shard_map/mixing/pallas_call | solution.py:85
  39.8 10.2 %all_to_all.27.received = f32[16,1,768]{2,1,0:T(1,128)S(1)} all-to-all(f32[16,1,768]{2,1,0:T(1,128)S(1)} %get-tuple-element.51), channel_id=1, replica_groups=mesh['tm'=2,'cell'=16] {'cell'}, dimensions={0} | all-to-all | bytes 98304 | tf_op jit(solution)/shard_map/all_to_all | solution.py:79
  50.0 0.7 push.2
  50.8 1.6 %collective-permute-start.4 = (f32[2,8,128]{2,1,0:T(8,128)S(1)}, f32[2,8,128]{2,1,0:T(8,128)S(1)}, u32[]{:S(2)}, u32[]{:S(2)}) collective-permute-start(f32[2,8,128]{2,1,0:T(8,128)S(1)} %get-tuple-element.54), channel_id=1, source_target_pairs={{0,16},{16,0},{1,17},{17,1},{2,18},{18,2},{3,19},{19,3},{4,20},{20... | collective-permute-start | bytes 24584 | tf_op jit(solution)/shard_map/ppermute | solution.py:51
  52.3 2.3 %sweep.3 = (f32[2,2,8,128]{3,2,1,0:T(8,128)S(1)}, f32[2,256,128]{2,1,0:T(8,128)S(1)}) custom-call(f32[256,128]{1,0:T(8,128)S(1)} %copy-done.2, f32[3,256,128]{2,1,0:T(8,128)S(1)} %collective-permute-done.5.refs_1_, f32[2,256,128]{2,1,0:T(8,128)S(1)} %copy-done.1, f32[2,2,128,128]{3,2,1,0:T(8,128)S(1)} %copy-done, ...), custom_call_target="tpu_custom_call" | custom-call | bytes 3694592 | tf_op jit(solution)/shard_map/sweep/pallas_call | solution.py:85
  55.1 9.7 %all_to_all.28.received = f32[16,1,1280]{2,1,0:T(1,128)S(1)} all-to-all(f32[16,1,1280]{2,1,0:T(1,128)S(1)} %get-tuple-element.59), channel_id=1, replica_groups=mesh['tm'=2,'cell'=16] {'cell'}, dimensions={0} | all-to-all | bytes 163840 | tf_op jit(solution)/shard_map/all_to_all | solution.py:79
  64.8 1.2 %first.1 = (f32[2,2,16,128]{3,2,1,0:T(8,128)S(1)}, f32[16,1,768]{2,1,0:T(1,128)S(1)}) custom-call(f32[16,1,1280]{2,1,0:T(1,128)S(1)} %all_to_all.28.received, f32[16,128]{1,0:T(8,128)S(1)} %get-tuple-element.60.base, bf16[2,256,896]{2,1,0:T(8,128)(2,1)S(1)} %get-tuple-element.53.mixing, bf16[2,2,256,1152]{3,2,1,0:T(8,128)(2,1)S(1)} %extend.1.powers.refs_3_.refs_4_, ...), custom_call_target="tpu_custom_call" | custom-call | bytes 3457024 | tf_op jit(solution)/shard_map/first/pallas_call | solution.py:85
  66.0 9.3 %all_to_all.29.received = f32[16,1,768]{2,1,0:T(1,128)S(1)} all-to-all(f32[16,1,768]{2,1,0:T(1,128)S(1)} %get-tuple-element.61), channel_id=1, replica_groups=mesh['tm'=2,'cell'=16] {'cell'}, dimensions={0} | all-to-all | bytes 98304 | tf_op jit(solution)/shard_map/all_to_all | solution.py:79
  75.3 0.9 %push.3 = (f32[2,2,8,128]{3,2,1,0:T(8,128)S(1)}, f32[2,8,128]{2,1,0:T(8,128)S(1)}) custom-call(f32[16,1,768]{2,1,0:T(1,128)S(1)} %all_to_all.29.received, f32[2,2,16,128]{3,2,1,0:T(8,128)S(1)} %get-tuple-element.62.partial, bf16[2,256,896]{2,1,0:T(8,128)(2,1)S(1)} %get-tuple-element.53.mixing, bf16[2,2,256,1152]{3,2,1,0:T(8,128)(2,1)S(1)} %extend.1.powers.refs_3_.refs_4_, ...), custom_call_target="tpu_custom_call" | custom-call | bytes 3670016 | tf_op jit(solution)/shard_map/push/pallas_call | solution.py:85
  76.3 1.4 %collective-permute-start.6 = (f32[2,8,128]{2,1,0:T(8,128)S(1)}, f32[2,8,128]{2,1,0:T(8,128)S(1)}, u32[]{:S(2)}, u32[]{:S(2)}) collective-permute-start(f32[2,8,128]{2,1,0:T(8,128)S(1)} %get-tuple-element.64), channel_id=1, source_target_pairs={{0,16},{16,0},{1,17},{17,1},{2,18},{18,2},{3,19},{19,3},{4,20},{20... | collective-permute-start | bytes 24584 | tf_op jit(solution)/shard_map/ppermute | solution.py:51
  77.7 2.3 %collective-permute-done.6.received = f32[2,8,128]{2,1,0:T(8,128)S(1)} collective-permute-done((f32[2,8,128]{2,1,0:T(8,128)S(1)}, f32[2,8,128]{2,1,0:T(8,128)S(1)}, u32[]{:S(2)}, u32[]{:S(2)}) %collective-permute-start.6) | collective-permute-done | bytes 8224 | tf_op jit(solution)/shard_map/ppermute | solution.py:51
  80.0 1.0 %finish.1 = f32[2,256,128]{2,1,0:T(8,128)} custom-call(f32[2,8,128]{2,1,0:T(8,128)S(1)} %collective-permute-done.6.received, f32[2,2,8,128]{3,2,1,0:T(8,128)S(1)} %get-tuple-element.65.pushes, f32[2,2,8,128]{3,2,1,0:T(8,128)S(1)} %get-tuple-element.63.refs_0_.starts, f32[2,2,128,128]{3,2,1,0:T(8,128)S(1)} %copy-done, ...), custom_call_target="tpu_custom_call" | custom-call | bytes 835584 | tf_op jit(solution)/shard_map/finish/pallas_call | solution.py:85
  (23 shorter events, 2.3 us)
Async XLA Ops:
  0.0 0.9 %copy-start = (f32[2,2,128,128]{3,2,1,0:T(8,128)S(1)}, f32[2,2,128,128]{3,2,1,0:T(8,128)}, u32[]{:S(2)}) copy-start(f32[2,2,128,128]{3,2,1,0:T(8,128)} %coarse.11) | copy-start | bytes 786436
  0.0 1.0 %copy-start.1 = (f32[2,256,128]{2,1,0:T(8,128)S(1)}, f32[2,256,128]{2,1,0:T(8,128)}, u32[]{:S(2)}) copy-start(f32[2,256,128]{2,1,0:T(8,128)} %refs_2_.3) | copy-start | bytes 786436
  0.0 1.1 %copy-start.2 = (f32[256,128]{1,0:T(8,128)S(1)}, f32[256,128]{1,0:T(8,128)}, u32[]{:S(2)}) copy-start(f32[256,128]{1,0:T(8,128)} %refs_0_.2) | copy-start | bytes 393220
  0.0 1.1 %copy-start.4 = (s32[256]{0:T(256)S(1)}, s32[256]{0:T(256)}, u32[]{:S(2)}) copy-start(s32[256]{0:T(256)} %param.11) | copy-start | bytes 3076
  0.0 1.7 %copy-start.3 = (f32[2,2,128,128]{3,2,1,0:T(8,128)S(1)}, f32[2,2,128,128]{3,2,1,0:T(8,128)}, u32[]{:S(2)}) copy-start(f32[2,2,128,128]{3,2,1,0:T(8,128)} %fine) | copy-start | bytes 786436
  0.0 1.7 %copy-start.5 = (f32[128]{0:T(128)S(1)}, f32[128]{0:T(128)}, u32[]{:S(2)}) copy-start(f32[128]{0:T(128)} %param.8) | copy-start | bytes 1540
  2.9 5.4 %collective-permute-start = (f32[896,128]{1,0:T(8,128)S(1)}, f32[896,128]{1,0:T(8,128)S(1)}, u32[]{:S(2)}, u32[]{:S(2)}) collective-permute-start(f32[896,128]{1,0:T(8,128)S(1)} %get-tuple-element.39), channel_id=1, source_target_pairs={{0,1},{1,0},{2,3},{3,2},{4,5},{5,4},{6,7},{7,6},{8,9},{9,8},{10,11... | collective-permute-start | bytes 1376264 | tf_op jit(solution)/shard_map/ppermute | solution.py:56
  3.4 4.2 %collective-permute-start.1 = (f32[2,8,128]{2,1,0:T(8,128)S(1)}, f32[2,8,128]{2,1,0:T(8,128)S(1)}, u32[]{:S(2)}, u32[]{:S(2)}) collective-permute-start(f32[2,8,128]{2,1,0:T(8,128)S(1)} %get-tuple-element.41), channel_id=1, source_target_pairs={{0,16},{16,0},{1,17},{17,1},{2,18},{18,2},{3,19},{19,3},{4,20},{20... | collective-permute-start | bytes 24584 | tf_op jit(solution)/shard_map/ppermute | solution.py:51
  19.9 7.2 %collective-permute-start.2 = (f32[240,128]{1,0:T(8,128)S(1)}, f32[240,128]{1,0:T(8,128)S(1)}, u32[]{:S(2)}, u32[]{:S(2)}) collective-permute-start(f32[240,128]{1,0:T(8,128)S(1)} %middle.1.a), channel_id=1, source_target_pairs={{0,8},{1,9},{2,10},{3,11},{4,12},{5,13},{6,14},{7,15},{8,0},{9,1},... | collective-permute-start | bytes 368648 | tf_op jit(solution)/shard_map/ppermute | solution.py:75
  36.6 1.9 %collective-permute-start.3 = (f32[4,240,128]{2,1,0:T(8,128)S(1)}, f32[4,240,128]{2,1,0:T(8,128)S(1)}, u32[]{:S(2)}, u32[]{:S(2)}) collective-permute-start(f32[4,240,128]{2,1,0:T(8,128)S(1)} %all_to_all.26.mine), channel_id=1, source_target_pairs={{0,1},{1,0},{2,3},{3,2},{4,5},{5,4},{6,7},{7,6},{8,9},{9,8},{10,11... | collective-permute-start | bytes 1474568 | tf_op jit(solution)/shard_map/ppermute | solution.py:56
  36.6 15.7 %collective-permute-start.5 = (f32[3,256,128]{2,1,0:T(8,128)S(1)}, f32[3,256,128]{2,1,0:T(8,128)S(1)}, u32[]{:S(2)}, u32[]{:S(2)}) collective-permute-start(f32[3,256,128]{2,1,0:T(8,128)S(1)} %sweep.2), channel_id=1, source_target_pairs={{0,16},{16,0},{1,17},{17,1},{2,18},{18,2},{3,19},{19,3},{4,20},{20... | collective-permute-start | bytes 1179656 | tf_op jit(solution)/shard_map/ppermute | solution.py:51
  50.8 3.8 %collective-permute-start.4 = (f32[2,8,128]{2,1,0:T(8,128)S(1)}, f32[2,8,128]{2,1,0:T(8,128)S(1)}, u32[]{:S(2)}, u32[]{:S(2)}) collective-permute-start(f32[2,8,128]{2,1,0:T(8,128)S(1)} %get-tuple-element.54), channel_id=1, source_target_pairs={{0,16},{16,0},{1,17},{17,1},{2,18},{18,2},{3,19},{19,3},{4,20},{20... | collective-permute-start | bytes 24584 | tf_op jit(solution)/shard_map/ppermute | solution.py:51
  76.3 3.7 %collective-permute-start.6 = (f32[2,8,128]{2,1,0:T(8,128)S(1)}, f32[2,8,128]{2,1,0:T(8,128)S(1)}, u32[]{:S(2)}, u32[]{:S(2)}) collective-permute-start(f32[2,8,128]{2,1,0:T(8,128)S(1)} %get-tuple-element.64), channel_id=1, source_target_pairs={{0,16},{16,0},{1,17},{17,1},{2,18},{18,2},{3,19},{19,3},{4,20},{20... | collective-permute-start | bytes 24584 | tf_op jit(solution)/shard_map/ppermute | solution.py:51

commit v9 on v8

--- a/solution.py
+++ b/solution.py
@@ -124,7 +124,8 @@
     out[...] = jnp.zeros_like(out)
 
 
-def setup_kernel(everyone, fine, rate, counts, opened, own, other, lows, table):
+def setup_kernel(everyone, fine, rate, counts, initial, source, coarse, opened,
+                 own, other, lows, table, start_sums, source_sums, end):
     slices, groups, width, _ = fine.shape
     per = counts.shape[1]
     half = slices // 2
@@ -143,6 +144,17 @@
             if n is not None:
                 filled = jnp.where(row_is(i, filled.shape), n, filled)
         table[g] = filled
+    for g in range(groups):
+        here = group_rows(g, per)
+        k = counts[g:g + 1].astype(F32)
+        V = class_sums(initial[here], k)
+        start_sums[g] = V
+        for l in range(slices):
+            S = class_sums(source[l, here], k)
+            source_sums[l, g] = S
+            V = mul(V + S, stacked(coarse[l, g]))
+        end[g] = V
+    made = []
     for l in range(slices):
         sums = [0.0] * 4
         e6, e7, e72 = 0.0, 0.0, 0.0
@@ -160,19 +172,13 @@
             e72 = e72 + alive[g][3] * w2
         mats = [t * (per / everyone) for t in sums]
         mats += [e6 / everyone, (e6 + e72 - e7) / everyone, e7 / everyone]
-        for i, m in enumerate(mats):
-            at = slice(((l % half) * MATS + i) * width, ((l % half) * MATS + i + 1) * width)
-
-            @pl.when(core == l // half)
-            def _():
-                own[at] = m
-
-            @pl.when(core != l // half)
-            def _():
-                other[at] = m
-
-
-def extend_kernel(lows, table, powers):
+        made.append(jnp.concatenate(mats, axis=0))
+    first = core == 0
+    own[...] = jnp.where(first, jnp.concatenate(made[:half]), jnp.concatenate(made[half:]))
+    other[...] = jnp.where(first, jnp.concatenate(made[half:]), jnp.concatenate(made[:half]))
+
+
+def extend_kernel(everyone, lows, table, source_sums, powers, ofsource):
     slices, groups, _, width = lows.shape
     keep = 1.0 - table[0, RATE_ROW]
     for l in range(slices):
@@ -183,21 +189,12 @@
             ws.append((ws[0] + ws[1]) + (ws[2] + ws[3]))
             for i, w in enumerate(ws):
                 powers[l, g, :, block(i + 1, width)] = stacked(w)
-
-
-def lead_kernel(counts, initial, source, coarse, opened, start_sums, source_sums, end):
-    slices, groups, _, _ = coarse.shape
-    per = initial.shape[0] // groups
-    for g in range(groups):
-        here = group_rows(g, per)
-        k = counts[g:g + 1].astype(F32)
-        V = class_sums(initial[here], k)
-        start_sums[g] = V
-        for l in range(slices):
-            S = class_sums(source[l, here], k)
-            source_sums[l, g] = S
-            V = mul(V + S, stacked(coarse[l, g]))
-        end[g] = V
+    for l in range(slices):
+        rows = 0.0
+        for g in range(groups):
+            w = powers[l, g, :, :FINE_MAX * width]
+            rows = rows + sums_of_source(source_sums[l, g], w, width)
+        ofsource[l * ROWS:(l + 1) * ROWS] = rows / everyone
 
 
 def add_kernel(a, b, out):
@@ -247,22 +244,19 @@
     return out
 
 
-def base_kernel(everyone, sums, received, source_sums, coarse, powers, table, base, ofsource):
+def base_kernel(everyone, sums, received, source_sums, coarse, powers, table, ofsource, base):
     slices, groups, width, _ = coarse.shape
     keep = 1.0 - table[0, RATE_ROW]
     states = [jnp.where(leading(), sums[g], received[g]) for g in range(groups)]
     for l in range(slices):
-        rows, rows_source = 0.0, 0.0
-        for g in range(groups):
-            V, S, w = states[g], source_sums[l, g], powers[l, g, :, :FINE_MAX * width]
-            rows = rows + sums_of_state(V, keep, w, width)
-            rows_source = rows_source + sums_of_source(S, w, width)
+        rows = 0.0
+        for g in range(groups):
+            V = states[g]
+            rows = rows + sums_of_state(V, keep, powers[l, g, :, :FINE_MAX * width], width)
             if l + 1 < slices:
-                states[g] = mul(V + S, stacked(coarse[l, g]))
-        rows_source = rows_source / everyone
+                states[g] = mul(V + source_sums[l, g], stacked(coarse[l, g]))
         at = slice(l * ROWS, (l + 1) * ROWS)
-        ofsource[at] = rows_source
-        base[at] = rows / everyone + rows_source
+        base[at] = rows / everyone + ofsource[at]
 
 
 def sweep_kernel(first, last, *refs):
@@ -273,15 +267,19 @@
     slices, groups, width, _ = coarse.shape
     per = initial.shape[0] // groups
     keep = 1.0 - table[0, RATE_ROW]
+    counts = [spread_counts(table[g, COUNT_ROW]) for g in range(groups)]
+    held = []
     for g in range(groups):
         here = group_rows(g, per)
-        n = spread_counts(table[g, COUNT_ROW])
         start = initial[here]
         states = [start] * 3
         if not first:
             states = [jnp.where(leading(), start, received[i, here]) for i in range(3)]
-        for l in range(slices):
-            s = source[l, here]
+        held.append(states)
+    for l in range(slices):
+        for g in range(groups):
+            here = group_rows(g, per)
+            states, n, s = held[g], counts[g], source[l, here]
             if last:
                 outs[0][l, g] = class_sums(states[1], table[g, COUNT_ROW])
             w = powers[l, g, :, FINE_MIN * width:]
@@ -299,16 +297,17 @@
                 ),
                 stacked(coarse[l, g]),
             )
-            states = [
+            held[g] = [
                 moved[:per],
                 sourced + by_count(x[:per], n, FINE_MIN, width) + moved[per:2 * per],
                 sourced + by_count(x[per:], n, FINE_MIN, width) + moved[2 * per:],
             ]
             if last:
-                outs[1][l, here] = states[2]
-        if not last:
+                outs[1][l, here] = held[g][2]
+    if not last:
+        for g in range(groups):
             for i in range(3):
-                outs[0][i, here] = states[i]
+                outs[0][i, group_rows(g, per)] = held[g][i]
 
 
 def middle_kernel(parts, base, out):
@@ -338,15 +337,18 @@
 
 
 def first_averages(rows, mixing, rate, width):
-    known, sent = [], []
+    slices = len(rows)
+    known = [[] for _ in range(slices)]
+    sent = [[] for _ in range(slices)]
     for m in range(FINE_MIN + 1):
-        a = wide(rows[m])
-        for j in range(m):
-            a = a + sent[j][:, block(m - j, width)]
-        known.append(a)
-        if m < FINE_MIN:
-            sent.append(mul(a * rate, mixing[:, :(FINE_MIN - m) * width]))
-    return assembled(known, width)
+        for l in range(slices):
+            a = wide(rows[l][m])
+            for j in range(m):
+                a = a + sent[l][j][:, block(m - j, width)]
+            known[l].append(a)
+            if m < FINE_MIN:
+                sent[l].append(mul(a * rate, mixing[l, :, :(FINE_MIN - m) * width]))
+    return [assembled(a, width) for a in known]
 
 
 def shifted(products, width):
@@ -407,13 +409,21 @@
             place = at * (half * MATS * width) + p * rows
             held[pl.ds(place, rows), :] = ref[p, :rows]
             mixed = mixed + ref[p, rows:]
-    a = []
-    for l in range(slices):
-        for i in range(MATS):
-            at = (l * MATS + i) * width
-            mixing[l, :, block(i + 1, width)] = stacked(held[at:at + width])
-        rows = [mixed[l * ROWS + m:l * ROWS + m + 1] for m in range(FINE_MIN + 1)]
-        a.append(first_averages(rows, mixing[l], rate, width))
+    def place(l, i):
+        at = (l * MATS + i) * width
+        mixing[l, :, block(i + 1, width)] = stacked(held[at:at + width])
+
+    for l in range(slices):
+        for i in range(FINE_MIN):
+            place(l, i)
+    rows = [
+        [mixed[l * ROWS + m:l * ROWS + m + 1] for m in range(FINE_MIN + 1)]
+        for l in range(slices)
+    ]
+    a = first_averages(rows, mixing, rate, width)
+    for l in range(slices):
+        for i in range(FINE_MIN, MATS):
+            place(l, i)
     send_rows(everyone, per, a, base, rate, powers, table, partial, out, width)
 
 
@@ -423,10 +433,8 @@
     rate = table[0, RATE_ROW]
     rows = received_rows(received, width)
     known = FINE_MIN + 1
-    a = [
-        first_averages(rows[l * known:(l + 1) * known], mixing[l], rate, width)
-        for l in range(slices)
-    ]
+    rows = [rows[l * known:(l + 1) * known] for l in range(slices)]
+    a = first_averages(rows, mixing, rate, width)
     send_rows(everyone, per, a, base, rate, powers, table, partial, out, width)
 
 
@@ -436,25 +444,28 @@
     width = wider // (FINE_MAX + 1)
     r = table[0, RATE_ROW]
     rows = received_rows(received, width)
-    x = [jnp.zeros((ROWS, width), F32) for _ in range(groups)]
-    for l in range(slices):
-        a5, a6, a7 = (wide(row) for row in rows[3 * l:3 * l + 3])
-        z = mul(a5 * r, mixing[l, :, 4 * width:6 * width])
-        a6 = a6 + z[:, :width]
-        a7 = a7 + z[:, width:] + mul(a6 * r, mixing[l, :, 6 * width:])
+    fives = [wide(rows[3 * l]) for l in range(slices)]
+    fed = [mul(fives[l] * r, mixing[l, :, 4 * width:6 * width]) for l in range(slices)]
+    sixes = [wide(rows[3 * l + 1]) + fed[l][:, :width] for l in range(slices)]
+    late = [mul(sixes[l] * r, mixing[l, :, 6 * width:]) for l in range(slices)]
+    h = [[None] * groups for _ in range(slices)]
+    for l in range(slices):
         a = jnp.zeros((ROWS, width), F32)
-        for m, row in ((5, a5), (6, a6), (7, a7)):
+        seven = wide(rows[3 * l + 2]) + fed[l][:, width:] + late[l]
+        for m, row in ((5, fives[l]), (6, sixes[l]), (7, seven)):
             a = jnp.where(row_is(m, a.shape), row, a)
         for g in range(groups):
             z = mul(a * r, powers[l, g, :, :3 * width])
-            h = (partial[l, g] + shifted(z, width))[FINE_MIN:FINE_MIN + ROWS]
-            old = x[g]
+            h[l][g] = (partial[l, g] + shifted(z, width))[FINE_MIN:FINE_MIN + ROWS]
             if starts is not None:
                 w = powers[l, g, :, (FINE_MIN - 1) * width:FINE_MAX * width]
-                h = h + picked(mul(starts[l, g] * (1.0 - r), w), 1, width)
-                old = x[g] - starts[l, g]
-            pushes[l, g] = h
-            x[g] = h + mul(old, stacked(coarse[l, g]))
+                h[l][g] = h[l][g] + picked(mul(starts[l, g] * (1.0 - r), w), 1, width)
+    x = [jnp.zeros((ROWS, width), F32) for _ in range(groups)]
+    for l in range(slices):
+        for g in range(groups):
+            old = x[g] if starts is None else x[g] - starts[l, g]
+            x[g] = h[l][g] + mul(old, stacked(coarse[l, g]))
+            pushes[l, g] = h[l][g]
     for g in range(groups):
         end[g] = x[g]
 
@@ -500,15 +511,15 @@
 def finish_kernel(received, pushes, starts, coarse, ends, table, out):
     slices, groups, width, _ = coarse.shape
     per = ends.shape[1] // groups
-    for g in range(groups):
-        here = group_rows(g, per)
-        n = spread_counts(table[g, COUNT_ROW])
-        x = jnp.where(leading(), 0.0, received[g])
-        for l in range(slices):
-            x = pushes[l, g] + mul(x - starts[l, g], stacked(coarse[l, g]))
+    counts = [spread_counts(table[g, COUNT_ROW]) for g in range(groups)]
+    x = [jnp.where(leading(), 0.0, received[g]) for g in range(groups)]
+    for l in range(slices):
+        for g in range(groups):
+            here = group_rows(g, per)
+            x[g] = pushes[l, g] + mul(x[g] - starts[l, g], stacked(coarse[l, g]))
             add = jnp.zeros((per, width), F32)
             for i in range(CLASSES):
-                add = jnp.where(n == float(FINE_MIN + i), x[i:i + 1], add)
+                add = jnp.where(counts[g] == float(FINE_MIN + i), x[g][i:i + 1], add)
             out[l, here] = ends[l, here] + add
 
 
@@ -534,27 +545,24 @@
     partial = shape(slices, groups, 2 * ROWS, width)
     mats = shape(half * MATS * width, width)
     opened, = call(opening_kernel, "opening", [shape(ROWS, width)], (), flops=OPENING_FLOPS)
-    sums0, source_sums, moved = call(
-        lead_kernel, "lead", [vector, vectors, vector], (counts, initial, source, coarse, opened)
+    own, other, lows, table, sums0, source_sums, moved = call(
+        functools.partial(setup_kernel, everyone), "setup",
+        [mats, mats, shape(slices, groups, 4 * width, width), vector, vector, vectors, vector],
+        (fine, rate, counts, initial, source, coarse, opened),
     )
     for turn in range(turns):
         moved = from_behind(moved, "tm", 1)
         if turn + 1 < turns:
             moved, = call(relay_kernel, "relay", [vector], (sums0, moved, source_sums, coarse))
-    fine, sums0 = lax.optimization_barrier((fine, sums0))
-    own, other, lows, table = call(
-        functools.partial(setup_kernel, everyone), "setup",
-        [mats, mats, shape(slices, groups, 4 * width, width), vector],
-        (fine, rate, counts, opened),
-    )
     swapped = swap_core(other)
-    powers, = call(
-        extend_kernel, "extend",
-        [shape(slices, groups, 2 * width, (FINE_MAX + 1) * width, dtype=BF16)], (lows, table),
-    )
-    base, ofsource = call(
-        functools.partial(base_kernel, everyone), "base", [rows8, rows8],
-        (sums0, moved, source_sums, coarse, powers, table),
+    powers, ofsource = call(
+        functools.partial(extend_kernel, everyone), "extend",
+        [shape(slices, groups, 2 * width, (FINE_MAX + 1) * width, dtype=BF16), rows8],
+        (lows, table, source_sums),
+    )
+    base, = call(
+        functools.partial(base_kernel, everyone), "base", [rows8],
+        (sums0, moved, source_sums, coarse, powers, table, ofsource),
     )
     swapped, base = lax.optimization_barrier((swapped, base))
     mine, = call(add_kernel, "add", [mats], (own, swapped))

time: 81.3 us -> 79.7 us (0.980)
  Pallas kernels: 13.2 us -> 11.5 us
    pallas_call x16 -> x15, Pallas kernels: 13.2 us -> 11.5 us  [call(): pl.pallas_call(kernel, out_shape=outs, in_specs=[pl.BlockSpec(memory_spac...]
  transfers between devices with their start and end apart: 7 -> 7, of which waited for: 4 -> 5; matrix products, arithmetic and copies ran while one was open for 0% -> 0% of each run, Pallas kernels for 9% -> 9%
where the time goes in v9:
time: 79.7 us; the launch traced here: 79.4 us
  blocking collectives  50.3 us (63%)
  Pallas kernels  11.5 us (14%)
  starting transfers between devices  10.5 us (13%)
  waiting for transfers between devices  5.94 us (7%)
  local copies, waits for them, and re-layouts  1.14 us (1%)
    all_to_all x5, blocking collectives, exchange(): return lax.all_to_all(block, 'cell', 0, 0, axis_index_groups=groups)  50.3 us
    pallas_call x15, Pallas kernels, call(): pl.pallas_call(kernel, out_shape=outs, in_specs=[pl.BlockSpec(memory_spac...  11.5 us
    ppermute x4, starting transfers between devices, from_behind(): lax.ppermute(block, axis, [(i, (i + distance) % n) for i in range(n)])  7.14 us
    ppermute x4, waiting for transfers between devices, from_behind(): lax.ppermute(block, axis, [(i, (i + distance) % n) for i in range(n)])  2.99 us
    ppermute x1, starting transfers between devices, far_swap(): return lax.ppermute(block, 'cell', [(i, i ^ distance) for i in range(n)])  2.77 us
    ppermute x1, waiting for transfers between devices, far_swap(): return lax.ppermute(block, 'cell', [(i, i ^ distance) for i in range(n)])  2.57 us
  transfers between devices with their start and end apart: 7, of which 5 were waited for; matrix products, arithmetic and copies ran while one was open for 0% of the time, Pallas kernels for 9%

profile of v9, /device:TPU:0, one launch (start us, length us, event | category | flops | bytes accessed | tf_op | source)
XLA Modules:
  0.0 79.4 jit_solution(11529138307476772453)
XLA Ops:
  0.0 0.9 %copy-done = f32[2,2,128,128]{3,2,1,0:T(8,128)S(1)} copy-done((f32[2,2,128,128]{3,2,1,0:T(8,128)S(1)}, f32[2,2,128,128]{3,2,1,0:T(8,128)}, u32[]{:S(2)}) %copy-start) | copy-done | bytes 262168
  1.2 1.4 %setup.1 = (f32[896,128]{1,0:T(8,128)S(1)}, f32[896,128]{1,0:T(8,128)S(1)}, f32[2,2,512,128]{3,2,1,0:T(8,128)S(1)}, f32[2,8,128]{2,1,0:T(8,128)S(1)}, f32[2,8,12...) custom-call(f32[2,2,128,128]{3,2,1,0:T(8,128)S(1)} %copy-done.3, f32[1,128]{1,0:T(1,128)S(1)} %bitcast.5, ...), custom_call_target="tpu_custom_call" | custom-call | bytes 2930176 | tf_op jit(solution)/shard_map/setup/pallas_call | solution.py:85
  2.5 0.6 collective-permute-start
  3.1 2.6 %collective-permute-start.1 = (f32[2,8,128]{2,1,0:T(8,128)S(1)}, f32[2,8,128]{2,1,0:T(8,128)S(1)}, u32[]{:S(2)}, u32[]{:S(2)}) collective-permute-start(f32[2,8,128]{2,1,0:T(8,128)S(1)} %get-tuple-element.37), channel_id=1, source_target_pairs={{0,16},{16,0},{1,17},{17,1},{2,18},{18,2},{3,19},{19,3},{4,20},{20... | collective-permute-start | bytes 24584 | tf_op jit(solution)/shard_map/ppermute | solution.py:51
  5.6 1.0 %extend.1 = (bf16[2,2,256,1152]{3,2,1,0:T(8,128)(2,1)S(1)}, f32[16,128]{1,0:T(8,128)S(1)}) custom-call(f32[2,2,512,128]{3,2,1,0:T(8,128)S(1)} %get-tuple-element.39.lows, f32[2,8,128]{2,1,0:T(8,128)S(1)} %get-tuple-element.40.table.refs_4_.refs_5_, f32[2,2,8,128]{3,2,1,0:T(8,128)S(1)} %get-tuple-element.38.source_sums), custom_call_target="tpu_custom_call" | custom-call | bytes 3440640 | tf_op jit(solution)/shard_map/extend/pallas_call | solution.py:85
  6.7 0.6 collective-permute-done.1.received
  7.8 11.6 %all_to_all.25.parts = f32[4,224,128]{2,1,0:T(8,128)S(1)} all-to-all(f32[4,224,128]{2,1,0:T(8,128)S(1)} %bitcast.3), channel_id=1, replica_groups={{0,2,4,6},{1,3,5,7},{8,10,12,14},{9,11,13,15},{16,18,20,22},{17,19,21,2..., dimensions={0} | all-to-all | bytes 917504 | tf_op jit(solution)/shard_map/all_to_all | solution.py:79
  19.4 2.8 %collective-permute-start.2 = (f32[240,128]{1,0:T(8,128)S(1)}, f32[240,128]{1,0:T(8,128)S(1)}, u32[]{:S(2)}, u32[]{:S(2)}) collective-permute-start(f32[240,128]{1,0:T(8,128)S(1)} %middle.1.a), channel_id=1, source_target_pairs={{0,8},{1,9},{2,10},{3,11},{4,12},{5,13},{6,14},{7,15},{8,0},{9,1},... | collective-permute-start | bytes 368648 | tf_op jit(solution)/shard_map/ppermute | solution.py:75
  22.1 1.8 %sweep.2 = f32[3,256,128]{2,1,0:T(8,128)S(1)} custom-call(f32[256,128]{1,0:T(8,128)S(1)} %copy-done.2, f32[2,256,128]{2,1,0:T(8,128)S(1)} %copy-done.1, f32[2,2,128,128]{3,2,1,0:T(8,128)S(1)} %copy-done, bf16[2,2,256,1152]{3,2,1,0:T(8,128)(2,1)S(1)} %get-tuple-element.41.powers.refs_3_.refs_4_, f32[2,8,128]{2,1,0:T(8,128)S(1)} %get-tuple-element.40.table.refs_4_.refs_5_), custom_call_target="tpu_custom_call" | custom-call | bytes 3416064 | tf_op jit(solution)/shard_map/sweep/pallas_call | solution.py:85
  24.0 2.6 %collective-permute-done.2.b = f32[240,128]{1,0:T(8,128)S(1)} collective-permute-done((f32[240,128]{1,0:T(8,128)S(1)}, f32[240,128]{1,0:T(8,128)S(1)}, u32[]{:S(2)}, u32[]{:S(2)}) %collective-permute-start.2) | collective-permute-done | bytes 122912 | tf_op jit(solution)/shard_map/ppermute | solution.py:75
  26.6 9.4 %all_to_all.26.mine = f32[4,240,128]{2,1,0:T(8,128)S(1)} all-to-all(f32[4,240,128]{2,1,0:T(8,128)S(1)} %gather.1), channel_id=1, replica_groups={{0,2,4,6},{1,3,5,7},{8,10,12,14},{9,11,13,15},{16,18,20,22},{17,19,21,2..., dimensions={0} | all-to-all | bytes 983040 | tf_op jit(solution)/shard_map/all_to_all | solution.py:79
  36.0 1.5 %collective-permute-start.5 = (f32[3,256,128]{2,1,0:T(8,128)S(1)}, f32[3,256,128]{2,1,0:T(8,128)S(1)}, u32[]{:S(2)}, u32[]{:S(2)}) collective-permute-start(f32[3,256,128]{2,1,0:T(8,128)S(1)} %sweep.2), channel_id=1, source_target_pairs={{0,16},{16,0},{1,17},{17,1},{2,18},{18,2},{3,19},{19,3},{4,20},{20... | collective-permute-start | bytes 1179656 | tf_op jit(solution)/shard_map/ppermute | solution.py:51
  37.9 1.0 %mixing.1 = (bf16[2,256,896]{2,1,0:T(8,128)(2,1)S(1)}, f32[2,2,16,128]{3,2,1,0:T(8,128)S(1)}, f32[16,1,768]{2,1,0:T(1,128)S(1)}) custom-call(f32[4,240,128]{2,1,0:T(8,128)S(1)} %all_to_all.26.mine, f32[4,240,128]{2,1,0:T(8,128)S(1)} %collective-permute-done.3.theirs, f32[16,128]{1,0:T(8,128)S(1)} %base.1, ...), custom_call_target="tpu_custom_call" | custom-call | bytes 4358144 | tf_op jit(solution)/shard_map/mixing/pallas_call | solution.py:85
  38.9 10.2 %all_to_all.27.received = f32[16,1,768]{2,1,0:T(1,128)S(1)} all-to-all(f32[16,1,768]{2,1,0:T(1,128)S(1)} %get-tuple-element.48), channel_id=1, replica_groups=mesh['tm'=2,'cell'=16] {'cell'}, dimensions={0} | all-to-all | bytes 98304 | tf_op jit(solution)/shard_map/all_to_all | solution.py:79
  49.1 0.6 push.2
  49.7 1.6 %collective-permute-start.4 = (f32[2,8,128]{2,1,0:T(8,128)S(1)}, f32[2,8,128]{2,1,0:T(8,128)S(1)}, u32[]{:S(2)}, u32[]{:S(2)}) collective-permute-start(f32[2,8,128]{2,1,0:T(8,128)S(1)} %get-tuple-element.51), channel_id=1, source_target_pairs={{0,16},{16,0},{1,17},{17,1},{2,18},{18,2},{3,19},{19,3},{4,20},{20... | collective-permute-start | bytes 24584 | tf_op jit(solution)/shard_map/ppermute | solution.py:51
  51.3 1.9 %sweep.3 = (f32[2,2,8,128]{3,2,1,0:T(8,128)S(1)}, f32[2,256,128]{2,1,0:T(8,128)S(1)}) custom-call(f32[256,128]{1,0:T(8,128)S(1)} %copy-done.2, f32[3,256,128]{2,1,0:T(8,128)S(1)} %collective-permute-done.5.refs_1_, f32[2,256,128]{2,1,0:T(8,128)S(1)} %copy-done.1, f32[2,2,128,128]{3,2,1,0:T(8,128)S(1)} %copy-done, ...), custom_call_target="tpu_custom_call" | custom-call | bytes 3694592 | tf_op jit(solution)/shard_map/sweep/pallas_call | solution.py:85
  53.9 9.7 %all_to_all.28.received = f32[16,1,1280]{2,1,0:T(1,128)S(1)} all-to-all(f32[16,1,1280]{2,1,0:T(1,128)S(1)} %get-tuple-element.55), channel_id=1, replica_groups=mesh['tm'=2,'cell'=16] {'cell'}, dimensions={0} | all-to-all | bytes 163840 | tf_op jit(solution)/shard_map/all_to_all | solution.py:79
  63.6 0.9 %first.1 = (f32[2,2,16,128]{3,2,1,0:T(8,128)S(1)}, f32[16,1,768]{2,1,0:T(1,128)S(1)}) custom-call(f32[16,1,1280]{2,1,0:T(1,128)S(1)} %all_to_all.28.received, f32[16,128]{1,0:T(8,128)S(1)} %get-tuple-element.56.base, bf16[2,256,896]{2,1,0:T(8,128)(2,1)S(1)} %get-tuple-element.50.mixing, ...), custom_call_target="tpu_custom_call" | custom-call | bytes 3457024 | tf_op jit(solution)/shard_map/first/pallas_call | solution.py:85
  64.5 9.3 %all_to_all.29.received = f32[16,1,768]{2,1,0:T(1,128)S(1)} all-to-all(f32[16,1,768]{2,1,0:T(1,128)S(1)} %get-tuple-element.57), channel_id=1, replica_groups=mesh['tm'=2,'cell'=16] {'cell'}, dimensions={0} | all-to-all | bytes 98304 | tf_op jit(solution)/shard_map/all_to_all | solution.py:79
  73.9 0.8 push.3
  74.7 1.5 %collective-permute-start.6 = (f32[2,8,128]{2,1,0:T(8,128)S(1)}, f32[2,8,128]{2,1,0:T(8,128)S(1)}, u32[]{:S(2)}, u32[]{:S(2)}) collective-permute-start(f32[2,8,128]{2,1,0:T(8,128)S(1)} %get-tuple-element.60), channel_id=1, source_target_pairs={{0,16},{16,0},{1,17},{17,1},{2,18},{18,2},{3,19},{19,3},{4,20},{20... | collective-permute-start | bytes 24584 | tf_op jit(solution)/shard_map/ppermute | solution.py:51
  76.2 2.2 %collective-permute-done.6.received = f32[2,8,128]{2,1,0:T(8,128)S(1)} collective-permute-done((f32[2,8,128]{2,1,0:T(8,128)S(1)}, f32[2,8,128]{2,1,0:T(8,128)S(1)}, u32[]{:S(2)}, u32[]{:S(2)}) %collective-permute-start.6) | collective-permute-done | bytes 8224 | tf_op jit(solution)/shard_map/ppermute | solution.py:51
  78.4 1.1 %finish.1 = f32[2,256,128]{2,1,0:T(8,128)} custom-call(f32[2,8,128]{2,1,0:T(8,128)S(1)} %collective-permute-done.6.received, f32[2,2,8,128]{3,2,1,0:T(8,128)S(1)} %get-tuple-element.61.pushes, f32[2,2,8,128]{3,2,1,0:T(8,128)S(1)} %get-tuple-element.59.refs_0_.starts, f32[2,2,128,128]{3,2,1,0:T(8,128)S(1)} %copy-done, ...), custom_call_target="tpu_custom_call" | custom-call | bytes 835584 | tf_op jit(solution)/shard_map/finish/pallas_call | solution.py:85
  (22 shorter events, 1.8 us)
Async XLA Ops:
  0.0 0.9 %copy-start = (f32[2,2,128,128]{3,2,1,0:T(8,128)S(1)}, f32[2,2,128,128]{3,2,1,0:T(8,128)}, u32[]{:S(2)}) copy-start(f32[2,2,128,128]{3,2,1,0:T(8,128)} %coarse.11) | copy-start | bytes 786436
  0.0 1.0 %copy-start.1 = (f32[2,256,128]{2,1,0:T(8,128)S(1)}, f32[2,256,128]{2,1,0:T(8,128)}, u32[]{:S(2)}) copy-start(f32[2,256,128]{2,1,0:T(8,128)} %refs_2_.3) | copy-start | bytes 786436
  0.0 1.1 %copy-start.2 = (f32[256,128]{1,0:T(8,128)S(1)}, f32[256,128]{1,0:T(8,128)}, u32[]{:S(2)}) copy-start(f32[256,128]{1,0:T(8,128)} %refs_0_.2) | copy-start | bytes 393220
  0.0 1.1 %copy-start.4 = (s32[256]{0:T(256)S(1)}, s32[256]{0:T(256)}, u32[]{:S(2)}) copy-start(s32[256]{0:T(256)} %param.11) | copy-start | bytes 3076
  0.0 1.2 %copy-start.3 = (f32[2,2,128,128]{3,2,1,0:T(8,128)S(1)}, f32[2,2,128,128]{3,2,1,0:T(8,128)}, u32[]{:S(2)}) copy-start(f32[2,2,128,128]{3,2,1,0:T(8,128)} %fine.1) | copy-start | bytes 786436
  0.0 1.2 %copy-start.5 = (f32[128]{0:T(128)S(1)}, f32[128]{0:T(128)}, u32[]{:S(2)}) copy-start(f32[128]{0:T(128)} %param.8) | copy-start | bytes 1540
  2.5 5.2 %collective-permute-start = (f32[896,128]{1,0:T(8,128)S(1)}, f32[896,128]{1,0:T(8,128)S(1)}, u32[]{:S(2)}, u32[]{:S(2)}) collective-permute-start(f32[896,128]{1,0:T(8,128)S(1)} %get-tuple-element.35), channel_id=1, source_target_pairs={{0,1},{1,0},{2,3},{3,2},{4,5},{5,4},{6,7},{7,6},{8,9},{9,8},{10,11... | collective-permute-start | bytes 1376264 | tf_op jit(solution)/shard_map/ppermute | solution.py:56
  3.1 4.2 %collective-permute-start.1 = (f32[2,8,128]{2,1,0:T(8,128)S(1)}, f32[2,8,128]{2,1,0:T(8,128)S(1)}, u32[]{:S(2)}, u32[]{:S(2)}) collective-permute-start(f32[2,8,128]{2,1,0:T(8,128)S(1)} %get-tuple-element.37), channel_id=1, source_target_pairs={{0,16},{16,0},{1,17},{17,1},{2,18},{18,2},{3,19},{19,3},{4,20},{20... | collective-permute-start | bytes 24584 | tf_op jit(solution)/shard_map/ppermute | solution.py:51
  19.4 7.2 %collective-permute-start.2 = (f32[240,128]{1,0:T(8,128)S(1)}, f32[240,128]{1,0:T(8,128)S(1)}, u32[]{:S(2)}, u32[]{:S(2)}) collective-permute-start(f32[240,128]{1,0:T(8,128)S(1)} %middle.1.a), channel_id=1, source_target_pairs={{0,8},{1,9},{2,10},{3,11},{4,12},{5,13},{6,14},{7,15},{8,0},{9,1},... | collective-permute-start | bytes 368648 | tf_op jit(solution)/shard_map/ppermute | solution.py:75
  36.0 1.9 %collective-permute-start.3 = (f32[4,240,128]{2,1,0:T(8,128)S(1)}, f32[4,240,128]{2,1,0:T(8,128)S(1)}, u32[]{:S(2)}, u32[]{:S(2)}) collective-permute-start(f32[4,240,128]{2,1,0:T(8,128)S(1)} %all_to_all.26.mine), channel_id=1, source_target_pairs={{0,1},{1,0},{2,3},{3,2},{4,5},{5,4},{6,7},{7,6},{8,9},{9,8},{10,11... | collective-permute-start | bytes 1474568 | tf_op jit(solution)/shard_map/ppermute | solution.py:56
  36.0 15.3 %collective-permute-start.5 = (f32[3,256,128]{2,1,0:T(8,128)S(1)}, f32[3,256,128]{2,1,0:T(8,128)S(1)}, u32[]{:S(2)}, u32[]{:S(2)}) collective-permute-start(f32[3,256,128]{2,1,0:T(8,128)S(1)} %sweep.2), channel_id=1, source_target_pairs={{0,16},{16,0},{1,17},{17,1},{2,18},{18,2},{3,19},{19,3},{4,20},{20... | collective-permute-start | bytes 1179656 | tf_op jit(solution)/shard_map/ppermute | solution.py:51
  49.7 3.7 %collective-permute-start.4 = (f32[2,8,128]{2,1,0:T(8,128)S(1)}, f32[2,8,128]{2,1,0:T(8,128)S(1)}, u32[]{:S(2)}, u32[]{:S(2)}) collective-permute-start(f32[2,8,128]{2,1,0:T(8,128)S(1)} %get-tuple-element.51), channel_id=1, source_target_pairs={{0,16},{16,0},{1,17},{17,1},{2,18},{18,2},{3,19},{19,3},{4,20},{20... | collective-permute-start | bytes 24584 | tf_op jit(solution)/shard_map/ppermute | solution.py:51
  74.7 3.7 %collective-permute-start.6 = (f32[2,8,128]{2,1,0:T(8,128)S(1)}, f32[2,8,128]{2,1,0:T(8,128)S(1)}, u32[]{:S(2)}, u32[]{:S(2)}) collective-permute-start(f32[2,8,128]{2,1,0:T(8,128)S(1)} %get-tuple-element.60), channel_id=1, source_target_pairs={{0,16},{16,0},{1,17},{17,1},{2,18},{18,2},{3,19},{19,3},{4,20},{20... | collective-permute-start | bytes 24584 | tf_op jit(solution)/shard_map/ppermute | solution.py:51

commit v10 on v9

--- a/solution.py
+++ b/solution.py
@@ -79,14 +79,14 @@
     return lax.all_to_all(block, "cell", 0, 0, axis_index_groups=groups)
 
 
-def call(kernel, name, outs, args, scratch=(), flops=0):
+def call(kernel, name, outs, args, scratch=(), flops=0, space=pltpu.VMEM):
     size = sum(x.size * x.dtype.itemsize for x in args)
     size += sum(x.size * x.dtype.itemsize for x in outs)
     return pl.pallas_call(
         kernel,
         out_shape=outs,
         in_specs=[pl.BlockSpec(memory_space=pltpu.VMEM)] * len(args),
-        out_specs=[pl.BlockSpec(memory_space=pltpu.VMEM)] * len(outs),
+        out_specs=[pl.BlockSpec(memory_space=space)] * len(outs),
         scratch_shapes=list(scratch),
         compiler_params=pltpu.CompilerParams(vmem_limit_bytes=24 << 20),
         cost_estimate=pl.CostEstimate(flops=flops, bytes_accessed=size, transcendentals=0),
@@ -394,36 +394,49 @@
     send_line(rows, out)
 
 
-def mixing_kernel(everyone, per, mine, theirs, base, powers, table,
+def unpacked(parts, kept, held):
+    n, rows, _ = parts.shape
+    rows -= kept
+    mixed = parts[0, rows:]
+    for p in range(n):
+        held[p * rows:(p + 1) * rows] = parts[p, :rows]
+        if p:
+            mixed = mixed + parts[p, rows:]
+    return mixed
+
+
+def own_kernel(kept, mine, ready, mixed, held):
+    half, _, wider = ready.shape
+    width = wider // MATS
+    mixed[...] = unpacked(mine, kept, held)
+    for h in range(half):
+        for i in range(MATS):
+            at = (h * MATS + i) * width
+            ready[h, :, block(i + 1, width)] = stacked(held[at:at + width])
+
+
+def mixing_kernel(everyone, per, theirs, ready, mine, base, powers, table,
                   mixing, partial, out, held):
     slices, _, _, wider = powers.shape
     width = wider // (FINE_MAX + 1)
     half = slices // 2
-    n, rows, _ = mine.shape
-    rows -= slices * ROWS
     rate = table[0, RATE_ROW]
     core = lax.rem(lax.axis_index("cell"), 2)
-    mixed = 0.0
-    for ref, at in ((mine, core), (theirs, 1 - core)):
-        for p in range(n):
-            place = at * (half * MATS * width) + p * rows
-            held[pl.ds(place, rows), :] = ref[p, :rows]
-            mixed = mixed + ref[p, rows:]
-    def place(l, i):
-        at = (l * MATS + i) * width
-        mixing[l, :, block(i + 1, width)] = stacked(held[at:at + width])
-
-    for l in range(slices):
-        for i in range(FINE_MIN):
-            place(l, i)
+    mixing[pl.ds(core * half, half)] = ready[...]
+    mixed = mine[...] + unpacked(theirs, slices * ROWS, held)
+
+    def place(h, i):
+        at = (h * MATS + i) * width
+        mixing[(1 - core) * half + h, :, block(i + 1, width)] = stacked(held[at:at + width])
+
+    for h in range(half):
+        for i in range(MATS):
+            place(h, i)
     rows = [
         [mixed[l * ROWS + m:l * ROWS + m + 1] for m in range(FINE_MIN + 1)]
         for l in range(slices)
     ]
     a = first_averages(rows, mixing, rate, width)
-    for l in range(slices):
-        for i in range(FINE_MIN, MATS):
-            place(l, i)
     send_rows(everyone, per, a, base, rate, powers, table, partial, out, width)
 
 
@@ -508,11 +521,12 @@
     send_line(sent, out)
 
 
-def finish_kernel(received, pushes, starts, coarse, ends, table, out):
+def finish_kernel(received, pushes, starts, coarse, ends, table, out, held, sent):
     slices, groups, width, _ = coarse.shape
     per = ends.shape[1] // groups
     counts = [spread_counts(table[g, COUNT_ROW]) for g in range(groups)]
     x = [jnp.where(leading(), 0.0, received[g]) for g in range(groups)]
+    copies = []
     for l in range(slices):
         for g in range(groups):
             here = group_rows(g, per)
@@ -520,7 +534,15 @@
             add = jnp.zeros((per, width), F32)
             for i in range(CLASSES):
                 add = jnp.where(counts[g] == float(FINE_MIN + i), x[g][i:i + 1], add)
-            out[l, here] = ends[l, here] + add
+            held[l, here] = ends[l, here] + add
+            copies.append(
+                pltpu.make_async_copy(
+                    held.at[l, here], out.at[l, here], sent.at[l * groups + g]
+                )
+            )
+            copies[-1].start()
+    for copy in copies:
+        copy.wait()
 
 
 def body(initial, source, mix_rate, fine, coarse, step_counts):
@@ -600,11 +622,16 @@
         (initial, sent, source, coarse, powers, table),
     )
     theirs = swap_core(gathered)
+    ready, mixed = call(
+        functools.partial(own_kernel, slices * ROWS), "own",
+        [shape(half, 2 * width, MATS * width, dtype=BF16), rows8], (gathered,),
+        scratch=[pltpu.VMEM((half * MATS * width, width), F32)],
+    )
     mixing, first, out = call(
         functools.partial(mixing_kernel, everyone, per), "mixing",
         [shape(slices, 2 * width, MATS * width, dtype=BF16), partial, line3],
-        (gathered, theirs, base, powers, table),
-        scratch=[pltpu.VMEM((slices * MATS * width, width), F32)],
+        (theirs, ready, mixed, base, powers, table),
+        scratch=[pltpu.VMEM((half * MATS * width, width), F32)],
     )
     pushes1, end = call(
         push_kernel, "push", [vectors, vector],
@@ -635,7 +662,12 @@
         if turn + 1 < turns:
             moved, = call(vectors_kernel, "vectors", [vector], (moved, pushes2, moved1, coarse))
     out, = call(
-        finish_kernel, "finish", [states], (moved, pushes2, moved1, coarse, ends, table)
+        finish_kernel, "finish", [states], (moved, pushes2, moved1, coarse, ends, table),
+        scratch=[
+            pltpu.VMEM((slices, cells, width), F32),
+            pltpu.SemaphoreType.DMA((slices * groups,)),
+        ],
+        space=pltpu.HBM,
     )
     return out
 

time: 79.7 us -> 79.7 us (level)
    pallas_call x15 -> x16, Pallas kernels: 11.5 us -> 11.6 us  [call(): pl.pallas_call(kernel, out_shape=outs, in_specs=[pl.BlockSpec(memory_spac...]
where the time goes in v10:
time: 79.7 us; the launch traced here: 79.4 us
  blocking collectives  50.3 us (63%)
  Pallas kernels  11.6 us (15%)
  starting transfers between devices  10.5 us (13%)
  waiting for transfers between devices  5.83 us (7%)
  local copies, waits for them, and re-layouts  1.14 us (1%)
    all_to_all x5, blocking collectives, exchange(): return lax.all_to_all(block, 'cell', 0, 0, axis_index_groups=groups)  50.3 us
    pallas_call x16, Pallas kernels, call(): pl.pallas_call(kernel, out_shape=outs, in_specs=[pl.BlockSpec(memory_spac...  11.6 us
    ppermute x4, starting transfers between devices, from_behind(): lax.ppermute(block, axis, [(i, (i + distance) % n) for i in range(n)])  7.14 us
    ppermute x4, waiting for transfers between devices, from_behind(): lax.ppermute(block, axis, [(i, (i + distance) % n) for i in range(n)])  2.98 us
    ppermute x1, starting transfers between devices, far_swap(): return lax.ppermute(block, 'cell', [(i, i ^ distance) for i in range(n)])  2.77 us
    ppermute x1, waiting for transfers between devices, far_swap(): return lax.ppermute(block, 'cell', [(i, i ^ distance) for i in range(n)])  2.56 us
  transfers between devices with their start and end apart: 7, of which 5 were waited for; matrix products, arithmetic and copies ran while one was open for 0% of the time, Pallas kernels for 9%

profile of v10, /device:TPU:0, one launch (start us, length us, event | category | flops | bytes accessed | tf_op | source)
XLA Modules:
  0.0 79.4 jit_solution(3078362866207672188)
XLA Ops:
  0.0 0.9 %copy-done = f32[2,2,128,128]{3,2,1,0:T(8,128)S(1)} copy-done((f32[2,2,128,128]{3,2,1,0:T(8,128)S(1)}, f32[2,2,128,128]{3,2,1,0:T(8,128)}, u32[]{:S(2)}) %copy-start) | copy-done | bytes 262168
  1.2 1.4 %setup.1 = (f32[896,128]{1,0:T(8,128)S(1)}, f32[896,128]{1,0:T(8,128)S(1)}, f32[2,2,512,128]{3,2,1,0:T(8,128)S(1)}, f32[2,8,128]{2,1,0:T(8,128)S(1)}, f32[2,8,12...) custom-call(f32[2,2,128,128]{3,2,1,0:T(8,128)S(1)} %copy-done.3, f32[1,128]{1,0:T(1,128)S(1)} %bitcast.5, ...), custom_call_target="tpu_custom_call" | custom-call | bytes 2930176 | tf_op jit(solution)/shard_map/setup/pallas_call | solution.py:85
  2.5 0.6 collective-permute-start
  3.1 2.6 %collective-permute-start.1 = (f32[2,8,128]{2,1,0:T(8,128)S(1)}, f32[2,8,128]{2,1,0:T(8,128)S(1)}, u32[]{:S(2)}, u32[]{:S(2)}) collective-permute-start(f32[2,8,128]{2,1,0:T(8,128)S(1)} %get-tuple-element.39), channel_id=1, source_target_pairs={{0,16},{16,0},{1,17},{17,1},{2,18},{18,2},{3,19},{19,3},{4,20},{20... | collective-permute-start | bytes 24584 | tf_op jit(solution)/shard_map/ppermute | solution.py:51
  5.6 1.0 %extend.1 = (bf16[2,2,256,1152]{3,2,1,0:T(8,128)(2,1)S(1)}, f32[16,128]{1,0:T(8,128)S(1)}) custom-call(f32[2,2,512,128]{3,2,1,0:T(8,128)S(1)} %get-tuple-element.41.lows, f32[2,8,128]{2,1,0:T(8,128)S(1)} %get-tuple-element.42.table.refs_4_.refs_5_, f32[2,2,8,128]{3,2,1,0:T(8,128)S(1)} %get-tuple-element.40.source_sums), custom_call_target="tpu_custom_call" | custom-call | bytes 3440640 | tf_op jit(solution)/shard_map/extend/pallas_call | solution.py:85
  6.7 0.6 collective-permute-done.1.received
  7.8 11.6 %all_to_all.25.parts = f32[4,224,128]{2,1,0:T(8,128)S(1)} all-to-all(f32[4,224,128]{2,1,0:T(8,128)S(1)} %bitcast.3), channel_id=1, replica_groups={{0,2,4,6},{1,3,5,7},{8,10,12,14},{9,11,13,15},{16,18,20,22},{17,19,21,2..., dimensions={0} | all-to-all | bytes 917504 | tf_op jit(solution)/shard_map/all_to_all | solution.py:79
  19.4 2.8 %collective-permute-start.2 = (f32[240,128]{1,0:T(8,128)S(1)}, f32[240,128]{1,0:T(8,128)S(1)}, u32[]{:S(2)}, u32[]{:S(2)}) collective-permute-start(f32[240,128]{1,0:T(8,128)S(1)} %middle.1.a), channel_id=1, source_target_pairs={{0,8},{1,9},{2,10},{3,11},{4,12},{5,13},{6,14},{7,15},{8,0},{9,1},... | collective-permute-start | bytes 368648 | tf_op jit(solution)/shard_map/ppermute | solution.py:75
  22.1 1.8 %sweep.2 = f32[3,256,128]{2,1,0:T(8,128)S(1)} custom-call(f32[256,128]{1,0:T(8,128)S(1)} %copy-done.2, f32[2,256,128]{2,1,0:T(8,128)S(1)} %copy-done.1, f32[2,2,128,128]{3,2,1,0:T(8,128)S(1)} %copy-done, bf16[2,2,256,1152]{3,2,1,0:T(8,128)(2,1)S(1)} %get-tuple-element.43.powers.refs_3_.refs_4_, f32[2,8,128]{2,1,0:T(8,128)S(1)} %get-tuple-element.42.table.refs_4_.refs_5_), custom_call_target="tpu_custom_call" | custom-call | bytes 3416064 | tf_op jit(solution)/shard_map/sweep/pallas_call | solution.py:85
  24.0 2.6 %collective-permute-done.2.b = f32[240,128]{1,0:T(8,128)S(1)} collective-permute-done((f32[240,128]{1,0:T(8,128)S(1)}, f32[240,128]{1,0:T(8,128)S(1)}, u32[]{:S(2)}, u32[]{:S(2)}) %collective-permute-start.2) | collective-permute-done | bytes 122912 | tf_op jit(solution)/shard_map/ppermute | solution.py:75
  26.6 9.4 %all_to_all.26.mine = f32[4,240,128]{2,1,0:T(8,128)S(1)} all-to-all(f32[4,240,128]{2,1,0:T(8,128)S(1)} %gather.1), channel_id=1, replica_groups={{0,2,4,6},{1,3,5,7},{8,10,12,14},{9,11,13,15},{16,18,20,22},{17,19,21,2..., dimensions={0} | all-to-all | bytes 983040 | tf_op jit(solution)/shard_map/all_to_all | solution.py:79
  36.0 1.5 %collective-permute-start.5 = (f32[3,256,128]{2,1,0:T(8,128)S(1)}, f32[3,256,128]{2,1,0:T(8,128)S(1)}, u32[]{:S(2)}, u32[]{:S(2)}) collective-permute-start(f32[3,256,128]{2,1,0:T(8,128)S(1)} %sweep.2), channel_id=1, source_target_pairs={{0,16},{16,0},{1,17},{17,1},{2,18},{18,2},{3,19},{19,3},{4,20},{20... | collective-permute-start | bytes 1179656 | tf_op jit(solution)/shard_map/ppermute | solution.py:51
  37.9 1.0 %mixing.1 = (bf16[2,256,896]{2,1,0:T(8,128)(2,1)S(1)}, f32[2,2,16,128]{3,2,1,0:T(8,128)S(1)}, f32[16,1,768]{2,1,0:T(1,128)S(1)}) custom-call(f32[4,240,128]{2,1,0:T(8,128)S(1)} %collective-permute-done.3.theirs, bf16[1,256,896]{2,1,0:T(8,128)(2,1)S(1)} %get-tuple-element.50.ready, f32[16,128]{1,0:T(8,128)S(1)} %get-tuple-element.51.mine, ...), custom_call_target="tpu_custom_call" | custom-call | bytes 4333568 | tf_op jit(solution)/shard_map/mixing/pallas_call | solution.py:85
  38.9 10.2 %all_to_all.27.received = f32[16,1,768]{2,1,0:T(1,128)S(1)} all-to-all(f32[16,1,768]{2,1,0:T(1,128)S(1)} %get-tuple-element.52), channel_id=1, replica_groups=mesh['tm'=2,'cell'=16] {'cell'}, dimensions={0} | all-to-all | bytes 98304 | tf_op jit(solution)/shard_map/all_to_all | solution.py:79
  49.1 0.6 push.2
  49.7 1.6 %collective-permute-start.4 = (f32[2,8,128]{2,1,0:T(8,128)S(1)}, f32[2,8,128]{2,1,0:T(8,128)S(1)}, u32[]{:S(2)}, u32[]{:S(2)}) collective-permute-start(f32[2,8,128]{2,1,0:T(8,128)S(1)} %get-tuple-element.55), channel_id=1, source_target_pairs={{0,16},{16,0},{1,17},{17,1},{2,18},{18,2},{3,19},{19,3},{4,20},{20... | collective-permute-start | bytes 24584 | tf_op jit(solution)/shard_map/ppermute | solution.py:51
  51.3 1.9 %sweep.3 = (f32[2,2,8,128]{3,2,1,0:T(8,128)S(1)}, f32[2,256,128]{2,1,0:T(8,128)S(1)}) custom-call(f32[256,128]{1,0:T(8,128)S(1)} %copy-done.2, f32[3,256,128]{2,1,0:T(8,128)S(1)} %collective-permute-done.5.refs_1_, f32[2,256,128]{2,1,0:T(8,128)S(1)} %copy-done.1, f32[2,2,128,128]{3,2,1,0:T(8,128)S(1)} %copy-done, ...), custom_call_target="tpu_custom_call" | custom-call | bytes 3694592 | tf_op jit(solution)/shard_map/sweep/pallas_call | solution.py:85
  53.9 9.7 %all_to_all.28.received = f32[16,1,1280]{2,1,0:T(1,128)S(1)} all-to-all(f32[16,1,1280]{2,1,0:T(1,128)S(1)} %get-tuple-element.59), channel_id=1, replica_groups=mesh['tm'=2,'cell'=16] {'cell'}, dimensions={0} | all-to-all | bytes 163840 | tf_op jit(solution)/shard_map/all_to_all | solution.py:79
  63.6 0.9 %first.1 = (f32[2,2,16,128]{3,2,1,0:T(8,128)S(1)}, f32[16,1,768]{2,1,0:T(1,128)S(1)}) custom-call(f32[16,1,1280]{2,1,0:T(1,128)S(1)} %all_to_all.28.received, f32[16,128]{1,0:T(8,128)S(1)} %get-tuple-element.60.base, bf16[2,256,896]{2,1,0:T(8,128)(2,1)S(1)} %get-tuple-element.54.mixing, ...), custom_call_target="tpu_custom_call" | custom-call | bytes 3457024 | tf_op jit(solution)/shard_map/first/pallas_call | solution.py:85
  64.5 9.3 %all_to_all.29.received = f32[16,1,768]{2,1,0:T(1,128)S(1)} all-to-all(f32[16,1,768]{2,1,0:T(1,128)S(1)} %get-tuple-element.61), channel_id=1, replica_groups=mesh['tm'=2,'cell'=16] {'cell'}, dimensions={0} | all-to-all | bytes 98304 | tf_op jit(solution)/shard_map/all_to_all | solution.py:79
  73.9 0.8 push.3
  74.7 1.5 %collective-permute-start.6 = (f32[2,8,128]{2,1,0:T(8,128)S(1)}, f32[2,8,128]{2,1,0:T(8,128)S(1)}, u32[]{:S(2)}, u32[]{:S(2)}) collective-permute-start(f32[2,8,128]{2,1,0:T(8,128)S(1)} %get-tuple-element.64), channel_id=1, source_target_pairs={{0,16},{16,0},{1,17},{17,1},{2,18},{18,2},{3,19},{19,3},{4,20},{20... | collective-permute-start | bytes 24584 | tf_op jit(solution)/shard_map/ppermute | solution.py:51
  76.2 2.2 %collective-permute-done.6.received = f32[2,8,128]{2,1,0:T(8,128)S(1)} collective-permute-done((f32[2,8,128]{2,1,0:T(8,128)S(1)}, f32[2,8,128]{2,1,0:T(8,128)S(1)}, u32[]{:S(2)}, u32[]{:S(2)}) %collective-permute-start.6) | collective-permute-done | bytes 8224 | tf_op jit(solution)/shard_map/ppermute | solution.py:51
  78.4 1.0 %finish.1 = f32[2,256,128]{2,1,0:T(8,128)} custom-call(f32[2,8,128]{2,1,0:T(8,128)S(1)} %collective-permute-done.6.received, f32[2,2,8,128]{3,2,1,0:T(8,128)S(1)} %get-tuple-element.65.pushes, f32[2,2,8,128]{3,2,1,0:T(8,128)S(1)} %get-tuple-element.63.refs_0_.starts, f32[2,2,128,128]{3,2,1,0:T(8,128)S(1)} %copy-done, ...), custom_call_target="tpu_custom_call" | custom-call | bytes 835584 | tf_op jit(solution)/shard_map/finish/pallas_call | solution.py:85
  (23 shorter events, 1.8 us)
Async XLA Ops:
  0.0 0.9 %copy-start = (f32[2,2,128,128]{3,2,1,0:T(8,128)S(1)}, f32[2,2,128,128]{3,2,1,0:T(8,128)}, u32[]{:S(2)}) copy-start(f32[2,2,128,128]{3,2,1,0:T(8,128)} %coarse.11) | copy-start | bytes 786436
  0.0 1.0 %copy-start.1 = (f32[2,256,128]{2,1,0:T(8,128)S(1)}, f32[2,256,128]{2,1,0:T(8,128)}, u32[]{:S(2)}) copy-start(f32[2,256,128]{2,1,0:T(8,128)} %refs_2_.3) | copy-start | bytes 786436
  0.0 1.1 %copy-start.2 = (f32[256,128]{1,0:T(8,128)S(1)}, f32[256,128]{1,0:T(8,128)}, u32[]{:S(2)}) copy-start(f32[256,128]{1,0:T(8,128)} %refs_0_.2) | copy-start | bytes 393220
  0.0 1.1 %copy-start.4 = (s32[256]{0:T(256)S(1)}, s32[256]{0:T(256)}, u32[]{:S(2)}) copy-start(s32[256]{0:T(256)} %param.11) | copy-start | bytes 3076
  0.0 1.2 %copy-start.3 = (f32[2,2,128,128]{3,2,1,0:T(8,128)S(1)}, f32[2,2,128,128]{3,2,1,0:T(8,128)}, u32[]{:S(2)}) copy-start(f32[2,2,128,128]{3,2,1,0:T(8,128)} %fine.1) | copy-start | bytes 786436
  0.0 1.2 %copy-start.5 = (f32[128]{0:T(128)S(1)}, f32[128]{0:T(128)}, u32[]{:S(2)}) copy-start(f32[128]{0:T(128)} %param.8) | copy-start | bytes 1540
  2.5 5.2 %collective-permute-start = (f32[896,128]{1,0:T(8,128)S(1)}, f32[896,128]{1,0:T(8,128)S(1)}, u32[]{:S(2)}, u32[]{:S(2)}) collective-permute-start(f32[896,128]{1,0:T(8,128)S(1)} %get-tuple-element.37), channel_id=1, source_target_pairs={{0,1},{1,0},{2,3},{3,2},{4,5},{5,4},{6,7},{7,6},{8,9},{9,8},{10,11... | collective-permute-start | bytes 1376264 | tf_op jit(solution)/shard_map/ppermute | solution.py:56
  3.1 4.2 %collective-permute-start.1 = (f32[2,8,128]{2,1,0:T(8,128)S(1)}, f32[2,8,128]{2,1,0:T(8,128)S(1)}, u32[]{:S(2)}, u32[]{:S(2)}) collective-permute-start(f32[2,8,128]{2,1,0:T(8,128)S(1)} %get-tuple-element.39), channel_id=1, source_target_pairs={{0,16},{16,0},{1,17},{17,1},{2,18},{18,2},{3,19},{19,3},{4,20},{20... | collective-permute-start | bytes 24584 | tf_op jit(solution)/shard_map/ppermute | solution.py:51
  19.4 7.2 %collective-permute-start.2 = (f32[240,128]{1,0:T(8,128)S(1)}, f32[240,128]{1,0:T(8,128)S(1)}, u32[]{:S(2)}, u32[]{:S(2)}) collective-permute-start(f32[240,128]{1,0:T(8,128)S(1)} %middle.1.a), channel_id=1, source_target_pairs={{0,8},{1,9},{2,10},{3,11},{4,12},{5,13},{6,14},{7,15},{8,0},{9,1},... | collective-permute-start | bytes 368648 | tf_op jit(solution)/shard_map/ppermute | solution.py:75
  36.0 1.9 %collective-permute-start.3 = (f32[4,240,128]{2,1,0:T(8,128)S(1)}, f32[4,240,128]{2,1,0:T(8,128)S(1)}, u32[]{:S(2)}, u32[]{:S(2)}) collective-permute-start(f32[4,240,128]{2,1,0:T(8,128)S(1)} %all_to_all.26.mine), channel_id=1, source_target_pairs={{0,1},{1,0},{2,3},{3,2},{4,5},{5,4},{6,7},{7,6},{8,9},{9,8},{10,11... | collective-permute-start | bytes 1474568 | tf_op jit(solution)/shard_map/ppermute | solution.py:56
  36.0 15.3 %collective-permute-start.5 = (f32[3,256,128]{2,1,0:T(8,128)S(1)}, f32[3,256,128]{2,1,0:T(8,128)S(1)}, u32[]{:S(2)}, u32[]{:S(2)}) collective-permute-start(f32[3,256,128]{2,1,0:T(8,128)S(1)} %sweep.2), channel_id=1, source_target_pairs={{0,16},{16,0},{1,17},{17,1},{2,18},{18,2},{3,19},{19,3},{4,20},{20... | collective-permute-start | bytes 1179656 | tf_op jit(solution)/shard_map/ppermute | solution.py:51
  49.7 3.7 %collective-permute-start.4 = (f32[2,8,128]{2,1,0:T(8,128)S(1)}, f32[2,8,128]{2,1,0:T(8,128)S(1)}, u32[]{:S(2)}, u32[]{:S(2)}) collective-permute-start(f32[2,8,128]{2,1,0:T(8,128)S(1)} %get-tuple-element.55), channel_id=1, source_target_pairs={{0,16},{16,0},{1,17},{17,1},{2,18},{18,2},{3,19},{19,3},{4,20},{20... | collective-permute-start | bytes 24584 | tf_op jit(solution)/shard_map/ppermute | solution.py:51
  74.7 3.7 %collective-permute-start.6 = (f32[2,8,128]{2,1,0:T(8,128)S(1)}, f32[2,8,128]{2,1,0:T(8,128)S(1)}, u32[]{:S(2)}, u32[]{:S(2)}) collective-permute-start(f32[2,8,128]{2,1,0:T(8,128)S(1)} %get-tuple-element.64), channel_id=1, source_target_pairs={{0,16},{16,0},{1,17},{17,1},{2,18},{18,2},{3,19},{19,3},{4,20},{20... | collective-permute-start | bytes 24584 | tf_op jit(solution)/shard_map/ppermute | solution.py:51

commit v11 on v9

--- a/solution.py
+++ b/solution.py
@@ -320,9 +320,7 @@
 
 
 def gather_kernel(a, b, out):
-    total = a[...] + b[...]
-    for p in range(out.shape[0]):
-        out[p] = total
+    out[...] = a[...] + b[...]
 
 
 def wide(row):
@@ -394,21 +392,24 @@
     send_line(rows, out)
 
 
-def mixing_kernel(everyone, per, mine, theirs, base, powers, table,
-                  mixing, partial, out, held):
+def mixing_kernel(everyone, per, near, *refs):
+    blocks, refs = refs[:2 * near], refs[2 * near:]
+    base, powers, table, mixing, partial, out, held = refs
     slices, _, _, wider = powers.shape
     width = wider // (FINE_MAX + 1)
     half = slices // 2
-    n, rows, _ = mine.shape
-    rows -= slices * ROWS
+    rows = blocks[0].shape[0] - slices * ROWS
     rate = table[0, RATE_ROW]
-    core = lax.rem(lax.axis_index("cell"), 2)
+    index = lax.axis_index("cell")
+    core = lax.rem(index, 2)
+    here = lax.rem(lax.div(index, 2), near)
     mixed = 0.0
-    for ref, at in ((mine, core), (theirs, 1 - core)):
-        for p in range(n):
-            place = at * (half * MATS * width) + p * rows
-            held[pl.ds(place, rows), :] = ref[p, :rows]
-            mixed = mixed + ref[p, rows:]
+    for refs, at in ((blocks[:near], core), (blocks[near:], 1 - core)):
+        for j, ref in enumerate(refs):
+            shard = jnp.bitwise_xor(here, j)
+            held[pl.ds(at * (half * MATS * width) + shard * rows, rows), :] = ref[:rows]
+            mixed = mixed + ref[rows:]
+
     def place(l, i):
         at = (l * MATS + i) * width
         mixing[l, :, block(i + 1, width)] = stacked(held[at:at + width])
@@ -592,18 +593,19 @@
                 (initial, sent, source, coarse, powers, table),
             )
     payload, = call(
-        gather_kernel, "gather", [shape(near, shard + slices * ROWS, width)], (block, far)
-    )
-    gathered = exchange(payload, near_groups())
+        gather_kernel, "gather", [shape(shard + slices * ROWS, width)], (block, far)
+    )
+    crossed = {j: far_swap(payload, 2 * j) for j in reversed(range(1, near))}
+    gathered = [payload] + [crossed[j] for j in range(1, near)]
     sums, ends = call(
         functools.partial(sweep_kernel, False, True), "sweep", [vectors, states],
         (initial, sent, source, coarse, powers, table),
     )
-    theirs = swap_core(gathered)
+    theirs = [swap_core(x) for x in gathered]
     mixing, first, out = call(
-        functools.partial(mixing_kernel, everyone, per), "mixing",
+        functools.partial(mixing_kernel, everyone, per, near), "mixing",
         [shape(slices, 2 * width, MATS * width, dtype=BF16), partial, line3],
-        (gathered, theirs, base, powers, table),
+        (*gathered, *theirs, base, powers, table),
         scratch=[pltpu.VMEM((slices * MATS * width, width), F32)],
     )
     pushes1, end = call(

time: 79.7 us -> 79.6 us (level)
  blocking collectives: 50.3 us -> 41.5 us
  waiting for transfers between devices: 5.94 us -> 12.9 us
  starting transfers between devices: 10.5 us -> 12.1 us
    all_to_all x5 -> x4, blocking collectives: 50.3 us -> 41.5 us  [exchange(): return lax.all_to_all(block, 'cell', 0, 0, axis_index_groups=groups)]
    ppermute x1 -> x4, waiting for transfers between devices: 2.57 us -> 6.73 us  [far_swap(): return lax.ppermute(block, 'cell', [(i, i ^ distance) for i in range(n)])]
    ppermute x1 -> x4, starting transfers between devices: 2.77 us -> 6.33 us  [far_swap(): return lax.ppermute(block, 'cell', [(i, i ^ distance) for i in range(n)])]
    ppermute x4, starting transfers between devices: 7.14 us -> 5.23 us  [from_behind(): lax.ppermute(block, axis, [(i, (i + distance) % n) for i in range(n)])]
    ppermute x4, waiting for transfers between devices: 2.99 us -> 4.9 us  [from_behind(): lax.ppermute(block, axis, [(i, (i + distance) % n) for i in range(n)])]
    ppermute x2 -> x5, waiting for transfers between devices: 0.37 us -> 1.32 us  [swap_core(): return lax.ppermute(block, 'cell', [(i, i ^ 1) for i in range(n)])]
  transfers between devices with their start and end apart: 7 -> 13, of which waited for: 5 -> 8; matrix products, arithmetic and copies ran while one was open for 0% -> 0% of each run, Pallas kernels for 9% -> 9%
where the time goes in v11:
time: 79.6 us; the launch traced here: 79.3 us
  blocking collectives  41.5 us (52%)
  waiting for transfers between devices  12.9 us (16%)
  starting transfers between devices  12.1 us (15%)
  Pallas kernels  11.5 us (14%)
  local copies, waits for them, and re-layouts  1.17 us (1%)
    all_to_all x4, blocking collectives, exchange(): return lax.all_to_all(block, 'cell', 0, 0, axis_index_groups=groups)  41.5 us
    pallas_call x15, Pallas kernels, call(): pl.pallas_call(kernel, out_shape=outs, in_specs=[pl.BlockSpec(memory_spac...  11.5 us
    ppermute x4, waiting for transfers between devices, far_swap(): return lax.ppermute(block, 'cell', [(i, i ^ distance) for i in range(n)])  6.73 us
    ppermute x4, starting transfers between devices, far_swap(): return lax.ppermute(block, 'cell', [(i, i ^ distance) for i in range(n)])  6.33 us
    ppermute x4, starting transfers between devices, from_behind(): lax.ppermute(block, axis, [(i, (i + distance) % n) for i in range(n)])  5.23 us
    ppermute x4, waiting for transfers between devices, from_behind(): lax.ppermute(block, axis, [(i, (i + distance) % n) for i in range(n)])  4.9 us
  transfers between devices with their start and end apart: 13, of which 8 were waited for; matrix products, arithmetic and copies ran while one was open for 0% of the time, Pallas kernels for 9%

profile of v11, /device:TPU:0, one launch (start us, length us, event | category | flops | bytes accessed | tf_op | source)
XLA Modules:
  0.0 79.3 jit_solution(9450147095205515966)
XLA Ops:
  1.2 1.4 %setup.1 = (f32[896,128]{1,0:T(8,128)S(1)}, f32[896,128]{1,0:T(8,128)S(1)}, f32[2,2,512,128]{3,2,1,0:T(8,128)S(1)}, f32[2,8,128]{2,1,0:T(8,128)S(1)}, f32[2,8,12...) custom-call(f32[2,2,128,128]{3,2,1,0:T(8,128)S(1)} %copy-done.3, f32[1,128]{1,0:T(1,128)S(1)} %bitcast.5, ...), custom_call_target="tpu_custom_call" | custom-call | bytes 2930176 | tf_op jit(solution)/shard_map/setup/pallas_call | solution.py:85
  3.1 2.5 %collective-permute-start.1 = (f32[2,8,128]{2,1,0:T(8,128)S(1)}, f32[2,8,128]{2,1,0:T(8,128)S(1)}, u32[]{:S(2)}, u32[]{:S(2)}) collective-permute-start(f32[2,8,128]{2,1,0:T(8,128)S(1)} %get-tuple-element.37), channel_id=1, source_target_pairs={{0,16},{16,0},{1,17},{17,1},{2,18},{18,2},{3,19},{19,3},{4,20},{20... | collective-permute-start | bytes 24584 | tf_op jit(solution)/shard_map/ppermute | solution.py:51
  5.7 1.0 %extend.1 = (bf16[2,2,256,1152]{3,2,1,0:T(8,128)(2,1)S(1)}, f32[16,128]{1,0:T(8,128)S(1)}) custom-call(f32[2,2,512,128]{3,2,1,0:T(8,128)S(1)} %get-tuple-element.39.lows, f32[2,8,128]{2,1,0:T(8,128)S(1)} %get-tuple-element.40.table.refs_4_.refs_10_.refs_5_, f32[2,2,8,128]{3,2,1,0:T(8,128)S(1)} %get-tuple-element.38.source_sums), custom_call_target="tpu_custom_call" | custom-call | bytes 3440640 | tf_op jit(solution)/shard_map/extend/pallas_call | solution.py:85
  7.8 11.6 %all_to_all.20.parts = f32[4,224,128]{2,1,0:T(8,128)S(1)} all-to-all(f32[4,224,128]{2,1,0:T(8,128)S(1)} %bitcast.3), channel_id=1, replica_groups={{0,2,4,6},{1,3,5,7},{8,10,12,14},{9,11,13,15},{16,18,20,22},{17,19,21,2..., dimensions={0} | all-to-all | bytes 917504 | tf_op jit(solution)/shard_map/all_to_all | solution.py:79
  19.4 2.8 %collective-permute-start.2 = (f32[240,128]{1,0:T(8,128)S(1)}, f32[240,128]{1,0:T(8,128)S(1)}, u32[]{:S(2)}, u32[]{:S(2)}) collective-permute-start(f32[240,128]{1,0:T(8,128)S(1)} %middle.1.a), channel_id=1, source_target_pairs={{0,8},{1,9},{2,10},{3,11},{4,12},{5,13},{6,14},{7,15},{8,0},{9,1},... | collective-permute-start | bytes 368648 | tf_op jit(solution)/shard_map/ppermute | solution.py:75
  22.2 1.8 %sweep.2 = f32[3,256,128]{2,1,0:T(8,128)S(1)} custom-call(f32[256,128]{1,0:T(8,128)S(1)} %copy-done.2, f32[2,256,128]{2,1,0:T(8,128)S(1)} %copy-done.1, f32[2,2,128,128]{3,2,1,0:T(8,128)S(1)} %copy-done, bf16[2,2,256,1152]{3,2,1,0:T(8,128)(2,1)S(1)} %get-tuple-element.41.powers.refs_3_.refs_9_.refs_4_, ...), custom_call_target="tpu_custom_call" | custom-call | bytes 3416064 | tf_op jit(solution)/shard_map/sweep/pallas_call | solution.py:85
  24.0 2.6 %collective-permute-done.2.b = f32[240,128]{1,0:T(8,128)S(1)} collective-permute-done((f32[240,128]{1,0:T(8,128)S(1)}, f32[240,128]{1,0:T(8,128)S(1)}, u32[]{:S(2)}, u32[]{:S(2)}) %collective-permute-start.2) | collective-permute-done | bytes 122912 | tf_op jit(solution)/shard_map/ppermute | solution.py:75
  26.6 1.5 %collective-permute-start.11 = (f32[3,256,128]{2,1,0:T(8,128)S(1)}, f32[3,256,128]{2,1,0:T(8,128)S(1)}, u32[]{:S(2)}, u32[]{:S(2)}) collective-permute-start(f32[3,256,128]{2,1,0:T(8,128)S(1)} %sweep.2), channel_id=1, source_target_pairs={{0,16},{16,0},{1,17},{17,1},{2,18},{18,2},{3,19},{19,3},{4,20},{20... | collective-permute-start | bytes 1179656 | tf_op jit(solution)/shard_map/ppermute | solution.py:51
  28.1 0.8 %collective-permute-start.3 = (f32[240,128]{1,0:T(8,128)S(1)}, f32[240,128]{1,0:T(8,128)S(1)}, u32[]{:S(2)}, u32[]{:S(2)}) collective-permute-start(f32[240,128]{1,0:T(8,128)S(1)} %gather.1.refs_0_), channel_id=1, source_target_pairs={{0,2},{1,3},{2,0},{3,1},{4,6},{5,7},{6,4},{7,5},{8,10},{9,11},{10,... | collective-permute-start | bytes 368648 | tf_op jit(solution)/shard_map/ppermute | solution.py:75
  28.9 2.7 %collective-permute-start.5 = (f32[240,128]{1,0:T(8,128)S(1)}, f32[240,128]{1,0:T(8,128)S(1)}, u32[]{:S(2)}, u32[]{:S(2)}) collective-permute-start(f32[240,128]{1,0:T(8,128)S(1)} %gather.1.refs_0_), channel_id=1, source_target_pairs={{0,6},{1,7},{2,4},{3,5},{4,2},{5,3},{6,0},{7,1},{8,14},{9,15},{10,... | collective-permute-start | bytes 368648 | tf_op jit(solution)/shard_map/ppermute | solution.py:75
  31.6 1.4 %collective-permute-done.3.refs_1_ = f32[240,128]{1,0:T(8,128)S(1)} collective-permute-done((f32[240,128]{1,0:T(8,128)S(1)}, f32[240,128]{1,0:T(8,128)S(1)}, u32[]{:S(2)}, u32[]{:S(2)}) %collective-permute-start.3) | collective-permute-done | bytes 122912 | tf_op jit(solution)/shard_map/ppermute | solution.py:75
  33.0 0.7 collective-permute-done.4.refs_2_
  33.8 2.0 %collective-permute-done.5.refs_3_ = f32[240,128]{1,0:T(8,128)S(1)} collective-permute-done((f32[240,128]{1,0:T(8,128)S(1)}, f32[240,128]{1,0:T(8,128)S(1)}, u32[]{:S(2)}, u32[]{:S(2)}) %collective-permute-start.5) | collective-permute-done | bytes 122912 | tf_op jit(solution)/shard_map/ppermute | solution.py:75
  35.8 1.3 %collective-permute-done.9.refs_7_ = f32[240,128]{1,0:T(8,128)S(1)} collective-permute-done((f32[240,128]{1,0:T(8,128)S(1)}, f32[240,128]{1,0:T(8,128)S(1)}, u32[]{:S(2)}, u32[]{:S(2)}) %collective-permute-start.9) | collective-permute-done | bytes 122912 | tf_op jit(solution)/shard_map/ppermute | solution.py:56
  37.1 1.0 %mixing.1 = (bf16[2,256,896]{2,1,0:T(8,128)(2,1)S(1)}, f32[2,2,16,128]{3,2,1,0:T(8,128)S(1)}, f32[16,1,768]{2,1,0:T(1,128)S(1)}) custom-call(f32[240,128]{1,0:T(8,128)S(1)} %gather.1.refs_0_, f32[240,128]{1,0:T(8,128)S(1)} %collective-permute-done.3.refs_1_, f32[240,128]{1,0:T(8,128)S(1)} %collective-permute-done.4.refs_2_, ...), custom_call_target="tpu_custom_call" | custom-call | bytes 4358144 | tf_op jit(solution)/shard_map/mixing/pallas_call | solution.py:85
  38.1 10.9 %all_to_all.21.received = f32[16,1,768]{2,1,0:T(1,128)S(1)} all-to-all(f32[16,1,768]{2,1,0:T(1,128)S(1)} %get-tuple-element.48), channel_id=1, replica_groups=mesh['tm'=2,'cell'=16] {'cell'}, dimensions={0} | all-to-all | bytes 98304 | tf_op jit(solution)/shard_map/all_to_all | solution.py:79
  50.2 1.9 %sweep.3 = (f32[2,2,8,128]{3,2,1,0:T(8,128)S(1)}, f32[2,256,128]{2,1,0:T(8,128)S(1)}) custom-call(f32[256,128]{1,0:T(8,128)S(1)} %copy-done.2, f32[3,256,128]{2,1,0:T(8,128)S(1)} %collective-permute-done.11.refs_1_, f32[2,256,128]{2,1,0:T(8,128)S(1)} %copy-done.1, f32[2,2,128,128]{3,2,1,0:T(8,128)S(1)} %copy-done, ...), custom_call_target="tpu_custom_call" | custom-call | bytes 3694592 | tf_op jit(solution)/shard_map/sweep/pallas_call | solution.py:85
  52.1 1.2 %collective-permute-done.10.received = f32[2,8,128]{2,1,0:T(8,128)S(1)} collective-permute-done((f32[2,8,128]{2,1,0:T(8,128)S(1)}, f32[2,8,128]{2,1,0:T(8,128)S(1)}, u32[]{:S(2)}, u32[]{:S(2)}) %collective-permute-start.10) | collective-permute-done | bytes 8224 | tf_op jit(solution)/shard_map/ppermute | solution.py:51
  53.8 9.7 %all_to_all.22.received = f32[16,1,1280]{2,1,0:T(1,128)S(1)} all-to-all(f32[16,1,1280]{2,1,0:T(1,128)S(1)} %get-tuple-element.55), channel_id=1, replica_groups=mesh['tm'=2,'cell'=16] {'cell'}, dimensions={0} | all-to-all | bytes 163840 | tf_op jit(solution)/shard_map/all_to_all | solution.py:79
  63.5 0.9 %first.1 = (f32[2,2,16,128]{3,2,1,0:T(8,128)S(1)}, f32[16,1,768]{2,1,0:T(1,128)S(1)}) custom-call(f32[16,1,1280]{2,1,0:T(1,128)S(1)} %all_to_all.22.received, f32[16,128]{1,0:T(8,128)S(1)} %get-tuple-element.56.base, bf16[2,256,896]{2,1,0:T(8,128)(2,1)S(1)} %get-tuple-element.50.mixing, ...), custom_call_target="tpu_custom_call" | custom-call | bytes 3457024 | tf_op jit(solution)/shard_map/first/pallas_call | solution.py:85
  64.4 9.3 %all_to_all.23.received = f32[16,1,768]{2,1,0:T(1,128)S(1)} all-to-all(f32[16,1,768]{2,1,0:T(1,128)S(1)} %get-tuple-element.57), channel_id=1, replica_groups=mesh['tm'=2,'cell'=16] {'cell'}, dimensions={0} | all-to-all | bytes 98304 | tf_op jit(solution)/shard_map/all_to_all | solution.py:79
  73.7 0.8 push.3
  75.1 3.1 %collective-permute-done.12.received = f32[2,8,128]{2,1,0:T(8,128)S(1)} collective-permute-done((f32[2,8,128]{2,1,0:T(8,128)S(1)}, f32[2,8,128]{2,1,0:T(8,128)S(1)}, u32[]{:S(2)}, u32[]{:S(2)}) %collective-permute-start.12) | collective-permute-done | bytes 8224 | tf_op jit(solution)/shard_map/ppermute | solution.py:51
  78.2 1.1 %finish.1 = f32[2,256,128]{2,1,0:T(8,128)} custom-call(f32[2,8,128]{2,1,0:T(8,128)S(1)} %collective-permute-done.12.received, f32[2,2,8,128]{3,2,1,0:T(8,128)S(1)} %get-tuple-element.61.pushes, f32[2,2,8,128]{3,2,1,0:T(8,128)S(1)} %get-tuple-element.59.refs_0_.starts, f32[2,2,128,128]{3,2,1,0:T(8,128)S(1)} %copy-done, ...), custom_call_target="tpu_custom_call" | custom-call | bytes 835584 | tf_op jit(solution)/shard_map/finish/pallas_call | solution.py:85
  (33 shorter events, 5.1 us)
Async XLA Ops:
  0.0 0.7 copy-start.5
  0.0 0.7 copy-start.4
  0.0 1.0 %copy-start = (f32[2,2,128,128]{3,2,1,0:T(8,128)S(1)}, f32[2,2,128,128]{3,2,1,0:T(8,128)}, u32[]{:S(2)}) copy-start(f32[2,2,128,128]{3,2,1,0:T(8,128)} %coarse.11) | copy-start | bytes 786436
  0.0 1.0 %copy-start.2 = (f32[256,128]{1,0:T(8,128)S(1)}, f32[256,128]{1,0:T(8,128)}, u32[]{:S(2)}) copy-start(f32[256,128]{1,0:T(8,128)} %refs_0_.2) | copy-start | bytes 393220
  0.0 1.1 %copy-start.1 = (f32[2,256,128]{2,1,0:T(8,128)S(1)}, f32[2,256,128]{2,1,0:T(8,128)}, u32[]{:S(2)}) copy-start(f32[2,256,128]{2,1,0:T(8,128)} %refs_2_.3) | copy-start | bytes 786436
  0.0 1.2 %copy-start.3 = (f32[2,2,128,128]{3,2,1,0:T(8,128)S(1)}, f32[2,2,128,128]{3,2,1,0:T(8,128)}, u32[]{:S(2)}) copy-start(f32[2,2,128,128]{3,2,1,0:T(8,128)} %fine.1) | copy-start | bytes 786436
  2.6 5.2 %collective-permute-start = (f32[896,128]{1,0:T(8,128)S(1)}, f32[896,128]{1,0:T(8,128)S(1)}, u32[]{:S(2)}, u32[]{:S(2)}) collective-permute-start(f32[896,128]{1,0:T(8,128)S(1)} %get-tuple-element.35), channel_id=1, source_target_pairs={{0,1},{1,0},{2,3},{3,2},{4,5},{5,4},{6,7},{7,6},{8,9},{9,8},{10,11... | collective-permute-start | bytes 1376264 | tf_op jit(solution)/shard_map/ppermute | solution.py:56
  3.1 4.2 %collective-permute-start.1 = (f32[2,8,128]{2,1,0:T(8,128)S(1)}, f32[2,8,128]{2,1,0:T(8,128)S(1)}, u32[]{:S(2)}, u32[]{:S(2)}) collective-permute-start(f32[2,8,128]{2,1,0:T(8,128)S(1)} %get-tuple-element.37), channel_id=1, source_target_pairs={{0,16},{16,0},{1,17},{17,1},{2,18},{18,2},{3,19},{19,3},{4,20},{20... | collective-permute-start | bytes 24584 | tf_op jit(solution)/shard_map/ppermute | solution.py:51
  19.4 7.2 %collective-permute-start.2 = (f32[240,128]{1,0:T(8,128)S(1)}, f32[240,128]{1,0:T(8,128)S(1)}, u32[]{:S(2)}, u32[]{:S(2)}) collective-permute-start(f32[240,128]{1,0:T(8,128)S(1)} %middle.1.a), channel_id=1, source_target_pairs={{0,8},{1,9},{2,10},{3,11},{4,12},{5,13},{6,14},{7,15},{8,0},{9,1},... | collective-permute-start | bytes 368648 | tf_op jit(solution)/shard_map/ppermute | solution.py:75
  26.6 23.6 %collective-permute-start.11 = (f32[3,256,128]{2,1,0:T(8,128)S(1)}, f32[3,256,128]{2,1,0:T(8,128)S(1)}, u32[]{:S(2)}, u32[]{:S(2)}) collective-permute-start(f32[3,256,128]{2,1,0:T(8,128)S(1)} %sweep.2), channel_id=1, source_target_pairs={{0,16},{16,0},{1,17},{17,1},{2,18},{18,2},{3,19},{19,3},{4,20},{20... | collective-permute-start | bytes 1179656 | tf_op jit(solution)/shard_map/ppermute | solution.py:51
  28.1 4.9 %collective-permute-start.3 = (f32[240,128]{1,0:T(8,128)S(1)}, f32[240,128]{1,0:T(8,128)S(1)}, u32[]{:S(2)}, u32[]{:S(2)}) collective-permute-start(f32[240,128]{1,0:T(8,128)S(1)} %gather.1.refs_0_), channel_id=1, source_target_pairs={{0,2},{1,3},{2,0},{3,1},{4,6},{5,7},{6,4},{7,5},{8,10},{9,11},{10,... | collective-permute-start | bytes 368648 | tf_op jit(solution)/shard_map/ppermute | solution.py:75
  28.9 4.9 %collective-permute-start.4 = (f32[240,128]{1,0:T(8,128)S(1)}, f32[240,128]{1,0:T(8,128)S(1)}, u32[]{:S(2)}, u32[]{:S(2)}) collective-permute-start(f32[240,128]{1,0:T(8,128)S(1)} %gather.1.refs_0_), channel_id=1, source_target_pairs={{0,4},{1,5},{2,6},{3,7},{4,0},{5,1},{6,2},{7,3},{8,12},{9,13},{10,... | collective-permute-start | bytes 368648 | tf_op jit(solution)/shard_map/ppermute | solution.py:75
  28.9 6.9 %collective-permute-start.5 = (f32[240,128]{1,0:T(8,128)S(1)}, f32[240,128]{1,0:T(8,128)S(1)}, u32[]{:S(2)}, u32[]{:S(2)}) collective-permute-start(f32[240,128]{1,0:T(8,128)S(1)} %gather.1.refs_0_), channel_id=1, source_target_pairs={{0,6},{1,7},{2,4},{3,5},{4,2},{5,3},{6,0},{7,1},{8,14},{9,15},{10,... | collective-permute-start | bytes 368648 | tf_op jit(solution)/shard_map/ppermute | solution.py:75
  31.6 4.2 %collective-permute-start.6 = (f32[240,128]{1,0:T(8,128)S(1)}, f32[240,128]{1,0:T(8,128)S(1)}, u32[]{:S(2)}, u32[]{:S(2)}) collective-permute-start(f32[240,128]{1,0:T(8,128)S(1)} %gather.1.refs_0_), channel_id=1, source_target_pairs={{0,1},{1,0},{2,3},{3,2},{4,5},{5,4},{6,7},{7,6},{8,9},{9,8},{10,11... | collective-permute-start | bytes 368648 | tf_op jit(solution)/shard_map/ppermute | solution.py:56
  33.0 2.8 %collective-permute-start.7 = (f32[240,128]{1,0:T(8,128)S(1)}, f32[240,128]{1,0:T(8,128)S(1)}, u32[]{:S(2)}, u32[]{:S(2)}) collective-permute-start(f32[240,128]{1,0:T(8,128)S(1)} %collective-permute-done.3.refs_1_), channel_id=1, source_target_pairs={{0,1},{1,0},{2,3},{3,2},{4,5},{5,4},{6,7},{7,6},{8,9},{9,8},{10,11... | collective-permute-start | bytes 368648 | tf_op jit(solution)/shard_map/ppermute | solution.py:56
  33.8 2.1 %collective-permute-start.8 = (f32[240,128]{1,0:T(8,128)S(1)}, f32[240,128]{1,0:T(8,128)S(1)}, u32[]{:S(2)}, u32[]{:S(2)}) collective-permute-start(f32[240,128]{1,0:T(8,128)S(1)} %collective-permute-done.4.refs_2_), channel_id=1, source_target_pairs={{0,1},{1,0},{2,3},{3,2},{4,5},{5,4},{6,7},{7,6},{8,9},{9,8},{10,11... | collective-permute-start | bytes 368648 | tf_op jit(solution)/shard_map/ppermute | solution.py:56
  35.8 1.3 %collective-permute-start.9 = (f32[240,128]{1,0:T(8,128)S(1)}, f32[240,128]{1,0:T(8,128)S(1)}, u32[]{:S(2)}, u32[]{:S(2)}) collective-permute-start(f32[240,128]{1,0:T(8,128)S(1)} %collective-permute-done.5.refs_3_), channel_id=1, source_target_pairs={{0,1},{1,0},{2,3},{3,2},{4,5},{5,4},{6,7},{7,6},{8,9},{9,8},{10,11... | collective-permute-start | bytes 368648 | tf_op jit(solution)/shard_map/ppermute | solution.py:56
  49.6 3.7 %collective-permute-start.10 = (f32[2,8,128]{2,1,0:T(8,128)S(1)}, f32[2,8,128]{2,1,0:T(8,128)S(1)}, u32[]{:S(2)}, u32[]{:S(2)}) collective-permute-start(f32[2,8,128]{2,1,0:T(8,128)S(1)} %get-tuple-element.51), channel_id=1, source_target_pairs={{0,16},{16,0},{1,17},{17,1},{2,18},{18,2},{3,19},{19,3},{4,20},{20... | collective-permute-start | bytes 24584 | tf_op jit(solution)/shard_map/ppermute | solution.py:51
  74.5 3.7 %collective-permute-start.12 = (f32[2,8,128]{2,1,0:T(8,128)S(1)}, f32[2,8,128]{2,1,0:T(8,128)S(1)}, u32[]{:S(2)}, u32[]{:S(2)}) collective-permute-start(f32[2,8,128]{2,1,0:T(8,128)S(1)} %get-tuple-element.60), channel_id=1, source_target_pairs={{0,16},{16,0},{1,17},{17,1},{2,18},{18,2},{3,19},{19,3},{4,20},{20... | collective-permute-start | bytes 24584 | tf_op jit(solution)/shard_map/ppermute | solution.py:51
